TPU v7x, 32 devices: a whole 2x2x4 slice. The times are simulated.
32 devices in a mesh: grp: 2 (over x), slab: 16 (over z, y, core).
Axes of the slice: x: 2, y: 2, z: 4, core: 2. Of those that a mesh axis runs over, the one named last changes fastest.
Arguments:
- features: bfloat16 [4, 96, 128, 192], P(None, ('grp', 'slab')), parts along dimension 1, may hold values from -6 to 6
- time_cache: bfloat16 [2, 96, 128, 192], P(None, ('grp', 'slab')), parts along dimension 1, may hold values from -6 to 6
- cotangent: bfloat16 [4, 96, 128, 192], P(None, ('grp', 'slab')), parts along dimension 1, may hold values from -6 to 6
- kernel: bfloat16 [3, 3, 3, 192, 192], replicated, may hold values from -0.078125 to 0.078125
- norm_gain: float32 [192], replicated, may hold values from 0.5 to 1.5
- norm_shift: float32 [192], replicated, may hold values from -0.5 to 0.5
- conv_bias: float32 [192], replicated, may hold values from -3 to 3
Outputs:
- decoded: bfloat16 [4, 96, 128, 192], P(None, ('grp', 'slab')), parts along dimension 1
- feature_grad: bfloat16 [4, 96, 128, 192], P(None, 'grp', 'slab'), parts along dimension 1
There are 2 independent parts, one for each index of `grp`. A program takes and returns all parts, laid end to end along the dimension named above; an argument that names none is the same for every part. Nothing has to cross between parts.
All inputs are finite; a program needn't handle non-finite values.
Results may differ from a plain program's by a relative error of at most 0.0029.
Values may be sent and summed in bfloat16 or wider, within the bound.
No kernel may reach another device: no remote copies, remote signals or barrier semaphores. Data moves between devices by JAX's collectives and lax.ppermute only.
A program may use at most 128 MiB of HBM per device.

v0:
```python
import jax
import jax.numpy as jnp
from jax import lax
from jax.sharding import PartitionSpec as P


def padded_2(x, sides, width):
    for axis, dim in sides:
        count, length = (lax.axis_size(axis), x.shape[dim])
        up = [(i, (i + 1) % count) for i in range(count - 1)]
        down = [(j, i) for i, j in up]
        last = lax.slice_in_dim(x, length - width, length, axis=dim)
        leading = lax.slice_in_dim(x, 0, width, axis=dim)
        before = lax.ppermute(last, axis, up)
        after = lax.ppermute(leading, axis, down)
        x = jnp.concatenate([before, x, after], axis=dim)
    return x


def convolve(padded, kernel):
    frames = padded.shape[0] - 2
    rows = padded.shape[1] - 2
    cols = padded.shape[2] - 2
    chans = padded.shape[3]
    total = jnp.zeros((frames * rows * cols, kernel.shape[4]), jnp.float32)
    for t in range(3):
        pieces = [
            padded[t : t + frames, i : i + rows, j : j + cols, :]
            for i in range(3)
            for j in range(3)
        ]
        stacked = jnp.concatenate(pieces, axis=-1).reshape(-1, 9 * chans)
        total = total + jnp.dot(
            stacked, kernel[t].reshape(9 * chans, -1), preferred_element_type=jnp.float32
        )
    return total.reshape(frames, rows, cols, -1)


def normalize(features, norm_gain, norm_shift):
    values = features.astype(jnp.float32)
    scale = lax.rsqrt(jnp.mean(values * values, axis=-1, keepdims=True) + 1e-06)
    normed = values * scale * norm_gain + norm_shift
    return (values, scale, normed)


def pad_cols(block):
    return jnp.pad(block, ((0, 0), (0, 0), (1, 1), (0, 0)))


def finish(values, scale, normed, act_grad, cotangent, norm_gain):
    sig = jax.nn.sigmoid(normed)
    norm_grad = act_grad * sig * (1.0 + normed * (1.0 - sig)) * norm_gain
    inner = jnp.mean(norm_grad * values, axis=-1, keepdims=True)
    result = (
        cotangent.astype(jnp.float32) + scale * norm_grad - values * scale * scale * scale * inner
    )
    return result.astype(jnp.bfloat16)


def body(features, time_cache, cotangent, kernel, norm_gain, norm_shift, conv_bias):
    flipped = jnp.swapaxes(kernel[::-1, ::-1, ::-1], 3, 4)
    values, scale, normed = normalize(features, norm_gain, norm_shift)
    activated = jax.nn.silu(normed).astype(jnp.bfloat16)
    joined = jnp.concatenate([time_cache, activated], axis=0)
    rimmed = padded_2(joined, (("slab", 1),), 1)
    conv = convolve(pad_cols(rimmed), kernel)
    grad_rim = padded_2(cotangent, (("slab", 1),), 1)
    grad_pad = pad_cols(jnp.pad(grad_rim, ((0, 2), (0, 0), (0, 0), (0, 0))))
    act_grad = convolve(grad_pad, flipped)
    decoded = (values + conv + conv_bias).astype(jnp.bfloat16)
    feature_grad = finish(values, scale, normed, act_grad, cotangent, norm_gain)
    relaid = lax.all_to_all(feature_grad, "slab", split_axis=2, concat_axis=1, tiled=True)
    return (decoded, relaid)


def solution(mesh):
    return jax.shard_map(
        body,
        mesh=mesh,
        in_specs=(
            P(None, ("grp", "slab"), None, None),
            P(None, ("grp", "slab"), None, None),
            P(None, ("grp", "slab"), None, None),
            P(),
            P(),
            P(),
            P(),
        ),
        out_specs=(P(None, ("grp", "slab"), None, None), P(None, "grp", "slab", None)),
        check_vma=False,
    )
```

profile of v0, /device:TPU:0, one launch (start us, length us, event | category | flops | bytes accessed | tf_op | source)
XLA Modules:
  0.0 172.1 jit_solution(17432203910121970982)
XLA Ops:
  0.6 1.8 %fusion.58 = (bf16[4,1,128,192]{2,3,1,0:T(8,128)(2,1)}, bf16[4,1,128,192]{2,3,1,0:T(8,128)(2,1)}) fusion(bf16[4,3,128,192]{2,3,1,0:T(8,128)(2,1)} %param.9), kind=kLoop, calls=%fused_computation.136 | loop fusion | bytes 786432 | tf_op jit(solution)/shard_map/slice | solution.py:12
  3.7 3.7 %collective-permute-start.2 = (bf16[4,1,128,192]{2,3,1,0:T(8,128)(2,1)}, bf16[4,1,128,192]{2,3,1,0:T(8,128)(2,1)}, u32[]{:S(2)}, u32[]{:S(2)}) collective-permute-start(bf16[4,1,128,192]{2,3,1,0:T(8,128)(2,1)} %get-tuple-element.58), channel_id=1, source_target_pairs={{0,1},{1,2},{2,3},{3,4},{4,5},{5,6},{6,7},{7,8},{8,9},{9,10},{10,1... | collective-permute-start | bytes 589832 | tf_op jit(solution)/shard_map/ppermute | solution.py:14
  8.6 1.9 %reverse_bitcast_fusion = bf16[3,3,3,192,192]{3,4,2,1,0:T(8,128)(2,1)S(1)} fusion(bf16[3,3,3,192,192]{4,3,2,1,0:T(8,128)(2,1)} %param.10), kind=kLoop, calls=%fused_computation.30 | loop fusion | bytes 3981312 | tf_op jit(solution)/shard_map/transpose | solution.py:61
  13.3 1.6 copy.94
  18.9 1.9 %fusion.51 = bf16[4,3,128,1728]{2,3,1,0:T(8,128)(2,1)} fusion(bf16[4,3,128,1728]{2,3,1,0:T(8,128)(2,1)} %get-tuple-element.40, bf16[4,3,128,192]{2,3,1,0:T(8,128)(2,1)S(1)} %copy-done.2, bf16[4,1,128,192]{2,3,1,0:T(8,128)(2,1)} %collective-permute-done.2), kind=kLoop, calls=%fused_computation.101 | loop fusion | flops 1179648 | bytes 1376256
  20.8 1.8 %fusion.49 = (bf16[4,3,128,1728]{2,3,1,0:T(8,128)(2,1)S(1)}, bf16[4,3,128,1728]{2,3,1,0:T(8,128)(2,1)}, bf16[4,3,128,1728]{2,3,1,0:T(8,128)(2,1)}) fusion(bf16[4,3,128,1728]{2,3,1,0:T(8,128)(2,1)S(1)} %get-tuple-element.39, bf16[6,5,128,192]{2,3,1,0:T(8,128)(2,1)S(1)} %fusion.8, bf16[4,3,128,1728]{2,3,1,0:T(8,128)(2,1)} %fusion.51), kind=kLoop, calls=%fused_computation.91 | loop fusion | bytes 3244032 | tf_op jit(solution)/shard_map/concatenate | solution.py:32
  23.7 1.6 fusion.39
  30.4 1.5 fusion.43
  37.0 8.2 %copy.89 = bf16[4,3,128,1728]{3,2,1,0:T(8,128)(2,1)} copy(bf16[4,3,128,1728]{2,3,1,0:T(8,128)(2,1)} %fusion.37) | data formatting | bytes 10616832 | tf_op jit(solution)/shard_map/concatenate | solution.py:32
  45.2 8.0 %copy.91 = bf16[4,3,128,1728]{3,2,1,0:T(8,128)(2,1)} copy(bf16[4,3,128,1728]{2,3,1,0:T(8,128)(2,1)} %get-tuple-element.41) | data formatting | bytes 10616832 | tf_op jit(solution)/shard_map/concatenate | solution.py:32
  53.2 7.9 %copy.93 = bf16[4,3,128,1728]{3,2,1,0:T(8,128)(2,1)} copy(bf16[4,3,128,1728]{2,3,1,0:T(8,128)(2,1)} %copy-done.7) | data formatting | bytes 10616832 | tf_op jit(solution)/shard_map/concatenate | solution.py:32
  61.1 4.7 %fusion.60 = f32[1536,192]{0,1:T(8,128)S(1)} fusion(bf16[1536,1728]{1,0:T(8,128)(2,1)} %bitcast.44, bf16[1728,192]{1,0:T(8,128)(2,1)S(1)} %bitcast.48), kind=kOutput, calls=%fused_computation.138 | convolution fusion | flops 1019215872 | bytes 7151616 | tf_op jit(solution)/shard_map/dot_general | solution.py:33
  65.8 2.0 %convolution_add_fusion.1 = f32[1536,192]{0,1:T(8,128)S(1)} fusion(f32[1536,192]{0,1:T(8,128)S(1)} %fusion.60, bf16[1536,1728]{1,0:T(8,128)(2,1)S(1)} %bitcast.42, bf16[1728,192]{1,0:T(8,128)(2,1)S(1)} %bitcast.47), kind=kOutput, calls=%fused_computation.32 | convolution fusion | flops 1019510784 | bytes 8331264 | tf_op jit(solution)/shard_map/dot_general | solution.py:33
  67.8 3.0 %convolution_add_fusion = f32[1536,192]{0,1:T(8,128)} fusion(f32[1536,192]{0,1:T(8,128)S(1)} %convolution_add_fusion.1, bf16[1536,1728]{1,0:T(8,128)(2,1)S(1)} %bitcast.41, bf16[1728,192]{1,0:T(8,128)(2,1)S(1)} %bitcast.46), kind=kOutput, calls=%fused_computation.31 | convolution fusion | flops 1019510784 | bytes 8331264 | tf_op jit(solution)/shard_map/dot_general | solution.py:33
  70.7 3.0 %reshape.50 = f32[4,3,128,192]{2,1,0,3:T(4,128)} reshape(f32[1536,192]{0,1:T(8,128)} %convolution_add_fusion) | data formatting | bytes 2359296 | tf_op jit(solution)/shard_map/reshape | solution.py:36
  73.7 3.6 %fusion.29 = (f32[4,3,128]{2,1,0:T(4,128)S(1)}, f32[4,3,128,192]{2,3,1,0:T(8,128)}, bf16[4,3,128,192]{2,3,1,0:T(8,128)(2,1)S(1)}) fusion(bf16[4,3,128,192]{2,3,1,0:T(8,128)(2,1)} %param.7, f32[192]{0:T(256)S(1)} %copy-done.12, f32[192]{0:T(256)S(1)} %copy-done.13, f32[4,3,128]{2,1,0:T(4,128)S(1)} %add_rsqrt_fusion, f32[4,3,128,192]{2,1,0,3:T(4,128)} %reshape.50), kind=kLoop, calls=%fused_computation.64 | loop fusion | flops 5011968 | bytes 3552768 | tf_op jit(solution)/shard_map/reduce_sum | solution.py:53
  77.4 1.3 collective-permute-start.1
  78.7 4.5 %collective-permute-start = (bf16[6,1,128,192]{2,3,1,0:T(8,128)(2,1)S(1)}, bf16[6,1,128,192]{2,3,1,0:T(8,128)(2,1)S(1)}, u32[]{:S(2)}, u32[]{:S(2)}) collective-permute-start(bf16[6,1,128,192]{2,3,1,0:T(8,128)(2,1)S(1)} %get-tuple-element.53), channel_id=1, source_target_pairs={{0,1},{1,2},{2,3},{3,4},{4,5},{5,6},{6,7},{7,8},{8,9},{9,10},{10,1... | collective-permute-start | bytes 884744 | tf_op jit(solution)/shard_map/ppermute | solution.py:14
  83.1 1.6 fusion.57
  84.8 2.5 %select_maximum_fusion = bf16[6,5,130,192]{2,3,1,0:T(8,128)(2,1)S(1)} fusion(bf16[6,1,128,192]{2,3,1,0:T(8,128)(2,1)S(1)} %collective-permute-done.1, bf16[6,1,128,192]{2,3,1,0:T(8,128)(2,1)S(1)} %collective-permute-done, bf16[4,3,128,192]{2,3,1,0:T(8,128)(2,1)S(1)} %get-tuple-element.55, bf16[2,3,128,192]{2,3,1,0:T(8,128)(2,1)S(1)} %copy-done.8), kind=kLoop, calls=%fused_computation.25 | loop fusion | flops 11232000 | bytes 2972160 | tf_op jit(solution)/shard_map/concatenate | solution.py:16
  92.8 2.3 %copy-done.4 = bf16[4,3,128,1728]{2,3,1,0:T(8,128)(2,1)} copy-done((bf16[4,3,128,1728]{2,3,1,0:T(8,128)(2,1)}, bf16[4,3,128,1728]{2,3,1,0:T(8,128)(2,1)S(1)}, u32[]{:S(2)}) %copy-start.4) | copy-done | bytes 5308440
  95.2 2.3 %copy-done.5 = bf16[4,3,128,1728]{2,3,1,0:T(8,128)(2,1)} copy-done((bf16[4,3,128,1728]{2,3,1,0:T(8,128)(2,1)}, bf16[4,3,128,1728]{2,3,1,0:T(8,128)(2,1)S(1)}, u32[]{:S(2)}) %copy-start.5) | copy-done | bytes 5308440
  97.5 2.4 %copy-done.6 = bf16[4,3,128,1728]{2,3,1,0:T(8,128)(2,1)} copy-done((bf16[4,3,128,1728]{2,3,1,0:T(8,128)(2,1)}, bf16[4,3,128,1728]{2,3,1,0:T(8,128)(2,1)S(1)}, u32[]{:S(2)}) %copy-start.6) | copy-done | bytes 5308440
  99.9 8.2 %copy.85 = bf16[4,3,128,1728]{3,2,1,0:T(8,128)(2,1)} copy(bf16[4,3,128,1728]{2,3,1,0:T(8,128)(2,1)} %copy-done.6) | data formatting | bytes 10616832 | tf_op jit(solution)/shard_map/concatenate | solution.py:32
  108.1 8.0 %copy.86 = bf16[4,3,128,1728]{3,2,1,0:T(8,128)(2,1)} copy(bf16[4,3,128,1728]{2,3,1,0:T(8,128)(2,1)} %copy-done.5) | data formatting | bytes 10616832 | tf_op jit(solution)/shard_map/concatenate | solution.py:32
  116.1 8.0 %copy.87 = bf16[4,3,128,1728]{3,2,1,0:T(8,128)(2,1)} copy(bf16[4,3,128,1728]{2,3,1,0:T(8,128)(2,1)} %copy-done.4) | data formatting | bytes 10616832 | tf_op jit(solution)/shard_map/concatenate | solution.py:32
  124.1 4.7 %fusion.59 = f32[1536,192]{0,1:T(8,128)S(1)} fusion(bf16[1536,1728]{1,0:T(8,128)(2,1)} %bitcast.45, bf16[1728,192]{1,0:T(8,128)(2,1)S(1)} %bitcast.51), kind=kOutput, calls=%fused_computation.137 | convolution fusion | flops 1019215872 | bytes 7151616 | tf_op jit(solution)/shard_map/dot_general | solution.py:33
  128.8 2.0 %convolution_add_fusion.3 = f32[1536,192]{0,1:T(8,128)S(1)} fusion(f32[1536,192]{0,1:T(8,128)S(1)} %fusion.59, bf16[1536,1728]{1,0:T(8,128)(2,1)S(1)} %bitcast.43, bf16[1728,192]{1,0:T(8,128)(2,1)S(1)} %bitcast.50), kind=kOutput, calls=%fused_computation.34 | convolution fusion | flops 1019510784 | bytes 8331264 | tf_op jit(solution)/shard_map/dot_general | solution.py:33
  130.8 2.0 %convolution_add_fusion.2 = f32[1536,192]{0,1:T(8,128)S(1)} fusion(f32[1536,192]{0,1:T(8,128)S(1)} %convolution_add_fusion.3, bf16[1536,1728]{1,0:T(8,128)(2,1)S(1)} %bitcast.38, bf16[1728,192]{1,0:T(8,128)(2,1)S(1)} %bitcast.49), kind=kOutput, calls=%fused_computation.33 | convolution fusion | flops 1019510784 | bytes 8331264 | tf_op jit(solution)/shard_map/dot_general | solution.py:33
  133.6 3.1 %fusion.25 = (bf16[4,3,128,192]{2,3,1,0:T(8,128)(2,1)}, bf16[4,3,128,192]{2,3,1,0:T(8,128)(2,1)}) fusion(bf16[4,3,128,192]{2,3,1,0:T(8,128)(2,1)} %param.7, f32[4,3,128,192]{2,3,1,0:T(8,128)} %get-tuple-element.11, bf16[4,3,128,192]{2,3,1,0:T(8,128)(2,1)S(1)} %copy-done.2, f32[4,3,128]{2,1,0:T(4,128)S(1)} %broadcast_multiply_fusion, ...), kind=kLoop, calls=%fused_computation.60 | loop fusion | flops 3833856 | bytes 4731648 | tf_op jit(solution)/shard_map/convert_element_type | solution.py:57
  136.8 1.7 copy.96
  138.4 32.6 %all_to_all.18 = bf16[4,3,128,192]{3,0,1,2:T(4,128)(2,1)S(1)} all-to-all(bf16[4,3,128,192]{3,0,1,2:T(4,128)(2,1)S(1)} %copy.96), channel_id=1, replica_groups=mesh['grp'=2,'slab'=16] {'slab'}, dimensions={2} | all-to-all | bytes 1179648 | tf_op jit(solution)/shard_map/all_to_all | solution.py:72
  (82 shorter events, 28.0 us)
Async XLA Ops:
  2.4 12.4 %collective-permute-start.3 = (bf16[4,1,128,192]{2,3,1,0:T(8,128)(2,1)}, bf16[4,1,128,192]{2,3,1,0:T(8,128)(2,1)S(1)}, u32[]{:S(2)}, u32[]{:S(2)}) collective-permute-start(bf16[4,1,128,192]{2,3,1,0:T(8,128)(2,1)} %get-tuple-element.59), channel_id=1, source_target_pairs={{1,0},{2,1},{3,2},{4,3},{5,4},{6,5},{7,6},{8,7},{9,8},{10,9},{11,1... | collective-permute-start | bytes 589832 | tf_op jit(solution)/shard_map/ppermute | solution.py:15
  3.7 11.2 %collective-permute-start.2 = (bf16[4,1,128,192]{2,3,1,0:T(8,128)(2,1)}, bf16[4,1,128,192]{2,3,1,0:T(8,128)(2,1)}, u32[]{:S(2)}, u32[]{:S(2)}) collective-permute-start(bf16[4,1,128,192]{2,3,1,0:T(8,128)(2,1)} %get-tuple-element.58), channel_id=1, source_target_pairs={{0,1},{1,2},{2,3},{3,4},{4,5},{5,6},{6,7},{7,8},{8,9},{9,10},{10,1... | collective-permute-start | bytes 589832 | tf_op jit(solution)/shard_map/ppermute | solution.py:14
  10.6 4.3 %copy-start.2 = (bf16[4,3,128,192]{2,3,1,0:T(8,128)(2,1)S(1)}, bf16[4,3,128,192]{2,3,1,0:T(8,128)(2,1)}, u32[]{:S(2)}) copy-start(bf16[4,3,128,192]{2,3,1,0:T(8,128)(2,1)} %param.9) | copy-start | bytes 1769476
  22.6 6.8 %copy-start.7 = (bf16[4,3,128,1728]{2,3,1,0:T(8,128)(2,1)}, bf16[4,3,128,1728]{2,3,1,0:T(8,128)(2,1)S(1)}, u32[]{:S(2)}) copy-start(bf16[4,3,128,1728]{2,3,1,0:T(8,128)(2,1)S(1)} %get-tuple-element.36) | copy-start | bytes 15925252
  61.1 4.7 %copy-start = (bf16[4,3,128,1728]{3,2,1,0:T(8,128)(2,1)S(1)}, bf16[4,3,128,1728]{3,2,1,0:T(8,128)(2,1)}, u32[]{:S(2)}) copy-start(bf16[4,3,128,1728]{3,2,1,0:T(8,128)(2,1)} %copy.91) | copy-start | bytes 15925252
  61.1 6.6 %slice-start.2 = ((s8[5505024]{0:T(1024)(128)(4,1)}), s8[4194304]{0:T(1024)(128)(4,1)S(1)}, s32[]{:S(2)}) async-start(s8[5505024]{0:T(1024)(128)(4,1)} %bitcast.39), calls=%async_computation.3 | async-start | bytes 8388608
  65.7 2.0 %slice-start.3 = ((s8[5505024]{0:T(1024)(128)(4,1)}), s8[1310720]{0:T(1024)(128)(4,1)S(1)}, s32[]{:S(2)}) async-start(s8[5505024]{0:T(1024)(128)(4,1)} %bitcast.39), calls=%async_computation.4 | async-start | bytes 2621440
  67.7 6.0 %copy-start.12 = (f32[192]{0:T(256)S(1)}, f32[192]{0:T(256)}, u32[]{:S(2)}) copy-start(f32[192]{0:T(256)} %param.12) | copy-start | bytes 2308
  67.8 6.0 %copy-start.13 = (f32[192]{0:T(256)S(1)}, f32[192]{0:T(256)}, u32[]{:S(2)}) copy-start(f32[192]{0:T(256)} %param.11) | copy-start | bytes 2308
  70.7 6.6 %copy-start.8 = (bf16[2,3,128,192]{2,3,1,0:T(8,128)(2,1)S(1)}, bf16[2,3,128,192]{2,3,1,0:T(8,128)(2,1)}, u32[]{:S(2)}) copy-start(bf16[2,3,128,192]{2,3,1,0:T(8,128)(2,1)} %param.8) | copy-start | bytes 884740
  70.7 12.4 %copy-start.3 = (bf16[3,3,3,192,192]{4,3,2,1,0:T(8,128)(2,1)S(1)}, bf16[3,3,3,192,192]{4,3,2,1,0:T(8,128)(2,1)}, u32[]{:S(2)}) copy-start(bf16[3,3,3,192,192]{4,3,2,1,0:T(8,128)(2,1)} %param.10) | copy-start | bytes 5971972
  77.4 7.4 %collective-permute-start.1 = (bf16[6,1,128,192]{2,3,1,0:T(8,128)(2,1)S(1)}, bf16[6,1,128,192]{2,3,1,0:T(8,128)(2,1)S(1)}, u32[]{:S(2)}, u32[]{:S(2)}) collective-permute-start(bf16[6,1,128,192]{2,3,1,0:T(8,128)(2,1)S(1)} %get-tuple-element.54), channel_id=1, source_target_pairs={{1,0},{2,1},{3,2},{4,3},{5,4},{6,5},{7,6},{8,7},{9,8},{10,9},{11,1... | collective-permute-start | bytes 884744 | tf_op jit(solution)/shard_map/ppermute | solution.py:15
  78.7 6.1 %collective-permute-start = (bf16[6,1,128,192]{2,3,1,0:T(8,128)(2,1)S(1)}, bf16[6,1,128,192]{2,3,1,0:T(8,128)(2,1)S(1)}, u32[]{:S(2)}, u32[]{:S(2)}) collective-permute-start(bf16[6,1,128,192]{2,3,1,0:T(8,128)(2,1)S(1)} %get-tuple-element.53), channel_id=1, source_target_pairs={{0,1},{1,2},{2,3},{3,4},{4,5},{5,6},{6,7},{7,8},{8,9},{9,10},{10,1... | collective-permute-start | bytes 884744 | tf_op jit(solution)/shard_map/ppermute | solution.py:14
  92.8 2.4 %copy-start.4 = (bf16[4,3,128,1728]{2,3,1,0:T(8,128)(2,1)}, bf16[4,3,128,1728]{2,3,1,0:T(8,128)(2,1)S(1)}, u32[]{:S(2)}) copy-start(bf16[4,3,128,1728]{2,3,1,0:T(8,128)(2,1)S(1)} %get-tuple-element.12) | copy-start | bytes 15925252
  95.2 2.3 %copy-start.5 = (bf16[4,3,128,1728]{2,3,1,0:T(8,128)(2,1)}, bf16[4,3,128,1728]{2,3,1,0:T(8,128)(2,1)S(1)}, u32[]{:S(2)}) copy-start(bf16[4,3,128,1728]{2,3,1,0:T(8,128)(2,1)S(1)} %get-tuple-element.13) | copy-start | bytes 15925252
  97.5 2.4 %copy-start.6 = (bf16[4,3,128,1728]{2,3,1,0:T(8,128)(2,1)}, bf16[4,3,128,1728]{2,3,1,0:T(8,128)(2,1)S(1)}, u32[]{:S(2)}) copy-start(bf16[4,3,128,1728]{2,3,1,0:T(8,128)(2,1)S(1)} %get-tuple-element.14) | copy-start | bytes 15925252
  116.1 8.0 %copy-start.11 = (bf16[1,3,3,192,192]{4,3,2,1,0:T(8,128)(2,1)S(1)}, bf16[1,3,3,192,192]{4,3,2,1,0:T(8,128)(2,1)}, u32[]{:S(2)}) copy-start(bf16[1,3,3,192,192]{4,3,2,1,0:T(8,128)(2,1)} %get-tuple-element.35) | copy-start | bytes 1990660
  124.1 4.7 %copy-start.1 = (bf16[4,3,128,1728]{3,2,1,0:T(8,128)(2,1)S(1)}, bf16[4,3,128,1728]{3,2,1,0:T(8,128)(2,1)}, u32[]{:S(2)}) copy-start(bf16[4,3,128,1728]{3,2,1,0:T(8,128)(2,1)} %copy.86) | copy-start | bytes 15925252
  124.1 4.7 %copy-start.10 = (bf16[1,3,3,192,192]{4,3,2,1,0:T(8,128)(2,1)S(1)}, bf16[1,3,3,192,192]{4,3,2,1,0:T(8,128)(2,1)}, u32[]{:S(2)}) copy-start(bf16[1,3,3,192,192]{4,3,2,1,0:T(8,128)(2,1)} %get-tuple-element.34) | copy-start | bytes 1990660
  124.1 6.7 %slice-start = ((s8[5505024]{0:T(1024)(128)(4,1)}), s8[4194304]{0:T(1024)(128)(4,1)S(1)}, s32[]{:S(2)}) async-start(s8[5505024]{0:T(1024)(128)(4,1)} %bitcast.36), calls=%async_computation.1 | async-start | bytes 8388608
  128.8 2.0 %slice-start.1 = ((s8[5505024]{0:T(1024)(128)(4,1)}), s8[1310720]{0:T(1024)(128)(4,1)S(1)}, s32[]{:S(2)}) async-start(s8[5505024]{0:T(1024)(128)(4,1)} %bitcast.36), calls=%async_computation.2 | async-start | bytes 2621440
  128.8 2.0 %copy-start.9 = (bf16[1,3,3,192,192]{4,3,2,1,0:T(8,128)(2,1)S(1)}, bf16[1,3,3,192,192]{4,3,2,1,0:T(8,128)(2,1)}, u32[]{:S(2)}) copy-start(bf16[1,3,3,192,192]{4,3,2,1,0:T(8,128)(2,1)} %get-tuple-element.33) | copy-start | bytes 1990660
  130.8 2.9 %copy-start.14 = (f32[192]{0:T(256)S(1)}, f32[192]{0:T(256)}, u32[]{:S(2)}) copy-start(f32[192]{0:T(256)} %param.13) | copy-start | bytes 2308
where the time goes:
time: 174 us; the launch traced here: 172 us
  local copies, waits for them, and re-layouts  94.5 us (54%)
  blocking collectives  32.6 us (19%)
  matrix products  18.1 us (10%)
  other arithmetic  15 us (9%)
  starting transfers between devices  10.8 us (6%)
    concatenate x10, local copies, waits for them, and re-layouts, convolve(): stacked = jnp.concatenate(pieces, axis=-1).reshape(-1, 9 * chans)  53.4 us
    all_to_all x1, blocking collectives, body(): lax.all_to_all(feature_grad, 'slab', split_axis=2, concat_axis=1, tiled=T...  32.6 us
    unnamed x63, local copies, waits for them, and re-layouts  24.9 us
    dot_general x6, matrix products, convolve(): jnp.dot(stacked, kernel[t].reshape(9 * chans, -1), preferred_element_type...  18.1 us
    ppermute x2, starting transfers between devices, padded_2(): before = lax.ppermute(last, axis, up)  8.18 us
    slice x5, local copies, waits for them, and re-layouts, convolve(): kernel[t].reshape(9 * chans, -1)  5.89 us
    reshape x2, local copies, waits for them, and re-layouts, convolve(): return total.reshape(frames, rows, cols, -1)  3.88 us
    concatenate x3, other arithmetic, padded_2(): x = jnp.concatenate([before, x, after], axis=dim)  3.74 us
  transfers between devices with their start and end apart: 4, of which 0 were waited for; matrix products, arithmetic and copies ran while one was open for 5% of the time, Pallas kernels for 0%

commit v1 on v0

v1 whole, which is shorter than its diff:
```python
import functools

import jax
import jax.numpy as jnp
from jax import lax
from jax.experimental import pallas as pl
from jax.experimental.pallas import tpu as pltpu
from jax.sharding import PartitionSpec as P

EPS = 1e-06


def column(vector, cols):
    return jnp.transpose(jnp.broadcast_to(vector, (cols, vector.shape[-1])))


def shifted_to(dst, row0, lanes, x, order):
    chans, cols = x.shape
    x32 = x.astype(jnp.float32)
    at = lax.broadcasted_iota(jnp.int32, x.shape, 1)
    for n, s in enumerate(order):
        if s == 0:
            seen = x
        elif s == 1:
            seen = jnp.where(at < cols - 1, pltpu.roll(x32, cols - 1, 1), 0.0)
        else:
            seen = jnp.where(at > 0, pltpu.roll(x32, 1, 1), 0.0)
        dst[row0 + n * chans : row0 + (n + 1) * chans, lanes : lanes + cols] = seen.astype(dst.dtype)


def normalized(x, gain, shift):
    values = x.astype(jnp.float32)
    mean = jnp.sum(values * values, axis=0, keepdims=True) * (1.0 / values.shape[0])
    scale = lax.rsqrt(mean + EPS)
    return values, scale, values * scale * gain + shift


def side_by_side(dst, taps):
    chans = taps[0].shape[0]
    for k in range(0, len(taps), 2):
        pair = taps[k : k + 2]
        dst[:, k * chans : (k + len(pair)) * chans] = pair[0] if len(pair) == 1 else jnp.concatenate(pair, axis=1)


def local_taps(r, rows):
    first = max(r - 1, 0)
    last = min(r + 1, rows - 1)
    return first - (r - 1), last - first + 1, first


def dot(a, b):
    return jnp.dot(a, b, preferred_element_type=jnp.float32)


def grad_sum(lhs_of, stack, lo, hi, frames, cols):
    acc = [None] * frames
    for f0 in range(0, frames, 2):
        for t in range(2, -1, -1):
            g0 = f0 + 2 - t
            count = min(2, frames - g0)
            if count <= 0:
                continue
            part = dot(lhs_of(t), stack[lo:hi, g0 * cols : (g0 + count) * cols])
            for n in range(count):
                piece = part[:, n * cols : (n + 1) * cols]
                acc[f0 + n] = piece if acc[f0 + n] is None else acc[f0 + n] + piece
    return acc


def finish(act_grad, feat, cot, gain, shift):
    values, scale, normed = normalized(feat, gain, shift)
    sig = 1.0 / (1.0 + jnp.exp(-normed))
    norm_grad = act_grad * sig * (1.0 + normed * (1.0 - sig)) * gain
    inner = jnp.sum(norm_grad * values, axis=0, keepdims=True) * (1.0 / values.shape[0])
    return cot.astype(jnp.float32) + scale * norm_grad - values * (scale * scale * scale * inner)


def put_row(out, r, grads, packed):
    frames = len(grads)
    if packed:
        dests = out.shape[0]
        cols = grads[0].shape[1]
        wide = [g[:128] for g in grads]
        for f in range(0, frames, 2):
            wide.append(jnp.concatenate([grads[f][128:], grads[f + 1][128:]], axis=0))
        tiles = [jnp.transpose(w).reshape(dests, cols // dests, 128) for w in wide]
        out[:, r] = jnp.concatenate(tiles, axis=1).astype(jnp.bfloat16)
    else:
        for f in range(frames):
            out[f, r] = jnp.transpose(grads[f]).astype(jnp.bfloat16)


def backward_local_kernel(cot, feat, kern, gain_in, shift_in, out, partial, weights, stack, tail, *, packed):
    frames, rows, chans, cols = cot.shape
    block = 3 * chans
    for t in range(3):
        taps = [kern[t, 2 - d, j] for d in range(3) for j in range(3)]
        side_by_side(weights.at[t], taps)
        side_by_side(tail.at[t], taps[3:])
    for p in range(rows):
        for f in range(frames):
            shifted_to(stack, p * block, f * cols, cot[f, p], (1, 0, -1))
    gain = column(gain_in[...], cols)
    shift = column(shift_in[...], cols)
    edge = 0
    for r in range(rows):
        d0, n, first = local_taps(r, rows)

        def lhs_of(t):
            if d0 == 1:
                return tail[t, :, : n * block]
            return weights[t, :, : n * block]

        acc = grad_sum(lhs_of, stack, first * block, (first + n) * block, frames, cols)
        if n == 3:
            grads = [finish(acc[f], feat[f, r], cot[f, r], gain, shift) for f in range(frames)]
            put_row(out, r, grads, packed)
        else:
            for f in range(frames):
                partial[edge, f] = acc[f]
            edge += 1


def backward_edge_kernel(cot, up, down, feat, partial, weights, before, gain_in, shift_in, out, stack, *, packed):
    frames, rows, chans, cols = cot.shape
    block = 3 * chans
    for f in range(frames):
        shifted_to(stack, 0, f * cols, up[f, 0], (1, 0, -1))
        shifted_to(stack, block, f * cols, down[f, 0], (1, 0, -1))
    gain = column(gain_in[...], cols)
    shift = column(shift_in[...], cols)
    edge = 0
    for r in range(rows):
        if 0 < r < rows - 1:
            if packed:
                out[:, r] = before[:, r]
            else:
                out[:, r] = before[:, r]
            continue
        acc = [partial[edge, f] for f in range(frames)]
        edge += 1
        for d, there in ((0, r == 0), (2, r == rows - 1)):
            if there:
                lo = 0 if d == 0 else block
                more = grad_sum(
                    lambda t: weights[t, :, d * block : (d + 1) * block], stack, lo, lo + block, frames, cols
                )
                acc = [a + b for a, b in zip(acc, more)]
        grads = [finish(acc[f], feat[f, r], cot[f, r], gain, shift) for f in range(frames)]
        put_row(out, r, grads, packed)


def conv_sum(lhs_of, stack, lo, hi, frames, cols):
    acc = []
    for f0 in range(0, frames, 2):
        count = min(2, frames - f0)
        total = None
        for t in range(3):
            part = dot(lhs_of(t), stack[lo:hi, (f0 + t) * cols : (f0 + t + count) * cols])
            total = part if total is None else total + part
        acc += [total[:, n * cols : (n + 1) * cols] for n in range(count)]
    return acc


def activated(x, gain, shift):
    _, _, normed = normalized(x, gain, shift)
    return normed / (1.0 + jnp.exp(-normed))


def forward_local_kernel(feat, cache, kern, gain_in, shift_in, bias_in, out, partial, weights, stack, tail):
    frames, rows, chans, cols = feat.shape
    past = cache.shape[0]
    block = 3 * chans
    gain = column(gain_in[...], cols)
    shift = column(shift_in[...], cols)
    bias = column(bias_in[...], cols)
    for t in range(3):
        whole = jnp.transpose(kern[t].reshape(3 * block, chans))
        weights[t] = whole
        tail[t] = whole[:, block:]
    for p in range(rows):
        for f in range(past):
            shifted_to(stack, p * block, f * cols, cache[f, p], (-1, 0, 1))
        for f in range(frames):
            act = activated(feat[f, p], gain, shift).astype(jnp.bfloat16)
            shifted_to(stack, p * block, (past + f) * cols, act, (-1, 0, 1))
    edge = 0
    for r in range(rows):
        d0, n, first = local_taps(r, rows)

        def lhs_of(t):
            if d0 == 1:
                return tail[t, :, : n * block]
            return weights[t, :, : n * block]

        acc = conv_sum(lhs_of, stack, first * block, (first + n) * block, frames, cols)
        if n == 3:
            for f in range(frames):
                out[f, r] = (feat[f, r].astype(jnp.float32) + acc[f] + bias).astype(jnp.bfloat16)
        else:
            for f in range(frames):
                partial[edge, f] = acc[f]
            edge += 1


def forward_edge_kernel(
    edges, feat, up, down, partial, weights, before, gain_in, shift_in, bias_in, out, stack
):
    frames, rows, chans, cols = feat.shape
    past = up.shape[0] - frames
    block = 3 * chans
    gain = column(gain_in[...], cols)
    shift = column(shift_in[...], cols)
    bias = column(bias_in[...], cols)
    for n, side in enumerate((up, down)):
        for f in range(past):
            shifted_to(stack, n * block, f * cols, side[f, 0], (-1, 0, 1))
        for f in range(past, past + frames):
            act = activated(side[f, 0], gain, shift)
            act = jnp.where(edges[n] > 0, act, 0.0).astype(jnp.bfloat16)
            shifted_to(stack, n * block, f * cols, act, (-1, 0, 1))
    edge = 0
    for r in range(rows):
        if 0 < r < rows - 1:
            out[:, r] = before[:, r]
            continue
        acc = [partial[edge, f] for f in range(frames)]
        edge += 1
        for d, there in ((0, r == 0), (2, r == rows - 1)):
            if there:
                lo = 0 if d == 0 else block
                more = conv_sum(
                    lambda t: weights[t, :, d * block : (d + 1) * block], stack, lo, lo + block, frames, cols
                )
                acc = [a + b for a, b in zip(acc, more)]
        for f in range(frames):
            out[f, r] = (feat[f, r].astype(jnp.float32) + acc[f] + bias).astype(jnp.bfloat16)


def unpack_kernel(src, out):
    frames = out.shape[0]
    for f in range(frames):
        out[f, :, :, :128] = src[:, f * 8 : (f + 1) * 8, :]
        low = (frames + f // 2) * 8
        rest = src[:, low : low + 8, :]
        out[f, :, :, 128:] = rest[:, :, :64] if f % 2 == 0 else rest[:, :, 64:]


VMEM = functools.partial(pl.BlockSpec, memory_space=pltpu.VMEM)
SMEM = functools.partial(pl.BlockSpec, memory_space=pltpu.SMEM)


def call(kernel, name, outs, args, scratch, scalars=0):
    single = not isinstance(outs, list)
    return pl.pallas_call(
        kernel,
        out_shape=outs,
        in_specs=[SMEM()] * scalars + [VMEM()] * (len(args) - scalars),
        out_specs=VMEM() if single else [VMEM()] * len(outs),
        scratch_shapes=[pltpu.VMEM(shape, jnp.bfloat16) for shape in scratch],
        compiler_params=pltpu.CompilerParams(vmem_limit_bytes=24 * 1024 * 1024),
        name=name,
    )(*args)


def body(features, time_cache, cotangent, kernel, norm_gain, norm_shift, conv_bias):
    frames, rows, cols, chans = features.shape
    past = time_cache.shape[0]
    slabs = lax.axis_size("slab")
    index = lax.axis_index("slab")
    up = [(i, i + 1) for i in range(slabs - 1)]
    down = [(i + 1, i) for i in range(slabs - 1)]
    feat = jnp.swapaxes(features, 2, 3)
    cache = jnp.swapaxes(time_cache, 2, 3)
    cot = jnp.swapaxes(cotangent, 2, 3)
    gain = norm_gain.reshape(1, chans)
    shift = norm_shift.reshape(1, chans)
    bias = conv_bias.reshape(1, chans)
    block = 3 * chans
    edge_rows = min(rows, 2)
    per = cols // slabs
    packed = per % 8 == 0 and frames % 2 == 0 and chans == 192
    bf16 = functools.partial(jax.ShapeDtypeStruct, dtype=jnp.bfloat16)
    partial = jax.ShapeDtypeStruct((edge_rows, frames, chans, cols), jnp.float32)
    weights = bf16((3, chans, 3 * block))
    sent = bf16((slabs, rows, frames * per * chans // 128, 128) if packed else (frames, rows, cols, chans))

    cot_up = lax.ppermute(cot[:, rows - 1 :], "slab", up)
    cot_down = lax.ppermute(cot[:, :1], "slab", down)
    grad, part, lhs = call(
        functools.partial(backward_local_kernel, packed=packed),
        "backward_local",
        [sent, partial, weights],
        (cot, feat, kernel, gain, shift),
        [(rows * block, frames * cols), (3, chans, 2 * block)],
    )
    grad = call(
        functools.partial(backward_edge_kernel, packed=packed),
        "backward_edge",
        sent,
        (cot, cot_up, cot_down, feat, part, lhs, grad, gain, shift),
        [(2 * block, frames * cols)],
    )

    if packed:
        moved = lax.all_to_all(grad, "slab", split_axis=0, concat_axis=0, tiled=True)
        moved = moved.reshape(slabs * rows, -1, 128)
        relaid = call(unpack_kernel, "unpack", bf16((frames, slabs * rows, per, chans)), (moved,), [])
    else:
        relaid = lax.all_to_all(grad, "slab", split_axis=2, concat_axis=1, tiled=True)

    feat_b, cache_b, grad = lax.optimization_barrier((feat, cache, grad))
    last = jnp.concatenate([cache_b[:, rows - 1 :], feat_b[:, rows - 1 :]], axis=0)
    first = jnp.concatenate([cache_b[:, :1], feat_b[:, :1]], axis=0)
    above = lax.ppermute(last, "slab", up)
    below = lax.ppermute(first, "slab", down)
    edges = jnp.stack([index, slabs - 1 - index])
    decoded = bf16((frames, rows, chans, cols))
    early, part, lhs = call(
        forward_local_kernel,
        "forward_local",
        [decoded, partial, weights],
        (feat_b, cache_b, kernel, gain, shift, bias),
        [(rows * block, (past + frames) * cols), (3, chans, 2 * block)],
    )
    decoded = call(
        forward_edge_kernel,
        "forward_edge",
        decoded,
        (edges, feat_b, above, below, part, lhs, early, gain, shift, bias),
        [(2 * block, (past + frames) * cols)],
        scalars=1,
    )
    return (jnp.swapaxes(decoded, 2, 3), relaid)


def solution(mesh):
    rows = P(None, ("grp", "slab"), None, None)
    return jax.shard_map(
        body,
        mesh=mesh,
        in_specs=(rows, rows, rows, P(), P(), P(), P()),
        out_specs=(rows, P(None, "grp", "slab", None)),
        check_vma=False,
    )
```

time: 174 us -> 48.9 us (0.28)
  the two profiles are of different devices: /device:TPU:0 before, /device:TPU:13 now
where the time goes in v1:
time: 48.9 us; the launch traced here: 48.3 us
  starting transfers between devices  18.8 us (38%)
  Pallas kernels  13.4 us (27%)
  local copies, waits for them, and re-layouts  7.23 us (15%)
  waiting for transfers between devices  6.46 us (13%)
  other arithmetic  1.58 us (3%)
  between operations  0.8 us (2%)
    pallas_call x5, Pallas kernels, call(): pl.pallas_call(kernel, out_shape=outs, in_specs=[SMEM()] * scalars + [VME...  13.4 us
    all_to_all x1, starting transfers between devices, body(): lax.all_to_all(grad, 'slab', split_axis=0, concat_axis=0, tiled=True)  6.76 us
    ppermute x1, waiting for transfers between devices, body(): below = lax.ppermute(first, 'slab', down)  6.45 us
    unnamed x26, local copies, waits for them, and re-layouts  6.07 us
    ppermute x1, starting transfers between devices, body(): above = lax.ppermute(last, 'slab', up)  4.18 us
    ppermute x1, starting transfers between devices, body(): cot_up = lax.ppermute(cot[:, rows - 1:], 'slab', up)  3.71 us
    ppermute x1, starting transfers between devices, body(): below = lax.ppermute(first, 'slab', down)  2.26 us
    ppermute x1, starting transfers between devices, body(): cot_down = lax.ppermute(cot[:, :1], 'slab', down)  1.92 us
  transfers between devices with their start and end apart: 5, of which 1 were waited for; matrix products, arithmetic and copies ran while one was open for 3% of the time, Pallas kernels for 20%

profile of v1, /device:TPU:13, one launch (start us, length us, event | category | flops | bytes accessed | tf_op | source)
XLA Modules:
  0.0 48.3 jit_solution(8488093780260360300)
XLA Ops:
  0.6 0.0 copy-start.5
  0.6 1.1 %fusion.1 = (bf16[4,1,192,128]{3,2,1,0:T(8,128)(2,1)S(1)}, bf16[4,1,192,128]{3,2,1,0:T(8,128)(2,1)S(1)}) fusion(bf16[4,3,192,128]{3,2,1,0:T(8,128)(2,1)} %bitcast.15), kind=kLoop, calls=%fused_computation.4 | loop fusion | bytes 786432 | tf_op jit(solution)/shard_map/slice | solution.py:289
  1.8 3.7 %collective-permute-start = (bf16[4,1,192,128]{3,2,1,0:T(8,128)(2,1)S(1)}, bf16[4,1,192,128]{3,2,1,0:T(8,128)(2,1)S(1)}, u32[]{:S(2)}, u32[]{:S(2)}) collective-permute-start(bf16[4,1,192,128]{3,2,1,0:T(8,128)(2,1)S(1)} %get-tuple-element.21), channel_id=1, source_target_pairs={{0,1},{1,2},{2,3},{3,4},{4,5},{5,6},{6,7},{7,8},{8,9},{9,10},{10,1... | collective-permute-start | bytes 589832 | tf_op jit(solution)/shard_map/ppermute | solution.py:288
  5.5 1.9 %collective-permute-start.1 = (bf16[4,1,192,128]{3,2,1,0:T(8,128)(2,1)S(1)}, bf16[4,1,192,128]{3,2,1,0:T(8,128)(2,1)S(1)}, u32[]{:S(2)}, u32[]{:S(2)}) collective-permute-start(bf16[4,1,192,128]{3,2,1,0:T(8,128)(2,1)S(1)} %get-tuple-element.20), channel_id=1, source_target_pairs={{1,0},{2,1},{3,2},{4,3},{5,4},{6,5},{7,6},{8,7},{9,8},{10,9},{11,1... | collective-permute-start | bytes 589832 | tf_op jit(solution)/shard_map/ppermute | solution.py:289
  7.4 0.0 copy-start
  7.4 1.1 %copy-done = bf16[4,3,128,192]{2,3,1,0:T(8,128)(2,1)S(1)} copy-done((bf16[4,3,128,192]{2,3,1,0:T(8,128)(2,1)S(1)}, bf16[4,3,128,192]{2,3,1,0:T(8,128)(2,1)}, u32[]{:S(2)}) %copy-start) | copy-done | bytes 589848
  8.5 1.7 %copy-done.2 = bf16[3,3,3,192,192]{4,3,2,1,0:T(8,128)(2,1)S(1)} copy-done((bf16[3,3,3,192,192]{4,3,2,1,0:T(8,128)(2,1)S(1)}, bf16[3,3,3,192,192]{4,3,2,1,0:T(8,128)(2,1)}, u32[]{:S(2)}) %copy-start.2) | copy-done | bytes 1990680
  10.2 1.1 %copy-done.4 = bf16[4,3,128,192]{2,3,1,0:T(8,128)(2,1)S(1)} copy-done((bf16[4,3,128,192]{2,3,1,0:T(8,128)(2,1)S(1)}, bf16[4,3,128,192]{2,3,1,0:T(8,128)(2,1)}, u32[]{:S(2)}) %copy-start.4) | copy-done | bytes 589848
  11.3 0.7 %copy-done.8 = f32[192]{0:T(256)S(1)} copy-done((f32[192]{0:T(256)S(1)}, f32[192]{0:T(256)}, u32[]{:S(2)}) %copy-start.8) | copy-done | bytes 792
  12.0 0.7 %copy-done.10 = f32[192]{0:T(256)S(1)} copy-done((f32[192]{0:T(256)S(1)}, f32[192]{0:T(256)}, u32[]{:S(2)}) %copy-start.10) | copy-done | bytes 792
  12.6 2.7 %backward_local.1 = (bf16[16,3,48,128]{3,2,1,0:T(8,128)(2,1)S(1)}, f32[2,4,192,128]{3,2,1,0:T(8,128)S(1)}, bf16[3,192,1728]{2,1,0:T(8,128)(2,1)S(1)}) custom-call(bf16[4,3,192,128]{3,2,1,0:T(8,128)(2,1)S(1)} %bitcast.16, bf16[4,3,192,128]{3,2,1,0:T(8,128)(2,1)S(1)} %bitcast.10, bf16[3,3,3,192,192]{4,3,2,1,0:T(8,128)(2,1)S(1)} %copy-done.2, ...), custom_call_target="tpu_custom_call" | custom-call | tf_op jit(solution)/shard_map/backward_local/pallas_call | solution.py:255
  15.4 0.0 collective-permute-done.up
  15.4 0.0 collective-permute-done.1.down
  15.4 0.0 copy-done.5
  15.4 0.0 copy-start.7
  15.4 0.0 copy-start.1
  15.4 1.4 %backward_edge.1 = bf16[16,3,48,128]{3,2,1,0:T(8,128)(2,1)S(1)} custom-call(bf16[4,3,192,128]{3,2,1,0:T(8,128)(2,1)S(1)} %bitcast.17, bf16[4,1,192,128]{3,2,1,0:T(8,128)(2,1)S(1)} %collective-permute-done.up, bf16[4,1,192,128]{3,2,1,0:T(8,128)(2,1)S(1)} %collective-permute-done.1.down, bf16[4,3,192,128]{3,2,1,0:T(8,128)(2,1)S(1)} %bitcast.11, ...), custom_call_target="tpu_custom_call" | custom-call | tf_op jit(solution)/shard_map/backward_edge/pallas_call | solution.py:255
  16.9 0.0 copy-start.6
  16.9 0.8 %copy-done.6 = bf16[16,3,48,128]{3,2,1,0:T(8,128)(2,1)} copy-done((bf16[16,3,48,128]{3,2,1,0:T(8,128)(2,1)}, bf16[16,3,48,128]{3,2,1,0:T(8,128)(2,1)S(1)}, u32[]{:S(2)}) %copy-start.6) | copy-done | bytes 589848
  17.7 6.8 %all-to-all-start = ((bf16[16,3,48,128]{3,2,1,0:T(8,128)(2,1)}), bf16[16,3,48,128]{3,2,1,0:T(8,128)(2,1)}, u32[]{:S(2)}, u32[]{:S(2)}) async-start(bf16[16,3,48,128]{3,2,1,0:T(8,128)(2,1)} %copy-done.6), calls=%async_computation | async-start | bytes 1179648 | tf_op jit(solution)/shard_map/all_to_all | solution.py:306
  24.5 0.0 copy-done.7
  24.6 0.8 %pad_maximum_fusion.1 = bf16[6,1,192,128]{3,2,1,0:T(8,128)(2,1)} fusion(bf16[4,1,192,128]{3,2,1,0:T(8,128)(2,1)S(1)} %get-tuple-element.18, bf16[2,1,192,128]{3,2,1,0:T(8,128)(2,1)S(1)} %get-tuple-element.22), kind=kLoop, calls=%fused_computation.1 | loop fusion | flops 147456 | bytes 589824 | tf_op jit(solution)/shard_map/concatenate | solution.py:314
  25.3 2.3 %collective-permute-start.3 = (bf16[6,1,192,128]{3,2,1,0:T(8,128)(2,1)}, bf16[6,1,192,128]{3,2,1,0:T(8,128)(2,1)}, u32[]{:S(2)}, u32[]{:S(2)}) collective-permute-start(bf16[6,1,192,128]{3,2,1,0:T(8,128)(2,1)} %pad_maximum_fusion.1), channel_id=1, source_target_pairs={{1,0},{2,1},{3,2},{4,3},{5,4},{6,5},{7,6},{8,7},{9,8},{10,9},{11,1... | collective-permute-start | bytes 884744 | tf_op jit(solution)/shard_map/ppermute | solution.py:316
  27.6 0.7 %pad_maximum_fusion = bf16[6,1,192,128]{3,2,1,0:T(8,128)(2,1)} fusion(bf16[4,1,192,128]{3,2,1,0:T(8,128)(2,1)S(1)} %get-tuple-element.19, bf16[2,1,192,128]{3,2,1,0:T(8,128)(2,1)S(1)} %get-tuple-element.23), kind=kLoop, calls=%fused_computation | loop fusion | flops 147456 | bytes 589824 | tf_op jit(solution)/shard_map/concatenate | solution.py:313
  28.3 4.2 %collective-permute-start.2 = (bf16[6,1,192,128]{3,2,1,0:T(8,128)(2,1)}, bf16[6,1,192,128]{3,2,1,0:T(8,128)(2,1)}, u32[]{:S(2)}, u32[]{:S(2)}) collective-permute-start(bf16[6,1,192,128]{3,2,1,0:T(8,128)(2,1)} %pad_maximum_fusion), channel_id=1, source_target_pairs={{0,1},{1,2},{2,3},{3,4},{4,5},{5,6},{6,7},{7,8},{8,9},{9,10},{10,1... | collective-permute-start | bytes 884744 | tf_op jit(solution)/shard_map/ppermute | solution.py:315
  32.5 0.1 pad_add_fusion.edges
  32.6 3.7 %forward_local.1 = (bf16[4,3,192,128]{3,2,1,0:T(8,128)(2,1)S(1)}, f32[2,4,192,128]{3,2,1,0:T(8,128)S(1)}, bf16[3,192,1728]{2,1,0:T(8,128)(2,1)S(1)}) custom-call(bf16[4,3,192,128]{3,2,1,0:T(8,128)(2,1)S(1)} %bitcast.13, bf16[2,3,192,128]{3,2,1,0:T(8,128)(2,1)S(1)} %bitcast.19, bf16[3,3,3,192,192]{4,3,2,1,0:T(8,128)(2,1)S(1)} %copy-done.3, ...), custom_call_target="tpu_custom_call" | custom-call | tf_op jit(solution)/shard_map/forward_local/pallas_call | solution.py:255
  36.3 6.5 %collective-permute-done.3.down = bf16[6,1,192,128]{3,2,1,0:T(8,128)(2,1)} collective-permute-done((bf16[6,1,192,128]{3,2,1,0:T(8,128)(2,1)}, bf16[6,1,192,128]{3,2,1,0:T(8,128)(2,1)}, u32[]{:S(2)}, u32[]{:S(2)}) %collective-permute-start.3) | collective-permute-done | bytes 294944 | tf_op jit(solution)/shard_map/ppermute | solution.py:316
  42.8 0.0 collective-permute-done.2.up
  42.8 3.5 %forward_edge.1 = bf16[4,3,192,128]{3,2,1,0:T(8,128)(2,1)} custom-call(s32[2]{0:T(128)S(1)} %pad_add_fusion.edges, bf16[4,3,192,128]{3,2,1,0:T(8,128)(2,1)S(1)} %bitcast.14, bf16[6,1,192,128]{3,2,1,0:T(8,128)(2,1)} %collective-permute-done.2.up, bf16[6,1,192,128]{3,2,1,0:T(8,128)(2,1)} %collective-permute-done.3.down, ...), custom_call_target="tpu_custom_call" | custom-call | tf_op jit(solution)/shard_map/forward_edge/pallas_call | solution.py:255
  46.2 0.0 all-to-all-done
  46.2 2.1 %unpack.1 = bf16[4,48,8,192]{3,2,1,0:T(8,128)(2,1)} custom-call(bf16[48,48,128]{2,1,0:T(8,128)(2,1)} %bitcast.9.src), custom_call_target="tpu_custom_call" | custom-call | tf_op jit(solution)/shard_map/unpack/pallas_call | solution.py:255
  (15 shorter events, 0.1 us)
Async XLA Ops:
  0.6 14.8 %copy-start.5 = (bf16[4,3,128,192]{2,3,1,0:T(8,128)(2,1)S(1)}, bf16[4,3,128,192]{2,3,1,0:T(8,128)(2,1)}, u32[]{:S(2)}) copy-start(bf16[4,3,128,192]{2,3,1,0:T(8,128)(2,1)} %param.9) | copy-start | bytes 1769476
  1.8 13.6 %collective-permute-start = (bf16[4,1,192,128]{3,2,1,0:T(8,128)(2,1)S(1)}, bf16[4,1,192,128]{3,2,1,0:T(8,128)(2,1)S(1)}, u32[]{:S(2)}, u32[]{:S(2)}) collective-permute-start(bf16[4,1,192,128]{3,2,1,0:T(8,128)(2,1)S(1)} %get-tuple-element.21), channel_id=1, source_target_pairs={{0,1},{1,2},{2,3},{3,4},{4,5},{5,6},{6,7},{7,8},{8,9},{9,10},{10,1... | collective-permute-start | bytes 589832 | tf_op jit(solution)/shard_map/ppermute | solution.py:288
  5.5 9.9 %collective-permute-start.1 = (bf16[4,1,192,128]{3,2,1,0:T(8,128)(2,1)S(1)}, bf16[4,1,192,128]{3,2,1,0:T(8,128)(2,1)S(1)}, u32[]{:S(2)}, u32[]{:S(2)}) collective-permute-start(bf16[4,1,192,128]{3,2,1,0:T(8,128)(2,1)S(1)} %get-tuple-element.20), channel_id=1, source_target_pairs={{1,0},{2,1},{3,2},{4,3},{5,4},{6,5},{7,6},{8,7},{9,8},{10,9},{11,1... | collective-permute-start | bytes 589832 | tf_op jit(solution)/shard_map/ppermute | solution.py:289
  7.4 1.1 %copy-start = (bf16[4,3,128,192]{2,3,1,0:T(8,128)(2,1)S(1)}, bf16[4,3,128,192]{2,3,1,0:T(8,128)(2,1)}, u32[]{:S(2)}) copy-start(bf16[4,3,128,192]{2,3,1,0:T(8,128)(2,1)} %param.7) | copy-start | bytes 1769476
  8.5 1.7 %copy-start.2 = (bf16[3,3,3,192,192]{4,3,2,1,0:T(8,128)(2,1)S(1)}, bf16[3,3,3,192,192]{4,3,2,1,0:T(8,128)(2,1)}, u32[]{:S(2)}) copy-start(bf16[3,3,3,192,192]{4,3,2,1,0:T(8,128)(2,1)} %kern.3) | copy-start | bytes 5971972
  10.2 1.1 %copy-start.4 = (bf16[4,3,128,192]{2,3,1,0:T(8,128)(2,1)S(1)}, bf16[4,3,128,192]{2,3,1,0:T(8,128)(2,1)}, u32[]{:S(2)}) copy-start(bf16[4,3,128,192]{2,3,1,0:T(8,128)(2,1)} %param.9) | copy-start | bytes 1769476
  11.3 0.7 %copy-start.8 = (f32[192]{0:T(256)S(1)}, f32[192]{0:T(256)}, u32[]{:S(2)}) copy-start(f32[192]{0:T(256)} %param.11) | copy-start | bytes 2308
  12.0 0.7 %copy-start.10 = (f32[192]{0:T(256)S(1)}, f32[192]{0:T(256)}, u32[]{:S(2)}) copy-start(f32[192]{0:T(256)} %param.12) | copy-start | bytes 2308
  15.4 9.1 %copy-start.7 = (bf16[2,3,128,192]{2,3,1,0:T(8,128)(2,1)S(1)}, bf16[2,3,128,192]{2,3,1,0:T(8,128)(2,1)}, u32[]{:S(2)}) copy-start(bf16[2,3,128,192]{2,3,1,0:T(8,128)(2,1)} %param.8) | copy-start | bytes 884740
  15.4 9.1 %copy-start.1 = (bf16[4,3,128,192]{2,3,1,0:T(8,128)(2,1)S(1)}, bf16[4,3,128,192]{2,3,1,0:T(8,128)(2,1)}, u32[]{:S(2)}) copy-start(bf16[4,3,128,192]{2,3,1,0:T(8,128)(2,1)} %param.7) | copy-start | bytes 1769476
  16.9 0.8 %copy-start.6 = (bf16[16,3,48,128]{3,2,1,0:T(8,128)(2,1)}, bf16[16,3,48,128]{3,2,1,0:T(8,128)(2,1)S(1)}, u32[]{:S(2)}) copy-start(bf16[16,3,48,128]{3,2,1,0:T(8,128)(2,1)S(1)} %backward_edge.1) | copy-start | bytes 1769476
  17.7 14.9 %copy-start.3 = (bf16[3,3,3,192,192]{4,3,2,1,0:T(8,128)(2,1)S(1)}, bf16[3,3,3,192,192]{4,3,2,1,0:T(8,128)(2,1)}, u32[]{:S(2)}) copy-start(bf16[3,3,3,192,192]{4,3,2,1,0:T(8,128)(2,1)} %kern.3) | copy-start | bytes 5971972
  17.7 14.9 %copy-start.9 = (f32[192]{0:T(256)S(1)}, f32[192]{0:T(256)}, u32[]{:S(2)}) copy-start(f32[192]{0:T(256)} %param.11) | copy-start | bytes 2308
  17.7 14.9 %copy-start.11 = (f32[192]{0:T(256)S(1)}, f32[192]{0:T(256)}, u32[]{:S(2)}) copy-start(f32[192]{0:T(256)} %param.12) | copy-start | bytes 2308
  17.7 14.9 %copy-start.12 = (f32[192]{0:T(256)S(1)}, f32[192]{0:T(256)}, u32[]{:S(2)}) copy-start(f32[192]{0:T(256)} %param.13) | copy-start | bytes 2308
  17.7 28.5 %all-to-all-start = ((bf16[16,3,48,128]{3,2,1,0:T(8,128)(2,1)}), bf16[16,3,48,128]{3,2,1,0:T(8,128)(2,1)}, u32[]{:S(2)}, u32[]{:S(2)}) async-start(bf16[16,3,48,128]{3,2,1,0:T(8,128)(2,1)} %copy-done.6), calls=%async_computation | async-start | bytes 1179648 | tf_op jit(solution)/shard_map/all_to_all | solution.py:306
  25.3 17.5 %collective-permute-start.3 = (bf16[6,1,192,128]{3,2,1,0:T(8,128)(2,1)}, bf16[6,1,192,128]{3,2,1,0:T(8,128)(2,1)}, u32[]{:S(2)}, u32[]{:S(2)}) collective-permute-start(bf16[6,1,192,128]{3,2,1,0:T(8,128)(2,1)} %pad_maximum_fusion.1), channel_id=1, source_target_pairs={{1,0},{2,1},{3,2},{4,3},{5,4},{6,5},{7,6},{8,7},{9,8},{10,9},{11,1... | collective-permute-start | bytes 884744 | tf_op jit(solution)/shard_map/ppermute | solution.py:316
  28.3 14.4 %collective-permute-start.2 = (bf16[6,1,192,128]{3,2,1,0:T(8,128)(2,1)}, bf16[6,1,192,128]{3,2,1,0:T(8,128)(2,1)}, u32[]{:S(2)}, u32[]{:S(2)}) collective-permute-start(bf16[6,1,192,128]{3,2,1,0:T(8,128)(2,1)} %pad_maximum_fusion), channel_id=1, source_target_pairs={{0,1},{1,2},{2,3},{3,4},{4,5},{5,6},{6,7},{7,8},{8,9},{9,10},{10,1... | collective-permute-start | bytes 884744 | tf_op jit(solution)/shard_map/ppermute | solution.py:315

commit v2 on v1

v2 whole, which is shorter than its diff:
```python
import functools

import jax
import jax.numpy as jnp
from jax import lax
from jax.experimental import pallas as pl
from jax.experimental.pallas import tpu as pltpu
from jax.sharding import PartitionSpec as P

EPS = 1e-06


def column(vector, cols):
    return jnp.transpose(jnp.broadcast_to(vector, (cols, vector.shape[-1])))


def shifted_to(dst, row0, lanes, x, order):
    chans, cols = x.shape
    x32 = x.astype(jnp.float32)
    at = lax.broadcasted_iota(jnp.int32, x.shape, 1)
    for n, s in enumerate(order):
        if s == 0:
            seen = x
        elif s == 1:
            seen = jnp.where(at < cols - 1, pltpu.roll(x32, cols - 1, 1), 0.0)
        else:
            seen = jnp.where(at > 0, pltpu.roll(x32, 1, 1), 0.0)
        dst[row0 + n * chans : row0 + (n + 1) * chans, lanes : lanes + cols] = seen.astype(dst.dtype)


def normalized(x, gain, shift):
    values = x.astype(jnp.float32)
    mean = jnp.sum(values * values, axis=0, keepdims=True) * (1.0 / values.shape[0])
    scale = lax.rsqrt(mean + EPS)
    return values, scale, values * scale * gain + shift


def side_by_side(dst, taps):
    chans = taps[0].shape[0]
    for k in range(0, len(taps), 2):
        pair = taps[k : k + 2]
        dst[:, k * chans : (k + len(pair)) * chans] = pair[0] if len(pair) == 1 else jnp.concatenate(pair, axis=1)


def local_taps(r, rows):
    first = max(r - 1, 0)
    last = min(r + 1, rows - 1)
    return first - (r - 1), last - first + 1, first


def dot(a, b):
    return jnp.dot(a, b, preferred_element_type=jnp.float32)


def grad_sum(lhs_of, stack, lo, hi, frames, cols):
    acc = [None] * frames
    for f0 in range(0, frames, 2):
        for t in range(2, -1, -1):
            g0 = f0 + 2 - t
            count = min(2, frames - g0)
            if count <= 0:
                continue
            part = dot(lhs_of(t), stack[lo:hi, g0 * cols : (g0 + count) * cols])
            for n in range(count):
                piece = part[:, n * cols : (n + 1) * cols]
                acc[f0 + n] = piece if acc[f0 + n] is None else acc[f0 + n] + piece
    return acc


def finish(act_grad, feat, cot, gain, shift):
    values, scale, normed = normalized(feat, gain, shift)
    sig = 1.0 / (1.0 + jnp.exp(-normed))
    norm_grad = act_grad * sig * (1.0 + normed * (1.0 - sig)) * gain
    inner = jnp.sum(norm_grad * values, axis=0, keepdims=True) * (1.0 / values.shape[0])
    return cot.astype(jnp.float32) + scale * norm_grad - values * (scale * scale * scale * inner)


def put_row(out, r, grads, packed):
    frames = len(grads)
    if packed:
        dests = out.shape[0]
        cols = grads[0].shape[1]
        wide = [g[:128] for g in grads]
        for f in range(0, frames, 2):
            wide.append(jnp.concatenate([grads[f][128:], grads[f + 1][128:]], axis=0))
        tiles = [jnp.transpose(w).reshape(dests, cols // dests, 128) for w in wide]
        out[:, r] = jnp.concatenate(tiles, axis=1).astype(jnp.bfloat16)
    else:
        for f in range(frames):
            out[f, r] = jnp.transpose(grads[f]).astype(jnp.bfloat16)


def fetch(pairs, sems):
    copies = [pltpu.make_async_copy(s, d, sems.at[n]) for n, (s, d) in enumerate(pairs)]
    for c in copies:
        c.start()
    return copies


def rows_sent(rows):
    inner = jnp.where(lax.rem(lax.axis_index("slab"), 2) == 0, rows - 1, 0)
    return inner, rows - 1 - inner


def staging_kernel(cot, to_inner, to_outer, sems):
    inner, outer = rows_sent(cot.shape[1])
    for c in fetch([(cot.at[:, inner], to_inner), (cot.at[:, outer], to_outer)], sems):
        c.wait()


def backward_local_kernel(
    cot_hbm, feat_hbm, cache_hbm, kern_hbm, gain_hbm, shift_hbm,
    out, to_inner, to_outer, partial, weights, cot, feat, kern, gain_in, shift_in,
    stack, tail, sent, past_rows, sems, edge_sems, out_sem, *, packed,
):
    frames, rows, chans, cols = cot.shape
    past = cache_hbm.shape[0]
    block = 3 * chans
    edges = list(zip(rows_sent(rows), (to_inner, to_outer)))
    copies = fetch(
        [(cot_hbm, cot), (kern_hbm.at[2], kern.at[2]), (kern_hbm.at[1], kern.at[1]), (kern_hbm.at[0], kern.at[0]),
         (gain_hbm, gain_in), (shift_hbm, shift_in), (feat_hbm, feat)]
        + [(cache_hbm.at[:, row], past_rows.at[n]) for n, (row, _) in enumerate(edges)],
        sems,
    )
    copies[0].wait()
    for p in range(rows):
        for f in range(frames):
            shifted_to(stack, p * block, f * cols, cot[f, p], (1, 0, -1))
    for n, t in ((1, 2), (2, 1), (3, 0)):
        copies[n].wait()
        taps = [kern[t, 2 - d, j] for d in range(3) for j in range(3)]
        side_by_side(weights.at[t], taps)
        side_by_side(tail.at[t], taps[3:])
    for c in copies[4:]:
        c.wait()
    written = fetch(
        [(feat.at[:, row], to.at[pl.ds(past, frames)]) for row, to in edges]
        + [(past_rows.at[n], to.at[pl.ds(0, past)]) for n, (_, to) in enumerate(edges)],
        edge_sems,
    )
    gain = column(gain_in[...], cols)
    shift = column(shift_in[...], cols)
    for r in list(range(1, rows - 1)) + sorted({0, rows - 1}):
        d0, n, first = local_taps(r, rows)

        def lhs_of(t):
            if d0 == 1:
                return tail[t, :, : n * block]
            return weights[t, :, : n * block]

        acc = grad_sum(lhs_of, stack, first * block, (first + n) * block, frames, cols)
        if n == 3:
            grads = [finish(acc[f], feat[f, r], cot[f, r], gain, shift) for f in range(frames)]
            put_row(sent, r - 1, grads, packed)
            written.append(pltpu.make_async_copy(sent.at[:, r - 1], out.at[:, r], out_sem.at[r - 1]))
            written[-1].start()
        else:
            for f in range(frames):
                partial[min(r, 1), f] = acc[f]
    for c in written:
        c.wait()


def backward_edge_kernel(
    cot, inner, outer, feat, partial, weights, gain_in, shift_in, before, out, stack, sent, out_sem, *, packed
):
    del before
    frames, rows, chans, cols = cot.shape
    block = 3 * chans
    slot = jnp.where(lax.rem(lax.axis_index("slab"), 2) == 0, 1, 0)
    for f in range(frames):
        shifted_to(stack.at[slot], 0, f * cols, inner[f], (1, 0, -1))
        shifted_to(stack.at[1 - slot], 0, f * cols, outer[f], (1, 0, -1))
    gain = column(gain_in[...], cols)
    shift = column(shift_in[...], cols)
    written = []
    for edge, r in enumerate(sorted({0, rows - 1})):
        acc = [partial[edge, f] for f in range(frames)]
        for d, there in ((0, r == 0), (2, r == rows - 1)):
            if there:
                more = grad_sum(
                    lambda t: weights[t, :, d * block : (d + 1) * block], stack.at[d // 2], 0, block, frames, cols
                )
                acc = [a + b for a, b in zip(acc, more)]
        grads = [finish(acc[f], feat[f, r], cot[f, r], gain, shift) for f in range(frames)]
        put_row(sent, edge, grads, packed)
        written.append(pltpu.make_async_copy(sent.at[:, edge], out.at[:, r], out_sem.at[edge]))
        written[-1].start()
    for c in written:
        c.wait()


def conv_sum(lhs_of, stack, lo, hi, frames, cols):
    acc = []
    for f0 in range(0, frames, 2):
        count = min(2, frames - f0)
        total = None
        for t in range(3):
            part = dot(lhs_of(t), stack[lo:hi, (f0 + t) * cols : (f0 + t + count) * cols])
            total = part if total is None else total + part
        acc += [total[:, n * cols : (n + 1) * cols] for n in range(count)]
    return acc


def activated(x, gain, shift):
    _, _, normed = normalized(x, gain, shift)
    return normed / (1.0 + jnp.exp(-normed))


def forward_local_kernel(
    feat, cache, kern, gain_in, shift_in, bias_in, out, partial, weights, stack, tail, ready, out_sem
):
    frames, rows, chans, cols = feat.shape
    past = cache.shape[0]
    block = 3 * chans
    gain = column(gain_in[...], cols)
    shift = column(shift_in[...], cols)
    bias = column(bias_in[...], cols)
    for t in range(3):
        whole = jnp.transpose(kern[t].reshape(3 * block, chans))
        weights[t] = whole
        tail[t] = whole[:, block:]
    for p in range(rows):
        for f in range(past):
            shifted_to(stack, p * block, f * cols, cache[f, p], (-1, 0, 1))
        for f in range(frames):
            act = activated(feat[f, p], gain, shift).astype(jnp.bfloat16)
            shifted_to(stack, p * block, (past + f) * cols, act, (-1, 0, 1))
    written = []
    for r in list(range(1, rows - 1)) + sorted({0, rows - 1}):
        d0, n, first = local_taps(r, rows)

        def lhs_of(t):
            if d0 == 1:
                return tail[t, :, : n * block]
            return weights[t, :, : n * block]

        acc = conv_sum(lhs_of, stack, first * block, (first + n) * block, frames, cols)
        decoded = [feat[f, r].astype(jnp.float32) + acc[f] + bias for f in range(frames)]
        if n == 3:
            for f in range(frames):
                ready[f, r - 1] = decoded[f].astype(jnp.bfloat16)
            written.append(pltpu.make_async_copy(ready.at[:, r - 1], out.at[:, r], out_sem.at[r - 1]))
            written[-1].start()
        else:
            for f in range(frames):
                partial[min(r, 1), f] = decoded[f]
    for c in written:
        c.wait()


def forward_edge_kernel(
    inner_hbm, outer_hbm, partial, weights, gain_in, shift_in, before, out, inner, outer, stack, ready, sems, out_sem
):
    del before
    rows = out.shape[1]
    frames, chans, cols = partial.shape[1:]
    past = inner.shape[0] - frames
    block = 3 * chans
    arriving = fetch([(inner_hbm, inner), (outer_hbm, outer)], sems)
    index = lax.axis_index("slab")
    slot = jnp.where(lax.rem(index, 2) == 0, 1, 0)
    inside = jnp.logical_and(index > 0, index < lax.axis_size("slab") - 1)
    gain = column(gain_in[...], cols)
    shift = column(shift_in[...], cols)
    for n, (side, to, held) in enumerate(((inner, slot, None), (outer, 1 - slot, inside))):
        arriving[n].wait()
        for f in range(past):
            shifted_to(stack.at[to], 0, f * cols, side[f], (-1, 0, 1))
        for f in range(past, past + frames):
            act = activated(side[f], gain, shift)
            if held is not None:
                act = jnp.where(held, act, 0.0)
            shifted_to(stack.at[to], 0, f * cols, act.astype(jnp.bfloat16), (-1, 0, 1))
    written = []
    for edge, r in enumerate(sorted({0, rows - 1})):
        acc = [partial[edge, f] for f in range(frames)]
        for d, there in ((0, r == 0), (2, r == rows - 1)):
            if there:
                more = conv_sum(
                    lambda t: weights[t, :, d * block : (d + 1) * block], stack.at[d // 2], 0, block, frames, cols
                )
                acc = [a + b for a, b in zip(acc, more)]
        for f in range(frames):
            ready[f, edge] = acc[f].astype(jnp.bfloat16)
        written.append(pltpu.make_async_copy(ready.at[:, edge], out.at[:, r], out_sem.at[edge]))
        written[-1].start()
    for c in written:
        c.wait()


def unpack_kernel(src_hbm, out_hbm, src, out, in_sem, out_sem):
    frames, lines = out.shape[:2]
    parts = in_sem.shape[0]
    step = lines // parts
    spans = [pl.ds(n * step, step) for n in range(parts)]
    arriving = fetch([(src_hbm.at[s], src.at[s]) for s in spans], in_sem)
    leaving = [pltpu.make_async_copy(out.at[:, s], out_hbm.at[:, s], out_sem.at[n]) for n, s in enumerate(spans)]
    for n, s in enumerate(spans):
        arriving[n].wait()
        for f in range(frames):
            out[f, s, :, :128] = src[s, f * 8 : (f + 1) * 8, :]
            low = (frames + f // 2) * 8
            rest = src[s, low : low + 8, :]
            out[f, s, :, 128:] = rest[:, :, :64] if f % 2 == 0 else rest[:, :, 64:]
        leaving[n].start()
    for c in leaving:
        c.wait()


VMEM = functools.partial(pl.BlockSpec, memory_space=pltpu.VMEM)
HBM = functools.partial(pl.BlockSpec, memory_space=pltpu.HBM)


def call(kernel, name, ins, outs, scratch=(), aliases=None):
    result = pl.pallas_call(
        kernel,
        out_shape=[pltpu.HBM(o.shape, o.dtype) if where is HBM else o for o, where in outs],
        in_specs=[where() for _, where in ins],
        out_specs=[where() for _, where in outs],
        scratch_shapes=list(scratch),
        input_output_aliases=aliases or {},
        compiler_params=pltpu.CompilerParams(vmem_limit_bytes=24 * 1024 * 1024),
        name=name,
    )(*[pltpu.with_memory_space_constraint(a, pltpu.HBM) if where is HBM else a for a, where in ins])
    return result[0] if len(outs) == 1 else result


def body(features, time_cache, cotangent, kernel, norm_gain, norm_shift, conv_bias):
    frames, rows, cols, chans = features.shape
    past = time_cache.shape[0]
    slabs = lax.axis_size("slab")
    within = [(i, i ^ 1) for i in range(slabs)]
    across = [(i, i + 1) for i in range(1, slabs - 1, 2)] + [(i + 1, i) for i in range(1, slabs - 1, 2)]
    feat = jnp.swapaxes(features, 2, 3)
    cache = jnp.swapaxes(time_cache, 2, 3)
    cot = jnp.swapaxes(cotangent, 2, 3)
    gain = norm_gain.reshape(1, chans)
    shift = norm_shift.reshape(1, chans)
    bias = conv_bias.reshape(1, chans)
    block = 3 * chans
    edge_rows = min(rows, 2)
    per = cols // slabs
    packed = per % 8 == 0 and frames % 2 == 0 and chans == 192
    bf16 = functools.partial(jax.ShapeDtypeStruct, dtype=jnp.bfloat16)
    vmem16 = functools.partial(pltpu.VMEM, dtype=jnp.bfloat16)
    partial = jax.ShapeDtypeStruct((edge_rows, frames, chans, cols), jnp.float32)
    weights = bf16((3, chans, 3 * block))

    def sent(n):
        return (slabs, n, frames * per * chans // 128, 128) if packed else (frames, n, cols, chans)

    cot_in, cot_across = call(
        staging_kernel,
        "staging",
        [(cot, HBM)],
        [(bf16((frames, chans, cols)), VMEM)] * 2,
        [pltpu.SemaphoreType.DMA((2,))],
    )
    cot_in = lax.ppermute(cot_in, "slab", within)
    cot_across = lax.ppermute(cot_across, "slab", across)
    grad, act_in, act_across, part, lhs, cot_v, feat_v, kern_v, gain_v, shift_v = call(
        functools.partial(backward_local_kernel, packed=packed),
        "backward_local",
        [(a, HBM) for a in (cot, feat, cache, kernel, gain, shift)],
        [(bf16(sent(rows)), HBM)]
        + [(bf16((past + frames, chans, cols)), HBM)] * 2
        + [(partial, VMEM), (weights, VMEM)]
        + [(jax.ShapeDtypeStruct(a.shape, a.dtype), VMEM) for a in (cot, feat, kernel, gain, shift)],
        [
            vmem16((rows * block, frames * cols)),
            vmem16((3, chans, 2 * block)),
            vmem16(sent(max(rows - 2, 1))),
            vmem16((2, past, chans, cols)),
            pltpu.SemaphoreType.DMA((9,)),
            pltpu.SemaphoreType.DMA((4,)),
            pltpu.SemaphoreType.DMA((max(rows - 2, 1),)),
        ],
    )
    grad = call(
        functools.partial(backward_edge_kernel, packed=packed),
        "backward_edge",
        [(a, VMEM) for a in (cot_v, cot_in, cot_across, feat_v, part, lhs, gain_v, shift_v)] + [(grad, HBM)],
        [(bf16(sent(rows)), HBM)],
        [vmem16((2, block, frames * cols)), vmem16(sent(edge_rows)), pltpu.SemaphoreType.DMA((edge_rows,))],
        aliases={8: 0},
    )

    if packed:
        moved = lax.all_to_all(grad, "slab", split_axis=0, concat_axis=0, tiled=True)
        moved = moved.reshape(slabs * rows, -1, 128)
        relaid = (frames, slabs * rows, per, chans)
        parts = 4 if slabs * rows % 4 == 0 else 1
        relaid = call(
            unpack_kernel,
            "unpack",
            [(moved, HBM)],
            [(bf16(relaid), HBM)],
            [vmem16(moved.shape), vmem16(relaid), pltpu.SemaphoreType.DMA((parts,)), pltpu.SemaphoreType.DMA((parts,))],
        )
    else:
        relaid = lax.all_to_all(grad, "slab", split_axis=2, concat_axis=1, tiled=True)

    act_in, act_across, feat_v, kern_v, gain_v, shift_v, _ = lax.optimization_barrier(
        (act_in, act_across, feat_v, kern_v, gain_v, shift_v, grad)
    )
    act_in = lax.ppermute(act_in, "slab", within)
    act_across = lax.ppermute(act_across, "slab", across)
    decoded, part, lhs = call(
        forward_local_kernel,
        "forward_local",
        [(a, VMEM) for a in (feat_v, cache, kern_v, gain_v, shift_v, bias)],
        [(bf16((frames, rows, chans, cols)), HBM), (partial, VMEM), (weights, VMEM)],
        [
            vmem16((rows * block, (past + frames) * cols)),
            vmem16((3, chans, 2 * block)),
            vmem16((frames, max(rows - 2, 1), chans, cols)),
            pltpu.SemaphoreType.DMA((max(rows - 2, 1),)),
        ],
    )
    decoded = call(
        forward_edge_kernel,
        "forward_edge",
        [(act_in, HBM), (act_across, HBM)] + [(a, VMEM) for a in (part, lhs, gain_v, shift_v)] + [(decoded, HBM)],
        [(bf16((frames, rows, chans, cols)), HBM)],
        [
            vmem16((past + frames, chans, cols)),
            vmem16((past + frames, chans, cols)),
            vmem16((2, block, (past + frames) * cols)),
            vmem16((frames, edge_rows, chans, cols)),
            pltpu.SemaphoreType.DMA((2,)),
            pltpu.SemaphoreType.DMA((edge_rows,)),
        ],
        aliases={6: 0},
    )
    return (jnp.swapaxes(decoded, 2, 3), relaid)


def solution(mesh):
    rows = P(None, ("grp", "slab"), None, None)
    return jax.shard_map(
        body,
        mesh=mesh,
        in_specs=(rows, rows, rows, P(), P(), P(), P()),
        out_specs=(rows, P(None, "grp", "slab", None)),
        check_vma=False,
    )
```

time: 48.9 us -> 43.7 us (0.89)
  the two profiles are of different devices: /device:TPU:13 before, /device:TPU:15 now
where the time goes in v2:
time: 43.7 us; the launch traced here: 43.4 us
  Pallas kernels  17.9 us (41%)
  starting transfers between devices  13 us (30%)
  waiting for transfers between devices  11.1 us (25%)
  between operations  0.76 us (2%)
  local copies, waits for them, and re-layouts  0.72 us (2%)
    pallas_call x6, Pallas kernels, call(): pl.pallas_call(kernel, out_shape=[pltpu.HBM(o.shape, o.dtype) if where is...  17.9 us
    ppermute x1, waiting for transfers between devices, body(): act_across = lax.ppermute(act_across, 'slab', across)  11.1 us
    all_to_all x1, starting transfers between devices, body(): lax.all_to_all(grad, 'slab', split_axis=0, concat_axis=0, tiled=True)  5.71 us
    ppermute x1, starting transfers between devices, body(): act_across = lax.ppermute(act_across, 'slab', across)  3.11 us
    ppermute x1, starting transfers between devices, body(): cot_across = lax.ppermute(cot_across, 'slab', across)  3.05 us
  transfers between devices with their start and end apart: 5, of which 1 were waited for; matrix products, arithmetic and copies ran while one was open for 0% of the time, Pallas kernels for 29%

profile of v2, /device:TPU:15, one launch (start us, length us, event | category | flops | bytes accessed | tf_op | source)
XLA Modules:
  0.0 43.4 jit_solution(1480256563983206077)
XLA Ops:
  0.6 1.1 %staging.1 = (bf16[4,192,128]{2,1,0:T(8,128)(2,1)S(1)}, bf16[4,192,128]{2,1,0:T(8,128)(2,1)S(1)}) custom-call(bf16[4,3,192,128]{3,2,1,0:T(8,128)(2,1)} %bitcast.11), custom_call_target="tpu_custom_call" | custom-call | tf_op jit(solution)/shard_map/staging/pallas_call | solution.py:317
  1.7 0.7 %collective-permute-start = (bf16[4,192,128]{2,1,0:T(8,128)(2,1)S(1)}, bf16[4,192,128]{2,1,0:T(8,128)(2,1)S(1)}, u32[]{:S(2)}, u32[]{:S(2)}) collective-permute-start(bf16[4,192,128]{2,1,0:T(8,128)(2,1)S(1)} %get-tuple-element.30), channel_id=1, source_target_pairs={{0,1},{1,0},{2,3},{3,2},{4,5},{5,4},{6,7},{7,6},{8,9},{9,8},{10,11... | collective-permute-start | bytes 589832 | tf_op jit(solution)/shard_map/ppermute | solution.py:361
  2.4 3.0 %collective-permute-start.1 = (bf16[4,192,128]{2,1,0:T(8,128)(2,1)S(1)}, bf16[4,192,128]{2,1,0:T(8,128)(2,1)S(1)}, u32[]{:S(2)}, u32[]{:S(2)}) collective-permute-start(bf16[4,192,128]{2,1,0:T(8,128)(2,1)S(1)} %get-tuple-element.31), channel_id=1, source_target_pairs={{1,2},{3,4},{5,6},{7,8},{9,10},{11,12},{13,14},{2,1},{4,3},{6,5},{... | collective-permute-start | bytes 589832 | tf_op jit(solution)/shard_map/ppermute | solution.py:362
  5.5 5.3 %backward_local.1 = (bf16[16,3,48,128]{3,2,1,0:T(8,128)(2,1)}, bf16[6,192,128]{2,1,0:T(8,128)(2,1)}, bf16[6,192,128]{2,1,0:T(8,128)(2,1)}, f32[2,4,192,128]{3,2,...) custom-call(bf16[4,3,192,128]{3,2,1,0:T(8,128)(2,1)} %bitcast.12, ...), custom_call_target="tpu_custom_call" | custom-call | tf_op jit(solution)/shard_map/backward_local/pallas_call | solution.py:317
  10.8 0.0 collective-permute-done.inner
  10.8 0.0 collective-permute-done.1.outer
  10.8 0.0 copy-start
  10.8 0.0 copy-start.1
  10.9 2.4 %backward_edge.1 = bf16[16,3,48,128]{3,2,1,0:T(8,128)(2,1)} custom-call(bf16[4,3,192,128]{3,2,1,0:T(8,128)(2,1)S(1)} %get-tuple-element.29.cot, bf16[4,192,128]{2,1,0:T(8,128)(2,1)S(1)} %collective-permute-done.inner, bf16[4,192,128]{2,1,0:T(8,128)(2,1)S(1)} %collective-permute-done.1.outer, ...), custom_call_target="tpu_custom_call", output_to_operand_aliasing={{}: (8, {})} | custom-call | tf_op jit(solution)/shard_map/backward_edge/pallas_call | solution.py:317
  13.2 5.7 %all-to-all-start = ((bf16[16,3,48,128]{3,2,1,0:T(8,128)(2,1)}), bf16[16,3,48,128]{3,2,1,0:T(8,128)(2,1)}, u32[]{:S(2)}, u32[]{:S(2)}) async-start(bf16[16,3,48,128]{3,2,1,0:T(8,128)(2,1)} %backward_edge.1), calls=%async_computation | async-start | bytes 1179648 | tf_op jit(solution)/shard_map/all_to_all | solution.py:391
  18.9 0.4 collective-permute-start.2
  19.3 3.1 %collective-permute-start.3 = (bf16[6,192,128]{2,1,0:T(8,128)(2,1)}, bf16[6,192,128]{2,1,0:T(8,128)(2,1)S(1)}, u32[]{:S(2)}, u32[]{:S(2)}) collective-permute-start(bf16[6,192,128]{2,1,0:T(8,128)(2,1)} %get-tuple-element.36), channel_id=1, source_target_pairs={{1,2},{3,4},{5,6},{7,8},{9,10},{11,12},{13,14},{2,1},{4,3},{6,5},{... | collective-permute-start | bytes 884744 | tf_op jit(solution)/shard_map/ppermute | solution.py:409
  22.4 0.0 copy-done
  22.4 0.0 copy-done.1
  22.4 3.5 %forward_local.1 = (bf16[4,3,192,128]{3,2,1,0:T(8,128)(2,1)}, f32[2,4,192,128]{3,2,1,0:T(8,128)S(1)}, bf16[3,192,1728]{2,1,0:T(8,128)(2,1)S(1)}) custom-call(bf16[4,3,192,128]{3,2,1,0:T(8,128)(2,1)S(1)} %get-tuple-element.37.feat, bf16[2,3,192,128]{3,2,1,0:T(8,128)(2,1)S(1)} %bitcast.9, bf16[3,3,3,192,192]{4,3,2,1,0:T(8,128)(2,1)S(1)} %get-tuple-element.38.kern, ...), custom_call_target="tpu_custom_call" | custom-call | tf_op jit(solution)/shard_map/forward_local/pallas_call | solution.py:317
  26.0 0.0 collective-permute-done.2.inner_hbm
  26.0 0.0 copy-start.2
  26.0 11.1 %collective-permute-done.3.outer_hbm = bf16[6,192,128]{2,1,0:T(8,128)(2,1)S(1)} collective-permute-done((bf16[6,192,128]{2,1,0:T(8,128)(2,1)}, bf16[6,192,128]{2,1,0:T(8,128)(2,1)S(1)}, u32[]{:S(2)}, u32[]{:S(2)}) %collective-permute-start.3) | collective-permute-done | bytes 294944 | tf_op jit(solution)/shard_map/ppermute | solution.py:409
  37.1 0.0 copy-start.3
  37.1 0.0 copy-done.2
  37.1 0.7 %copy-done.3 = bf16[6,192,128]{2,1,0:T(8,128)(2,1)} copy-done((bf16[6,192,128]{2,1,0:T(8,128)(2,1)}, bf16[6,192,128]{2,1,0:T(8,128)(2,1)S(1)}, u32[]{:S(2)}) %copy-start.3) | copy-done | bytes 294936
  37.8 3.6 %forward_edge.1 = bf16[4,3,192,128]{3,2,1,0:T(8,128)(2,1)} custom-call(bf16[6,192,128]{2,1,0:T(8,128)(2,1)} %copy-done.2, bf16[6,192,128]{2,1,0:T(8,128)(2,1)} %copy-done.3, f32[2,4,192,128]{3,2,1,0:T(8,128)S(1)} %get-tuple-element.41.partial, bf16[3,192,1728]{2,1,0:T(8,128)(2,1)S(1)} %get-tuple-element.42.weights, ...), custom_call_target="tpu_custom_call", output_to_operand_aliasing={{}: (6, {})} | custom-call | tf_op jit(solution)/shard_map/forward_edge/pallas_call | solution.py:317
  41.4 0.0 all-to-all-done
  41.4 2.0 %unpack.1 = bf16[4,48,8,192]{3,2,1,0:T(8,128)(2,1)} custom-call(bf16[48,48,128]{2,1,0:T(8,128)(2,1)} %bitcast.7.src_hbm), custom_call_target="tpu_custom_call" | custom-call | tf_op jit(solution)/shard_map/unpack/pallas_call | solution.py:317
Async XLA Ops:
  1.7 9.1 %collective-permute-start = (bf16[4,192,128]{2,1,0:T(8,128)(2,1)S(1)}, bf16[4,192,128]{2,1,0:T(8,128)(2,1)S(1)}, u32[]{:S(2)}, u32[]{:S(2)}) collective-permute-start(bf16[4,192,128]{2,1,0:T(8,128)(2,1)S(1)} %get-tuple-element.30), channel_id=1, source_target_pairs={{0,1},{1,0},{2,3},{3,2},{4,5},{5,4},{6,7},{7,6},{8,9},{9,8},{10,11... | collective-permute-start | bytes 589832 | tf_op jit(solution)/shard_map/ppermute | solution.py:361
  2.4 8.4 %collective-permute-start.1 = (bf16[4,192,128]{2,1,0:T(8,128)(2,1)S(1)}, bf16[4,192,128]{2,1,0:T(8,128)(2,1)S(1)}, u32[]{:S(2)}, u32[]{:S(2)}) collective-permute-start(bf16[4,192,128]{2,1,0:T(8,128)(2,1)S(1)} %get-tuple-element.31), channel_id=1, source_target_pairs={{1,2},{3,4},{5,6},{7,8},{9,10},{11,12},{13,14},{2,1},{4,3},{6,5},{... | collective-permute-start | bytes 589832 | tf_op jit(solution)/shard_map/ppermute | solution.py:362
  10.8 11.6 %copy-start = (bf16[2,3,128,192]{2,3,1,0:T(8,128)(2,1)S(1)}, bf16[2,3,128,192]{2,3,1,0:T(8,128)(2,1)}, u32[]{:S(2)}) copy-start(bf16[2,3,128,192]{2,3,1,0:T(8,128)(2,1)} %param.8) | copy-start | bytes 884740
  10.8 11.6 %copy-start.1 = (f32[192]{0:T(256)S(1)}, f32[192]{0:T(256)}, u32[]{:S(2)}) copy-start(f32[192]{0:T(256)} %param.13) | copy-start | bytes 2308
  13.2 28.2 %all-to-all-start = ((bf16[16,3,48,128]{3,2,1,0:T(8,128)(2,1)}), bf16[16,3,48,128]{3,2,1,0:T(8,128)(2,1)}, u32[]{:S(2)}, u32[]{:S(2)}) async-start(bf16[16,3,48,128]{3,2,1,0:T(8,128)(2,1)} %backward_edge.1), calls=%async_computation | async-start | bytes 1179648 | tf_op jit(solution)/shard_map/all_to_all | solution.py:391
  18.9 7.1 %collective-permute-start.2 = (bf16[6,192,128]{2,1,0:T(8,128)(2,1)}, bf16[6,192,128]{2,1,0:T(8,128)(2,1)S(1)}, u32[]{:S(2)}, u32[]{:S(2)}) collective-permute-start(bf16[6,192,128]{2,1,0:T(8,128)(2,1)} %get-tuple-element.35), channel_id=1, source_target_pairs={{0,1},{1,0},{2,3},{3,2},{4,5},{5,4},{6,7},{7,6},{8,9},{9,8},{10,11... | collective-permute-start | bytes 884744 | tf_op jit(solution)/shard_map/ppermute | solution.py:408
  19.3 17.8 %collective-permute-start.3 = (bf16[6,192,128]{2,1,0:T(8,128)(2,1)}, bf16[6,192,128]{2,1,0:T(8,128)(2,1)S(1)}, u32[]{:S(2)}, u32[]{:S(2)}) collective-permute-start(bf16[6,192,128]{2,1,0:T(8,128)(2,1)} %get-tuple-element.36), channel_id=1, source_target_pairs={{1,2},{3,4},{5,6},{7,8},{9,10},{11,12},{13,14},{2,1},{4,3},{6,5},{... | collective-permute-start | bytes 884744 | tf_op jit(solution)/shard_map/ppermute | solution.py:409
  26.0 11.1 %copy-start.2 = (bf16[6,192,128]{2,1,0:T(8,128)(2,1)}, bf16[6,192,128]{2,1,0:T(8,128)(2,1)S(1)}, u32[]{:S(2)}) copy-start(bf16[6,192,128]{2,1,0:T(8,128)(2,1)S(1)} %collective-permute-done.2.inner_hbm) | copy-start | bytes 884740
  37.1 0.7 %copy-start.3 = (bf16[6,192,128]{2,1,0:T(8,128)(2,1)}, bf16[6,192,128]{2,1,0:T(8,128)(2,1)S(1)}, u32[]{:S(2)}) copy-start(bf16[6,192,128]{2,1,0:T(8,128)(2,1)S(1)} %collective-permute-done.3.outer_hbm) | copy-start | bytes 884740

commit v3 on v2

--- a/solution.py
+++ b/solution.py
@@ -8,6 +8,7 @@
 from jax.sharding import PartitionSpec as P
 
 EPS = 1e-06
+HINT = 10**10
 
 
 def column(vector, cols):
@@ -313,7 +314,7 @@
 HBM = functools.partial(pl.BlockSpec, memory_space=pltpu.HBM)
 
 
-def call(kernel, name, ins, outs, scratch=(), aliases=None):
+def call(kernel, name, ins, outs, scratch=(), aliases=None, flops=None):
     result = pl.pallas_call(
         kernel,
         out_shape=[pltpu.HBM(o.shape, o.dtype) if where is HBM else o for o, where in outs],
@@ -322,6 +323,7 @@
         scratch_shapes=list(scratch),
         input_output_aliases=aliases or {},
         compiler_params=pltpu.CompilerParams(vmem_limit_bytes=24 * 1024 * 1024),
+        cost_estimate=flops and pl.CostEstimate(flops=flops, transcendentals=0, bytes_accessed=0),
         name=name,
     )(*[pltpu.with_memory_space_constraint(a, pltpu.HBM) if where is HBM else a for a, where in ins])
     return result[0] if len(outs) == 1 else result
@@ -378,6 +380,8 @@
             pltpu.SemaphoreType.DMA((max(rows - 2, 1),)),
         ],
     )
+    act_in = lax.ppermute(act_in, "slab", within)
+    act_across = lax.ppermute(act_across, "slab", across)
     grad = call(
         functools.partial(backward_edge_kernel, packed=packed),
         "backward_edge",
@@ -402,11 +406,7 @@
     else:
         relaid = lax.all_to_all(grad, "slab", split_axis=2, concat_axis=1, tiled=True)
 
-    act_in, act_across, feat_v, kern_v, gain_v, shift_v, _ = lax.optimization_barrier(
-        (act_in, act_across, feat_v, kern_v, gain_v, shift_v, grad)
-    )
-    act_in = lax.ppermute(act_in, "slab", within)
-    act_across = lax.ppermute(act_across, "slab", across)
+    feat_v, kern_v, gain_v, shift_v, _ = lax.optimization_barrier((feat_v, kern_v, gain_v, shift_v, grad))
     decoded, part, lhs = call(
         forward_local_kernel,
         "forward_local",
@@ -418,6 +418,7 @@
             vmem16((frames, max(rows - 2, 1), chans, cols)),
             pltpu.SemaphoreType.DMA((max(rows - 2, 1),)),
         ],
+        flops=HINT,
     )
     decoded = call(
         forward_edge_kernel,
@@ -433,6 +434,7 @@
             pltpu.SemaphoreType.DMA((edge_rows,)),
         ],
         aliases={6: 0},
+        flops=HINT,
     )
     return (jnp.swapaxes(decoded, 2, 3), relaid)
 

time: 43.7 us -> 40.9 us (0.936)
  the two profiles are of different devices: /device:TPU:15 before, /device:TPU:0 now
where the time goes in v3:
time: 40.9 us; the launch traced here: 40.6 us
  Pallas kernels  17.9 us (44%)
  starting transfers between devices  13.5 us (33%)
  waiting for transfers between devices  8.47 us (21%)
  between operations  0.73 us (2%)
    pallas_call x6, Pallas kernels, call(): pl.pallas_call(kernel, out_shape=[pltpu.HBM(o.shape, o.dtype) if where is...  17.9 us
    all_to_all x1, waiting for transfers between devices, body(): lax.all_to_all(grad, 'slab', split_axis=0, concat_axis=0, tiled=True)  8.46 us
    all_to_all x1, starting transfers between devices, body(): lax.all_to_all(grad, 'slab', split_axis=0, concat_axis=0, tiled=True)  7.05 us
    ppermute x1, starting transfers between devices, body(): act_in = lax.ppermute(act_in, 'slab', within)  3.95 us
    ppermute x1, starting transfers between devices, body(): act_across = lax.ppermute(act_across, 'slab', across)  1.36 us
  transfers between devices with their start and end apart: 5, of which 1 were waited for; matrix products, arithmetic and copies ran while one was open for 0% of the time, Pallas kernels for 36%

profile of v3, /device:TPU:0, one launch (start us, length us, event | category | flops | bytes accessed | tf_op | source)
XLA Modules:
  0.0 40.6 jit_solution(15929634357550041253)
XLA Ops:
  0.6 1.1 %staging.1 = (bf16[4,192,128]{2,1,0:T(8,128)(2,1)S(1)}, bf16[4,192,128]{2,1,0:T(8,128)(2,1)S(1)}) custom-call(bf16[4,3,192,128]{3,2,1,0:T(8,128)(2,1)} %bitcast.11), custom_call_target="tpu_custom_call" | custom-call | tf_op jit(solution)/shard_map/staging/pallas_call | solution.py:318
  1.7 0.5 %collective-permute-start.2 = (bf16[4,192,128]{2,1,0:T(8,128)(2,1)S(1)}, bf16[4,192,128]{2,1,0:T(8,128)(2,1)S(1)}, u32[]{:S(2)}, u32[]{:S(2)}) collective-permute-start(bf16[4,192,128]{2,1,0:T(8,128)(2,1)S(1)} %get-tuple-element.28), channel_id=1, source_target_pairs={{0,1},{1,0},{2,3},{3,2},{4,5},{5,4},{6,7},{7,6},{8,9},{9,8},{10,11... | collective-permute-start | bytes 589832 | tf_op jit(solution)/shard_map/ppermute | solution.py:363
  2.2 0.7 %collective-permute-start.3 = (bf16[4,192,128]{2,1,0:T(8,128)(2,1)S(1)}, bf16[4,192,128]{2,1,0:T(8,128)(2,1)S(1)}, u32[]{:S(2)}, u32[]{:S(2)}) collective-permute-start(bf16[4,192,128]{2,1,0:T(8,128)(2,1)S(1)} %get-tuple-element.29), channel_id=1, source_target_pairs={{1,2},{3,4},{5,6},{7,8},{9,10},{11,12},{13,14},{2,1},{4,3},{6,5},{... | collective-permute-start | bytes 589832 | tf_op jit(solution)/shard_map/ppermute | solution.py:364
  2.9 5.3 %backward_local.1 = (bf16[16,3,48,128]{3,2,1,0:T(8,128)(2,1)}, bf16[6,192,128]{2,1,0:T(8,128)(2,1)}, bf16[6,192,128]{2,1,0:T(8,128)(2,1)}, f32[2,4,192,128]{3,2,...) custom-call(bf16[4,3,192,128]{3,2,1,0:T(8,128)(2,1)} %bitcast.12, ...), custom_call_target="tpu_custom_call" | custom-call | tf_op jit(solution)/shard_map/backward_local/pallas_call | solution.py:318
  8.2 4.0 %collective-permute-start = (bf16[6,192,128]{2,1,0:T(8,128)(2,1)}, bf16[6,192,128]{2,1,0:T(8,128)(2,1)}, u32[]{:S(2)}, u32[]{:S(2)}) collective-permute-start(bf16[6,192,128]{2,1,0:T(8,128)(2,1)} %get-tuple-element.21), channel_id=1, source_target_pairs={{0,1},{1,0},{2,3},{3,2},{4,5},{5,4},{6,7},{7,6},{8,9},{9,8},{10,11... | collective-permute-start | bytes 884744 | tf_op jit(solution)/shard_map/ppermute | solution.py:383
  12.2 1.4 %collective-permute-start.1 = (bf16[6,192,128]{2,1,0:T(8,128)(2,1)}, bf16[6,192,128]{2,1,0:T(8,128)(2,1)}, u32[]{:S(2)}, u32[]{:S(2)}) collective-permute-start(bf16[6,192,128]{2,1,0:T(8,128)(2,1)} %get-tuple-element.22), channel_id=1, source_target_pairs={{1,2},{3,4},{5,6},{7,8},{9,10},{11,12},{13,14},{2,1},{4,3},{6,5},{... | collective-permute-start | bytes 884744 | tf_op jit(solution)/shard_map/ppermute | solution.py:384
  13.5 0.0 collective-permute-done.2.inner
  13.5 0.0 collective-permute-done.3.outer
  13.5 0.0 copy-start
  13.5 0.0 copy-start.1
  13.5 2.4 %backward_edge.1 = bf16[16,3,48,128]{3,2,1,0:T(8,128)(2,1)} custom-call(bf16[4,3,192,128]{3,2,1,0:T(8,128)(2,1)S(1)} %get-tuple-element.27.cot, bf16[4,192,128]{2,1,0:T(8,128)(2,1)S(1)} %collective-permute-done.2.inner, bf16[4,192,128]{2,1,0:T(8,128)(2,1)S(1)} %collective-permute-done.3.outer, ...), custom_call_target="tpu_custom_call", output_to_operand_aliasing={{}: (8, {})} | custom-call | tf_op jit(solution)/shard_map/backward_edge/pallas_call | solution.py:318
  15.9 7.0 %all-to-all-start = ((bf16[16,3,48,128]{3,2,1,0:T(8,128)(2,1)}), bf16[16,3,48,128]{3,2,1,0:T(8,128)(2,1)}, u32[]{:S(2)}, u32[]{:S(2)}) async-start(bf16[16,3,48,128]{3,2,1,0:T(8,128)(2,1)} %backward_edge.1), calls=%async_computation | async-start | bytes 1179648 | tf_op jit(solution)/shard_map/all_to_all | solution.py:395
  23.0 0.0 copy-done
  23.0 0.0 copy-done.1
  23.0 3.5 %forward_local.1 = (bf16[4,3,192,128]{3,2,1,0:T(8,128)(2,1)}, f32[2,4,192,128]{3,2,1,0:T(8,128)S(1)}, bf16[3,192,1728]{2,1,0:T(8,128)(2,1)S(1)}) custom-call(bf16[4,3,192,128]{3,2,1,0:T(8,128)(2,1)S(1)} %get-tuple-element.33.feat, bf16[2,3,192,128]{3,2,1,0:T(8,128)(2,1)S(1)} %bitcast.9, bf16[3,3,3,192,192]{4,3,2,1,0:T(8,128)(2,1)S(1)} %get-tuple-element.34.kern, ...), custom_call_target="tpu_custom_call" | custom-call | flops 10000000000 | tf_op jit(solution)/shard_map/forward_local/pallas_call | solution.py:318
  26.5 0.0 collective-permute-done.inner_hbm
  26.5 0.0 collective-permute-done.1.outer_hbm
  26.6 3.6 %forward_edge.1 = bf16[4,3,192,128]{3,2,1,0:T(8,128)(2,1)} custom-call(bf16[6,192,128]{2,1,0:T(8,128)(2,1)} %collective-permute-done.inner_hbm, bf16[6,192,128]{2,1,0:T(8,128)(2,1)} %collective-permute-done.1.outer_hbm, f32[2,4,192,128]{3,2,1,0:T(8,128)S(1)} %get-tuple-element.37.partial, ...), custom_call_target="tpu_custom_call", output_to_operand_aliasing={{}: (6, {})} | custom-call | flops 10000000000 | tf_op jit(solution)/shard_map/forward_edge/pallas_call | solution.py:318
  30.1 8.5 %all-to-all-done = bf16[16,3,48,128]{3,2,1,0:T(8,128)(2,1)} async-done(((bf16[16,3,48,128]{3,2,1,0:T(8,128)(2,1)}), bf16[16,3,48,128]{3,2,1,0:T(8,128)(2,1)}, u32[]{:S(2)}, u32[]{:S(2)}) %all-to-all-start) | async-done | bytes 589856 | tf_op jit(solution)/shard_map/all_to_all | solution.py:395
  38.6 2.0 %unpack.1 = bf16[4,48,8,192]{3,2,1,0:T(8,128)(2,1)} custom-call(bf16[48,48,128]{2,1,0:T(8,128)(2,1)} %bitcast.7.src_hbm), custom_call_target="tpu_custom_call" | custom-call | tf_op jit(solution)/shard_map/unpack/pallas_call | solution.py:318
Async XLA Ops:
  1.7 11.8 %collective-permute-start.2 = (bf16[4,192,128]{2,1,0:T(8,128)(2,1)S(1)}, bf16[4,192,128]{2,1,0:T(8,128)(2,1)S(1)}, u32[]{:S(2)}, u32[]{:S(2)}) collective-permute-start(bf16[4,192,128]{2,1,0:T(8,128)(2,1)S(1)} %get-tuple-element.28), channel_id=1, source_target_pairs={{0,1},{1,0},{2,3},{3,2},{4,5},{5,4},{6,7},{7,6},{8,9},{9,8},{10,11... | collective-permute-start | bytes 589832 | tf_op jit(solution)/shard_map/ppermute | solution.py:363
  2.2 11.3 %collective-permute-start.3 = (bf16[4,192,128]{2,1,0:T(8,128)(2,1)S(1)}, bf16[4,192,128]{2,1,0:T(8,128)(2,1)S(1)}, u32[]{:S(2)}, u32[]{:S(2)}) collective-permute-start(bf16[4,192,128]{2,1,0:T(8,128)(2,1)S(1)} %get-tuple-element.29), channel_id=1, source_target_pairs={{1,2},{3,4},{5,6},{7,8},{9,10},{11,12},{13,14},{2,1},{4,3},{6,5},{... | collective-permute-start | bytes 589832 | tf_op jit(solution)/shard_map/ppermute | solution.py:364
  8.2 18.3 %collective-permute-start = (bf16[6,192,128]{2,1,0:T(8,128)(2,1)}, bf16[6,192,128]{2,1,0:T(8,128)(2,1)}, u32[]{:S(2)}, u32[]{:S(2)}) collective-permute-start(bf16[6,192,128]{2,1,0:T(8,128)(2,1)} %get-tuple-element.21), channel_id=1, source_target_pairs={{0,1},{1,0},{2,3},{3,2},{4,5},{5,4},{6,7},{7,6},{8,9},{9,8},{10,11... | collective-permute-start | bytes 884744 | tf_op jit(solution)/shard_map/ppermute | solution.py:383
  12.2 14.4 %collective-permute-start.1 = (bf16[6,192,128]{2,1,0:T(8,128)(2,1)}, bf16[6,192,128]{2,1,0:T(8,128)(2,1)}, u32[]{:S(2)}, u32[]{:S(2)}) collective-permute-start(bf16[6,192,128]{2,1,0:T(8,128)(2,1)} %get-tuple-element.22), channel_id=1, source_target_pairs={{1,2},{3,4},{5,6},{7,8},{9,10},{11,12},{13,14},{2,1},{4,3},{6,5},{... | collective-permute-start | bytes 884744 | tf_op jit(solution)/shard_map/ppermute | solution.py:384
  13.5 9.4 %copy-start = (bf16[2,3,128,192]{2,3,1,0:T(8,128)(2,1)S(1)}, bf16[2,3,128,192]{2,3,1,0:T(8,128)(2,1)}, u32[]{:S(2)}) copy-start(bf16[2,3,128,192]{2,3,1,0:T(8,128)(2,1)} %param.8) | copy-start | bytes 884740
  13.5 9.4 %copy-start.1 = (f32[192]{0:T(256)S(1)}, f32[192]{0:T(256)}, u32[]{:S(2)}) copy-start(f32[192]{0:T(256)} %param.13) | copy-start | bytes 2308
  15.9 22.7 %all-to-all-start = ((bf16[16,3,48,128]{3,2,1,0:T(8,128)(2,1)}), bf16[16,3,48,128]{3,2,1,0:T(8,128)(2,1)}, u32[]{:S(2)}, u32[]{:S(2)}) async-start(bf16[16,3,48,128]{3,2,1,0:T(8,128)(2,1)} %backward_edge.1), calls=%async_computation | async-start | bytes 1179648 | tf_op jit(solution)/shard_map/all_to_all | solution.py:395

commit v4 on v3

--- a/solution.py
+++ b/solution.py
@@ -110,36 +110,26 @@
 
 
 def backward_local_kernel(
-    cot_hbm, feat_hbm, cache_hbm, kern_hbm, gain_hbm, shift_hbm,
-    out, to_inner, to_outer, partial, weights, cot, feat, kern, gain_in, shift_in,
-    stack, tail, sent, past_rows, sems, edge_sems, out_sem, *, packed,
+    cot, feat, cache, kern, gain_in, shift_in,
+    out, to_inner, to_outer, partial, weights,
+    stack, tail, sent, edge_sems, out_sem, *, packed,
 ):
     frames, rows, chans, cols = cot.shape
-    past = cache_hbm.shape[0]
+    past = cache.shape[0]
     block = 3 * chans
     edges = list(zip(rows_sent(rows), (to_inner, to_outer)))
-    copies = fetch(
-        [(cot_hbm, cot), (kern_hbm.at[2], kern.at[2]), (kern_hbm.at[1], kern.at[1]), (kern_hbm.at[0], kern.at[0]),
-         (gain_hbm, gain_in), (shift_hbm, shift_in), (feat_hbm, feat)]
-        + [(cache_hbm.at[:, row], past_rows.at[n]) for n, (row, _) in enumerate(edges)],
-        sems,
-    )
-    copies[0].wait()
+    written = fetch(
+        [(feat.at[:, row], to.at[pl.ds(past, frames)]) for row, to in edges]
+        + [(cache.at[:, row], to.at[pl.ds(0, past)]) for row, to in edges],
+        edge_sems,
+    )
     for p in range(rows):
         for f in range(frames):
             shifted_to(stack, p * block, f * cols, cot[f, p], (1, 0, -1))
-    for n, t in ((1, 2), (2, 1), (3, 0)):
-        copies[n].wait()
+    for t in range(3):
         taps = [kern[t, 2 - d, j] for d in range(3) for j in range(3)]
         side_by_side(weights.at[t], taps)
         side_by_side(tail.at[t], taps[3:])
-    for c in copies[4:]:
-        c.wait()
-    written = fetch(
-        [(feat.at[:, row], to.at[pl.ds(past, frames)]) for row, to in edges]
-        + [(past_rows.at[n], to.at[pl.ds(0, past)]) for n, (_, to) in enumerate(edges)],
-        edge_sems,
-    )
     gain = column(gain_in[...], cols)
     shift = column(shift_in[...], cols)
     for r in list(range(1, rows - 1)) + sorted({0, rows - 1}):
@@ -359,23 +349,21 @@
         [(cot, HBM)],
         [(bf16((frames, chans, cols)), VMEM)] * 2,
         [pltpu.SemaphoreType.DMA((2,))],
+        flops=HINT,
     )
     cot_in = lax.ppermute(cot_in, "slab", within)
     cot_across = lax.ppermute(cot_across, "slab", across)
-    grad, act_in, act_across, part, lhs, cot_v, feat_v, kern_v, gain_v, shift_v = call(
+    grad, act_in, act_across, part, lhs = call(
         functools.partial(backward_local_kernel, packed=packed),
         "backward_local",
-        [(a, HBM) for a in (cot, feat, cache, kernel, gain, shift)],
+        [(a, VMEM) for a in (cot, feat, cache, kernel, gain, shift)],
         [(bf16(sent(rows)), HBM)]
         + [(bf16((past + frames, chans, cols)), HBM)] * 2
-        + [(partial, VMEM), (weights, VMEM)]
-        + [(jax.ShapeDtypeStruct(a.shape, a.dtype), VMEM) for a in (cot, feat, kernel, gain, shift)],
+        + [(partial, VMEM), (weights, VMEM)],
         [
             vmem16((rows * block, frames * cols)),
             vmem16((3, chans, 2 * block)),
             vmem16(sent(max(rows - 2, 1))),
-            vmem16((2, past, chans, cols)),
-            pltpu.SemaphoreType.DMA((9,)),
             pltpu.SemaphoreType.DMA((4,)),
             pltpu.SemaphoreType.DMA((max(rows - 2, 1),)),
         ],
@@ -385,7 +373,7 @@
     grad = call(
         functools.partial(backward_edge_kernel, packed=packed),
         "backward_edge",
-        [(a, VMEM) for a in (cot_v, cot_in, cot_across, feat_v, part, lhs, gain_v, shift_v)] + [(grad, HBM)],
+        [(a, VMEM) for a in (cot, cot_in, cot_across, feat, part, lhs, gain, shift)] + [(grad, HBM)],
         [(bf16(sent(rows)), HBM)],
         [vmem16((2, block, frames * cols)), vmem16(sent(edge_rows)), pltpu.SemaphoreType.DMA((edge_rows,))],
         aliases={8: 0},
@@ -406,7 +394,7 @@
     else:
         relaid = lax.all_to_all(grad, "slab", split_axis=2, concat_axis=1, tiled=True)
 
-    feat_v, kern_v, gain_v, shift_v, _ = lax.optimization_barrier((feat_v, kern_v, gain_v, shift_v, grad))
+    feat_v, kern_v, gain_v, shift_v, _ = lax.optimization_barrier((feat, kernel, gain, shift, grad))
     decoded, part, lhs = call(
         forward_local_kernel,
         "forward_local",

time: 40.9 us -> 39.6 us (0.968)
  Pallas kernels: 17.9 us -> 16.5 us
    pallas_call x6, Pallas kernels: 17.9 us -> 16.5 us  [call(): pl.pallas_call(kernel, out_shape=[pltpu.HBM(o.shape, o.dtype) if where is...]
  transfers between devices with their start and end apart: 5 -> 5, of which waited for: 1 -> 1; matrix products, arithmetic and copies ran while one was open for 0% -> 0% of each run, Pallas kernels for 36% -> 34%
where the time goes in v4:
time: 39.6 us; the launch traced here: 39.3 us
  Pallas kernels  16.5 us (42%)
  starting transfers between devices  13.5 us (34%)
  waiting for transfers between devices  8.39 us (21%)
  between operations  0.81 us (2%)
    pallas_call x6, Pallas kernels, call(): pl.pallas_call(kernel, out_shape=[pltpu.HBM(o.shape, o.dtype) if where is...  16.5 us
    all_to_all x1, waiting for transfers between devices, body(): lax.all_to_all(grad, 'slab', split_axis=0, concat_axis=0, tiled=True)  8.38 us
    all_to_all x1, starting transfers between devices, body(): lax.all_to_all(grad, 'slab', split_axis=0, concat_axis=0, tiled=True)  6.91 us
    ppermute x1, starting transfers between devices, body(): act_in = lax.ppermute(act_in, 'slab', within)  4.09 us
    ppermute x1, starting transfers between devices, body(): act_across = lax.ppermute(act_across, 'slab', across)  1.37 us
  transfers between devices with their start and end apart: 5, of which 1 were waited for; matrix products, arithmetic and copies ran while one was open for 0% of the time, Pallas kernels for 34%

profile of v4, /device:TPU:0, one launch (start us, length us, event | category | flops | bytes accessed | tf_op | source)
XLA Modules:
  0.0 39.3 jit_solution(9897667743471022729)
XLA Ops:
  0.6 0.0 copy-start
  0.6 0.0 copy-start.1
  0.7 0.0 copy-start.2
  0.7 0.0 copy-start.3
  0.7 0.0 copy-start.4
  0.7 0.0 copy-start.5
  0.7 1.2 %staging.1 = (bf16[4,192,128]{2,1,0:T(8,128)(2,1)S(1)}, bf16[4,192,128]{2,1,0:T(8,128)(2,1)S(1)}) custom-call(bf16[4,3,192,128]{3,2,1,0:T(8,128)(2,1)} %bitcast.8), custom_call_target="tpu_custom_call" | custom-call | flops 10000000000 | tf_op jit(solution)/shard_map/staging/pallas_call | solution.py:308
  1.9 0.5 %collective-permute-start.2 = (bf16[4,192,128]{2,1,0:T(8,128)(2,1)S(1)}, bf16[4,192,128]{2,1,0:T(8,128)(2,1)S(1)}, u32[]{:S(2)}, u32[]{:S(2)}) collective-permute-start(bf16[4,192,128]{2,1,0:T(8,128)(2,1)S(1)} %get-tuple-element.18), channel_id=1, source_target_pairs={{0,1},{1,0},{2,3},{3,2},{4,5},{5,4},{6,7},{7,6},{8,9},{9,8},{10,11... | collective-permute-start | bytes 589832 | tf_op jit(solution)/shard_map/ppermute | solution.py:354
  2.4 0.7 %collective-permute-start.3 = (bf16[4,192,128]{2,1,0:T(8,128)(2,1)S(1)}, bf16[4,192,128]{2,1,0:T(8,128)(2,1)S(1)}, u32[]{:S(2)}, u32[]{:S(2)}) collective-permute-start(bf16[4,192,128]{2,1,0:T(8,128)(2,1)S(1)} %get-tuple-element.19), channel_id=1, source_target_pairs={{1,2},{3,4},{5,6},{7,8},{9,10},{11,12},{13,14},{2,1},{4,3},{6,5},{... | collective-permute-start | bytes 589832 | tf_op jit(solution)/shard_map/ppermute | solution.py:355
  3.1 0.0 copy-done
  3.1 0.0 copy-done.1
  3.1 0.0 copy-done.2
  3.1 0.0 copy-done.3
  3.1 0.0 copy-done.4
  3.1 0.0 copy-done.5
  3.1 3.7 %backward_local.1 = (bf16[16,3,48,128]{3,2,1,0:T(8,128)(2,1)}, bf16[6,192,128]{2,1,0:T(8,128)(2,1)}, bf16[6,192,128]{2,1,0:T(8,128)(2,1)}, f32[2,4,192,128]{3,2,1,0:T(8,128)S(1)}, bf16[3,192,1728]{2,1,0:T(8,128)(2,1)S(1)}) custom-call(bf16[4,3,192,128]{3,2,1,0:T(8,128)(2,1)S(1)} %bitcast.9, bf16[4,3,192,128]{3,2,1,0:T(8,128)(2,1)S(1)} %bitcast.11, ...), custom_call_target="tpu_custom_call" | custom-call | tf_op jit(solution)/shard_map/backward_local/pallas_call | solution.py:308
  6.8 4.1 %collective-permute-start = (bf16[6,192,128]{2,1,0:T(8,128)(2,1)}, bf16[6,192,128]{2,1,0:T(8,128)(2,1)}, u32[]{:S(2)}, u32[]{:S(2)}) collective-permute-start(bf16[6,192,128]{2,1,0:T(8,128)(2,1)} %get-tuple-element.16), channel_id=1, source_target_pairs={{0,1},{1,0},{2,3},{3,2},{4,5},{5,4},{6,7},{7,6},{8,9},{9,8},{10,11... | collective-permute-start | bytes 884744 | tf_op jit(solution)/shard_map/ppermute | solution.py:371
  10.9 1.4 %collective-permute-start.1 = (bf16[6,192,128]{2,1,0:T(8,128)(2,1)}, bf16[6,192,128]{2,1,0:T(8,128)(2,1)}, u32[]{:S(2)}, u32[]{:S(2)}) collective-permute-start(bf16[6,192,128]{2,1,0:T(8,128)(2,1)} %get-tuple-element.17), channel_id=1, source_target_pairs={{1,2},{3,4},{5,6},{7,8},{9,10},{11,12},{13,14},{2,1},{4,3},{6,5},{... | collective-permute-start | bytes 884744 | tf_op jit(solution)/shard_map/ppermute | solution.py:372
  12.3 0.0 collective-permute-done.2.inner
  12.3 0.0 collective-permute-done.3.outer
  12.3 0.0 copy-start.6
  12.3 2.4 %backward_edge.1 = bf16[16,3,48,128]{3,2,1,0:T(8,128)(2,1)} custom-call(bf16[4,3,192,128]{3,2,1,0:T(8,128)(2,1)S(1)} %bitcast.10, bf16[4,192,128]{2,1,0:T(8,128)(2,1)S(1)} %collective-permute-done.2.inner, bf16[4,192,128]{2,1,0:T(8,128)(2,1)S(1)} %collective-permute-done.3.outer, ...), custom_call_target="tpu_custom_call", output_to_operand_aliasing={{}: (8, {})} | custom-call | tf_op jit(solution)/shard_map/backward_edge/pallas_call | solution.py:308
  14.7 6.9 %all-to-all-start = ((bf16[16,3,48,128]{3,2,1,0:T(8,128)(2,1)}), bf16[16,3,48,128]{3,2,1,0:T(8,128)(2,1)}, u32[]{:S(2)}, u32[]{:S(2)}) async-start(bf16[16,3,48,128]{3,2,1,0:T(8,128)(2,1)} %backward_edge.1), calls=%async_computation | async-start | bytes 1179648 | tf_op jit(solution)/shard_map/all_to_all | solution.py:383
  21.6 0.0 copy-done.6
  21.7 3.6 %forward_local.1 = (bf16[4,3,192,128]{3,2,1,0:T(8,128)(2,1)}, f32[2,4,192,128]{3,2,1,0:T(8,128)S(1)}, bf16[3,192,1728]{2,1,0:T(8,128)(2,1)S(1)}) custom-call(bf16[4,3,192,128]{3,2,1,0:T(8,128)(2,1)S(1)} %bitcast.13, bf16[2,3,192,128]{3,2,1,0:T(8,128)(2,1)S(1)} %bitcast.15, bf16[3,3,3,192,192]{4,3,2,1,0:T(8,128)(2,1)S(1)} %copy-done, f32[1,192]{1,0:T(1,128)S(1)} %bitcast.18, ...), custom_call_target="tpu_custom_call" | custom-call | flops 10000000000 | tf_op jit(solution)/shard_map/forward_local/pallas_call | solution.py:308
  25.3 0.0 collective-permute-done.inner_hbm
  25.3 0.0 collective-permute-done.1.outer_hbm
  25.3 3.6 %forward_edge.1 = bf16[4,3,192,128]{3,2,1,0:T(8,128)(2,1)} custom-call(bf16[6,192,128]{2,1,0:T(8,128)(2,1)} %collective-permute-done.inner_hbm, bf16[6,192,128]{2,1,0:T(8,128)(2,1)} %collective-permute-done.1.outer_hbm, f32[2,4,192,128]{3,2,1,0:T(8,128)S(1)} %get-tuple-element.27.partial, ...), custom_call_target="tpu_custom_call", output_to_operand_aliasing={{}: (6, {})} | custom-call | flops 10000000000 | tf_op jit(solution)/shard_map/forward_edge/pallas_call | solution.py:308
  28.9 8.4 %all-to-all-done = bf16[16,3,48,128]{3,2,1,0:T(8,128)(2,1)} async-done(((bf16[16,3,48,128]{3,2,1,0:T(8,128)(2,1)}), bf16[16,3,48,128]{3,2,1,0:T(8,128)(2,1)}, u32[]{:S(2)}, u32[]{:S(2)}) %all-to-all-start) | async-done | bytes 589856 | tf_op jit(solution)/shard_map/all_to_all | solution.py:383
  37.3 2.0 %unpack.1 = bf16[4,48,8,192]{3,2,1,0:T(8,128)(2,1)} custom-call(bf16[48,48,128]{2,1,0:T(8,128)(2,1)} %bitcast.7.src_hbm), custom_call_target="tpu_custom_call" | custom-call | tf_op jit(solution)/shard_map/unpack/pallas_call | solution.py:308
Async XLA Ops:
  0.6 2.5 %copy-start = (bf16[3,3,3,192,192]{4,3,2,1,0:T(8,128)(2,1)S(1)}, bf16[3,3,3,192,192]{4,3,2,1,0:T(8,128)(2,1)}, u32[]{:S(2)}) copy-start(bf16[3,3,3,192,192]{4,3,2,1,0:T(8,128)(2,1)} %kern.2) | copy-start | bytes 5971972
  0.6 2.5 %copy-start.1 = (bf16[4,3,128,192]{2,3,1,0:T(8,128)(2,1)S(1)}, bf16[4,3,128,192]{2,3,1,0:T(8,128)(2,1)}, u32[]{:S(2)}) copy-start(bf16[4,3,128,192]{2,3,1,0:T(8,128)(2,1)} %param.9) | copy-start | bytes 1769476
  0.7 2.5 %copy-start.2 = (bf16[4,3,128,192]{2,3,1,0:T(8,128)(2,1)S(1)}, bf16[4,3,128,192]{2,3,1,0:T(8,128)(2,1)}, u32[]{:S(2)}) copy-start(bf16[4,3,128,192]{2,3,1,0:T(8,128)(2,1)} %param.7) | copy-start | bytes 1769476
  0.7 2.5 %copy-start.3 = (bf16[2,3,128,192]{2,3,1,0:T(8,128)(2,1)S(1)}, bf16[2,3,128,192]{2,3,1,0:T(8,128)(2,1)}, u32[]{:S(2)}) copy-start(bf16[2,3,128,192]{2,3,1,0:T(8,128)(2,1)} %param.8) | copy-start | bytes 884740
  0.7 2.5 %copy-start.4 = (f32[192]{0:T(256)S(1)}, f32[192]{0:T(256)}, u32[]{:S(2)}) copy-start(f32[192]{0:T(256)} %param.11) | copy-start | bytes 2308
  0.7 2.5 %copy-start.5 = (f32[192]{0:T(256)S(1)}, f32[192]{0:T(256)}, u32[]{:S(2)}) copy-start(f32[192]{0:T(256)} %param.12) | copy-start | bytes 2308
  1.9 10.4 %collective-permute-start.2 = (bf16[4,192,128]{2,1,0:T(8,128)(2,1)S(1)}, bf16[4,192,128]{2,1,0:T(8,128)(2,1)S(1)}, u32[]{:S(2)}, u32[]{:S(2)}) collective-permute-start(bf16[4,192,128]{2,1,0:T(8,128)(2,1)S(1)} %get-tuple-element.18), channel_id=1, source_target_pairs={{0,1},{1,0},{2,3},{3,2},{4,5},{5,4},{6,7},{7,6},{8,9},{9,8},{10,11... | collective-permute-start | bytes 589832 | tf_op jit(solution)/shard_map/ppermute | solution.py:354
  2.4 9.9 %collective-permute-start.3 = (bf16[4,192,128]{2,1,0:T(8,128)(2,1)S(1)}, bf16[4,192,128]{2,1,0:T(8,128)(2,1)S(1)}, u32[]{:S(2)}, u32[]{:S(2)}) collective-permute-start(bf16[4,192,128]{2,1,0:T(8,128)(2,1)S(1)} %get-tuple-element.19), channel_id=1, source_target_pairs={{1,2},{3,4},{5,6},{7,8},{9,10},{11,12},{13,14},{2,1},{4,3},{6,5},{... | collective-permute-start | bytes 589832 | tf_op jit(solution)/shard_map/ppermute | solution.py:355
  6.8 18.5 %collective-permute-start = (bf16[6,192,128]{2,1,0:T(8,128)(2,1)}, bf16[6,192,128]{2,1,0:T(8,128)(2,1)}, u32[]{:S(2)}, u32[]{:S(2)}) collective-permute-start(bf16[6,192,128]{2,1,0:T(8,128)(2,1)} %get-tuple-element.16), channel_id=1, source_target_pairs={{0,1},{1,0},{2,3},{3,2},{4,5},{5,4},{6,7},{7,6},{8,9},{9,8},{10,11... | collective-permute-start | bytes 884744 | tf_op jit(solution)/shard_map/ppermute | solution.py:371
  10.9 14.4 %collective-permute-start.1 = (bf16[6,192,128]{2,1,0:T(8,128)(2,1)}, bf16[6,192,128]{2,1,0:T(8,128)(2,1)}, u32[]{:S(2)}, u32[]{:S(2)}) collective-permute-start(bf16[6,192,128]{2,1,0:T(8,128)(2,1)} %get-tuple-element.17), channel_id=1, source_target_pairs={{1,2},{3,4},{5,6},{7,8},{9,10},{11,12},{13,14},{2,1},{4,3},{6,5},{... | collective-permute-start | bytes 884744 | tf_op jit(solution)/shard_map/ppermute | solution.py:372
  12.3 9.4 %copy-start.6 = (f32[192]{0:T(256)S(1)}, f32[192]{0:T(256)}, u32[]{:S(2)}) copy-start(f32[192]{0:T(256)} %param.13) | copy-start | bytes 2308
  14.7 22.5 %all-to-all-start = ((bf16[16,3,48,128]{3,2,1,0:T(8,128)(2,1)}), bf16[16,3,48,128]{3,2,1,0:T(8,128)(2,1)}, u32[]{:S(2)}, u32[]{:S(2)}) async-start(bf16[16,3,48,128]{3,2,1,0:T(8,128)(2,1)} %backward_edge.1), calls=%async_computation | async-start | bytes 1179648 | tf_op jit(solution)/shard_map/all_to_all | solution.py:383

commit v5 on v4

--- a/solution.py
+++ b/solution.py
@@ -53,18 +53,19 @@
     return jnp.dot(a, b, preferred_element_type=jnp.float32)
 
 
-def grad_sum(lhs_of, stack, lo, hi, frames, cols):
+def grad_sum(lhs, k0, k1, stack, lo, hi, frames, cols):
+    chans = lhs.shape[0] // 3
     acc = [None] * frames
-    for f0 in range(0, frames, 2):
-        for t in range(2, -1, -1):
-            g0 = f0 + 2 - t
-            count = min(2, frames - g0)
-            if count <= 0:
-                continue
-            part = dot(lhs_of(t), stack[lo:hi, g0 * cols : (g0 + count) * cols])
+    for g0 in range(0, frames, 2):
+        count = min(2, frames - g0)
+        reach = min(3, g0 + count)
+        part = dot(lhs[: reach * chans, k0:k1], stack[lo:hi, g0 * cols : (g0 + count) * cols])
+        for back in range(reach):
             for n in range(count):
-                piece = part[:, n * cols : (n + 1) * cols]
-                acc[f0 + n] = piece if acc[f0 + n] is None else acc[f0 + n] + piece
+                f = g0 + n - back
+                if f >= 0:
+                    piece = part[back * chans : (back + 1) * chans, n * cols : (n + 1) * cols]
+                    acc[f] = piece if acc[f] is None else acc[f] + piece
     return acc
 
 
@@ -111,16 +112,15 @@
 
 def backward_local_kernel(
     cot, feat, cache, kern, gain_in, shift_in,
-    out, to_inner, to_outer, partial, weights,
-    stack, tail, sent, edge_sems, out_sem, *, packed,
+    middle, to_outer, partial, weights,
+    stack, tail, edge_sems, *, packed,
 ):
     frames, rows, chans, cols = cot.shape
     past = cache.shape[0]
     block = 3 * chans
-    edges = list(zip(rows_sent(rows), (to_inner, to_outer)))
+    _, outer = rows_sent(rows)
     written = fetch(
-        [(feat.at[:, row], to.at[pl.ds(past, frames)]) for row, to in edges]
-        + [(cache.at[:, row], to.at[pl.ds(0, past)]) for row, to in edges],
+        [(feat.at[:, outer], to_outer.at[pl.ds(past, frames)]), (cache.at[:, outer], to_outer.at[pl.ds(0, past)])],
         edge_sems,
     )
     for p in range(rows):
@@ -128,24 +128,18 @@
             shifted_to(stack, p * block, f * cols, cot[f, p], (1, 0, -1))
     for t in range(3):
         taps = [kern[t, 2 - d, j] for d in range(3) for j in range(3)]
-        side_by_side(weights.at[t], taps)
-        side_by_side(tail.at[t], taps[3:])
+        rows_of_t = pl.ds((2 - t) * chans, chans)
+        side_by_side(weights.at[rows_of_t], taps)
+        side_by_side(tail.at[rows_of_t], taps[3:])
     gain = column(gain_in[...], cols)
     shift = column(shift_in[...], cols)
-    for r in list(range(1, rows - 1)) + sorted({0, rows - 1}):
+    for r in range(rows):
         d0, n, first = local_taps(r, rows)
-
-        def lhs_of(t):
-            if d0 == 1:
-                return tail[t, :, : n * block]
-            return weights[t, :, : n * block]
-
-        acc = grad_sum(lhs_of, stack, first * block, (first + n) * block, frames, cols)
+        lhs = tail if d0 == 1 else weights
+        acc = grad_sum(lhs, 0, n * block, stack, first * block, (first + n) * block, frames, cols)
         if n == 3:
             grads = [finish(acc[f], feat[f, r], cot[f, r], gain, shift) for f in range(frames)]
-            put_row(sent, r - 1, grads, packed)
-            written.append(pltpu.make_async_copy(sent.at[:, r - 1], out.at[:, r], out_sem.at[r - 1]))
-            written[-1].start()
+            put_row(middle, r - 1, grads, packed)
         else:
             for f in range(frames):
                 partial[min(r, 1), f] = acc[f]
@@ -154,25 +148,25 @@
 
 
 def backward_edge_kernel(
-    cot, inner, outer, feat, partial, weights, gain_in, shift_in, before, out, stack, sent, out_sem, *, packed
+    cot, inner, outer, feat, partial, weights, gain_in, shift_in, middle, out, stack, sent, out_sem, *, packed
 ):
-    del before
     frames, rows, chans, cols = cot.shape
     block = 3 * chans
+    written = []
+    if rows > 2:
+        written.append(pltpu.make_async_copy(middle, out.at[:, 1 : rows - 1], out_sem.at[2]))
+        written[0].start()
     slot = jnp.where(lax.rem(lax.axis_index("slab"), 2) == 0, 1, 0)
     for f in range(frames):
         shifted_to(stack.at[slot], 0, f * cols, inner[f], (1, 0, -1))
         shifted_to(stack.at[1 - slot], 0, f * cols, outer[f], (1, 0, -1))
     gain = column(gain_in[...], cols)
     shift = column(shift_in[...], cols)
-    written = []
     for edge, r in enumerate(sorted({0, rows - 1})):
         acc = [partial[edge, f] for f in range(frames)]
         for d, there in ((0, r == 0), (2, r == rows - 1)):
             if there:
-                more = grad_sum(
-                    lambda t: weights[t, :, d * block : (d + 1) * block], stack.at[d // 2], 0, block, frames, cols
-                )
+                more = grad_sum(weights, d * block, (d + 1) * block, stack.at[d // 2], 0, block, frames, cols)
                 acc = [a + b for a, b in zip(acc, more)]
         grads = [finish(acc[f], feat[f, r], cot[f, r], gain, shift) for f in range(frames)]
         put_row(sent, edge, grads, packed)
@@ -200,7 +194,8 @@
 
 
 def forward_local_kernel(
-    feat, cache, kern, gain_in, shift_in, bias_in, out, partial, weights, stack, tail, ready, out_sem
+    feat, cache, kern, gain_in, shift_in, bias_in,
+    out, to_inner, partial, weights, stack, tail, ready, out_sem, edge_sems,
 ):
     frames, rows, chans, cols = feat.shape
     past = cache.shape[0]
@@ -208,6 +203,11 @@
     gain = column(gain_in[...], cols)
     shift = column(shift_in[...], cols)
     bias = column(bias_in[...], cols)
+    inner, _ = rows_sent(rows)
+    written = fetch(
+        [(feat.at[:, inner], to_inner.at[pl.ds(past, frames)]), (cache.at[:, inner], to_inner.at[pl.ds(0, past)])],
+        edge_sems,
+    )
     for t in range(3):
         whole = jnp.transpose(kern[t].reshape(3 * block, chans))
         weights[t] = whole
@@ -218,7 +218,6 @@
         for f in range(frames):
             act = activated(feat[f, p], gain, shift).astype(jnp.bfloat16)
             shifted_to(stack, p * block, (past + f) * cols, act, (-1, 0, 1))
-    written = []
     for r in list(range(1, rows - 1)) + sorted({0, rows - 1}):
         d0, n, first = local_taps(r, rows)
 
@@ -353,30 +352,26 @@
     )
     cot_in = lax.ppermute(cot_in, "slab", within)
     cot_across = lax.ppermute(cot_across, "slab", across)
-    grad, act_in, act_across, part, lhs = call(
+    middle, act_across, part, lhs = call(
         functools.partial(backward_local_kernel, packed=packed),
         "backward_local",
         [(a, VMEM) for a in (cot, feat, cache, kernel, gain, shift)],
-        [(bf16(sent(rows)), HBM)]
-        + [(bf16((past + frames, chans, cols)), HBM)] * 2
-        + [(partial, VMEM), (weights, VMEM)],
+        [(bf16(sent(max(rows - 2, 1))), VMEM)]
+        + [(bf16((past + frames, chans, cols)), HBM)]
+        + [(partial, VMEM), (bf16((3 * chans, 3 * block)), VMEM)],
         [
             vmem16((rows * block, frames * cols)),
-            vmem16((3, chans, 2 * block)),
-            vmem16(sent(max(rows - 2, 1))),
-            pltpu.SemaphoreType.DMA((4,)),
-            pltpu.SemaphoreType.DMA((max(rows - 2, 1),)),
+            vmem16((3 * chans, 2 * block)),
+            pltpu.SemaphoreType.DMA((2,)),
         ],
     )
-    act_in = lax.ppermute(act_in, "slab", within)
     act_across = lax.ppermute(act_across, "slab", across)
     grad = call(
         functools.partial(backward_edge_kernel, packed=packed),
         "backward_edge",
-        [(a, VMEM) for a in (cot, cot_in, cot_across, feat, part, lhs, gain, shift)] + [(grad, HBM)],
+        [(a, VMEM) for a in (cot, cot_in, cot_across, feat, part, lhs, gain, shift, middle)],
         [(bf16(sent(rows)), HBM)],
-        [vmem16((2, block, frames * cols)), vmem16(sent(edge_rows)), pltpu.SemaphoreType.DMA((edge_rows,))],
-        aliases={8: 0},
+        [vmem16((2, block, frames * cols)), vmem16(sent(edge_rows)), pltpu.SemaphoreType.DMA((3,))],
     )
 
     if packed:
@@ -395,19 +390,21 @@
         relaid = lax.all_to_all(grad, "slab", split_axis=2, concat_axis=1, tiled=True)
 
     feat_v, kern_v, gain_v, shift_v, _ = lax.optimization_barrier((feat, kernel, gain, shift, grad))
-    decoded, part, lhs = call(
+    decoded, act_in, part, lhs = call(
         forward_local_kernel,
         "forward_local",
         [(a, VMEM) for a in (feat_v, cache, kern_v, gain_v, shift_v, bias)],
-        [(bf16((frames, rows, chans, cols)), HBM), (partial, VMEM), (weights, VMEM)],
+        [(bf16((frames, rows, chans, cols)), HBM), (bf16((past + frames, chans, cols)), HBM), (partial, VMEM), (weights, VMEM)],
         [
             vmem16((rows * block, (past + frames) * cols)),
             vmem16((3, chans, 2 * block)),
             vmem16((frames, max(rows - 2, 1), chans, cols)),
             pltpu.SemaphoreType.DMA((max(rows - 2, 1),)),
+            pltpu.SemaphoreType.DMA((2,)),
         ],
         flops=HINT,
     )
+    act_in = lax.ppermute(act_in, "slab", within)
     decoded = call(
         forward_edge_kernel,
         "forward_edge",
@@ -422,7 +419,6 @@
             pltpu.SemaphoreType.DMA((edge_rows,)),
         ],
         aliases={6: 0},
-        flops=HINT,
     )
     return (jnp.swapaxes(decoded, 2, 3), relaid)
 

time: 39.6 us -> 39 us (0.985)
  waiting for transfers between devices: 8.39 us -> 6.83 us
  local copies, waits for them, and re-layouts: 0.03 us -> 0.75 us
    all_to_all x1, starting transfers between devices: 6.91 us -> 10.7 us  [body(): lax.all_to_all(grad, 'slab', split_axis=0, concat_axis=0, tiled=True)]
    ppermute x1, starting transfers between devices: 4.09 us -> 0.43 us  [body(): act_in = lax.ppermute(act_in, 'slab', within)]
    all_to_all x1, waiting for transfers between devices: 8.38 us -> 5.4 us  [body(): lax.all_to_all(grad, 'slab', split_axis=0, concat_axis=0, tiled=True)]
    ppermute x1, waiting for transfers between devices: 0.01 us -> 1.42 us  [body(): act_in = lax.ppermute(act_in, 'slab', within)]
    unnamed x14 -> x16, local copies, waits for them, and re-layouts: 0.03 us -> 0.75 us
  transfers between devices with their start and end apart: 5 -> 5, of which waited for: 1 -> 2; matrix products, arithmetic and copies ran while one was open for 0% -> 0% of each run, Pallas kernels for 34% -> 35%
where the time goes in v5:
time: 39 us; the launch traced here: 38.7 us
  Pallas kernels  16.6 us (43%)
  starting transfers between devices  13.7 us (35%)
  waiting for transfers between devices  6.83 us (18%)
  between operations  0.8 us (2%)
  local copies, waits for them, and re-layouts  0.75 us (2%)
    pallas_call x6, Pallas kernels, call(): pl.pallas_call(kernel, out_shape=[pltpu.HBM(o.shape, o.dtype) if where is...  16.6 us
    all_to_all x1, starting transfers between devices, body(): lax.all_to_all(grad, 'slab', split_axis=0, concat_axis=0, tiled=True)  10.7 us
    all_to_all x1, waiting for transfers between devices, body(): lax.all_to_all(grad, 'slab', split_axis=0, concat_axis=0, tiled=True)  5.4 us
    ppermute x1, waiting for transfers between devices, body(): act_in = lax.ppermute(act_in, 'slab', within)  1.42 us
    ppermute x1, starting transfers between devices, body(): act_across = lax.ppermute(act_across, 'slab', across)  1.38 us
  transfers between devices with their start and end apart: 5, of which 2 were waited for; matrix products, arithmetic and copies ran while one was open for 0% of the time, Pallas kernels for 35%

profile of v5, /device:TPU:0, one launch (start us, length us, event | category | flops | bytes accessed | tf_op | source)
XLA Modules:
  0.0 38.7 jit_solution(9235578278274040154)
XLA Ops:
  0.6 0.0 copy-start
  0.6 0.0 copy-start.1
  0.7 0.0 copy-start.2
  0.7 0.0 copy-start.3
  0.7 0.0 copy-start.4
  0.7 0.0 copy-start.5
  0.7 1.2 %staging.1 = (bf16[4,192,128]{2,1,0:T(8,128)(2,1)S(1)}, bf16[4,192,128]{2,1,0:T(8,128)(2,1)S(1)}) custom-call(bf16[4,3,192,128]{3,2,1,0:T(8,128)(2,1)} %bitcast.8), custom_call_target="tpu_custom_call" | custom-call | flops 10000000000 | tf_op jit(solution)/shard_map/staging/pallas_call | solution.py:307
  1.9 0.5 %collective-permute-start = (bf16[4,192,128]{2,1,0:T(8,128)(2,1)S(1)}, bf16[4,192,128]{2,1,0:T(8,128)(2,1)S(1)}, u32[]{:S(2)}, u32[]{:S(2)}) collective-permute-start(bf16[4,192,128]{2,1,0:T(8,128)(2,1)S(1)} %get-tuple-element.16), channel_id=1, source_target_pairs={{0,1},{1,0},{2,3},{3,2},{4,5},{5,4},{6,7},{7,6},{8,9},{9,8},{10,11... | collective-permute-start | bytes 589832 | tf_op jit(solution)/shard_map/ppermute | solution.py:353
  2.4 0.7 %collective-permute-start.1 = (bf16[4,192,128]{2,1,0:T(8,128)(2,1)S(1)}, bf16[4,192,128]{2,1,0:T(8,128)(2,1)S(1)}, u32[]{:S(2)}, u32[]{:S(2)}) collective-permute-start(bf16[4,192,128]{2,1,0:T(8,128)(2,1)S(1)} %get-tuple-element.17), channel_id=1, source_target_pairs={{1,2},{3,4},{5,6},{7,8},{9,10},{11,12},{13,14},{2,1},{4,3},{6,5},{... | collective-permute-start | bytes 589832 | tf_op jit(solution)/shard_map/ppermute | solution.py:354
  3.1 0.0 copy-done
  3.1 0.0 copy-done.1
  3.1 0.0 copy-done.2
  3.1 0.0 copy-done.3
  3.1 0.0 copy-done.4
  3.1 0.0 copy-done.5
  3.1 3.3 %backward_local.1 = (bf16[16,1,48,128]{3,2,1,0:T(8,128)(2,1)S(1)}, bf16[6,192,128]{2,1,0:T(8,128)(2,1)}, f32[2,4,192,128]{3,2,1,0:T(8,128)S(1)}, bf16[576,1728]{1,0:T(8,128)(2,1)S(1)}) custom-call(bf16[4,3,192,128]{3,2,1,0:T(8,128)(2,1)S(1)} %bitcast.9, bf16[4,3,192,128]{3,2,1,0:T(8,128)(2,1)S(1)} %bitcast.11, bf16[2,3,192,128]{3,2,1,0:T(8,128)(2,1)S(1)} %bitcast.14, ...), custom_call_target="tpu_custom_call" | custom-call | tf_op jit(solution)/shard_map/backward_local/pallas_call | solution.py:307
  6.5 1.4 %collective-permute-start.3 = (bf16[6,192,128]{2,1,0:T(8,128)(2,1)}, bf16[6,192,128]{2,1,0:T(8,128)(2,1)}, u32[]{:S(2)}, u32[]{:S(2)}) collective-permute-start(bf16[6,192,128]{2,1,0:T(8,128)(2,1)} %get-tuple-element.26), channel_id=1, source_target_pairs={{1,2},{3,4},{5,6},{7,8},{9,10},{11,12},{13,14},{2,1},{4,3},{6,5},{... | collective-permute-start | bytes 884744 | tf_op jit(solution)/shard_map/ppermute | solution.py:368
  7.9 0.0 collective-permute-done.inner
  7.9 0.0 collective-permute-done.1.outer
  7.9 0.0 copy-start.6
  7.9 2.5 %backward_edge.1 = bf16[16,3,48,128]{3,2,1,0:T(8,128)(2,1)} custom-call(bf16[4,3,192,128]{3,2,1,0:T(8,128)(2,1)S(1)} %bitcast.10, bf16[4,192,128]{2,1,0:T(8,128)(2,1)S(1)} %collective-permute-done.inner, bf16[4,192,128]{2,1,0:T(8,128)(2,1)S(1)} %collective-permute-done.1.outer, bf16[4,3,192,128]{3,2,1,0:T(8,128)(2,1)S(1)} %bitcast.12, ...), custom_call_target="tpu_custom_call" | custom-call | tf_op jit(solution)/shard_map/backward_edge/pallas_call | solution.py:307
  10.3 10.7 %all-to-all-start = ((bf16[16,3,48,128]{3,2,1,0:T(8,128)(2,1)}), bf16[16,3,48,128]{3,2,1,0:T(8,128)(2,1)}, u32[]{:S(2)}, u32[]{:S(2)}) async-start(bf16[16,3,48,128]{3,2,1,0:T(8,128)(2,1)} %backward_edge.1), calls=%async_computation | async-start | bytes 1179648 | tf_op jit(solution)/shard_map/all_to_all | solution.py:378
  21.1 0.0 copy-done.6
  21.1 4.0 %forward_local.1 = (bf16[4,3,192,128]{3,2,1,0:T(8,128)(2,1)}, bf16[6,192,128]{2,1,0:T(8,128)(2,1)}, f32[2,4,192,128]{3,2,1,0:T(8,128)S(1)}, bf16[3,192,1728]{2,1,0:T(8,128)(2,1)S(1)}) custom-call(bf16[4,3,192,128]{3,2,1,0:T(8,128)(2,1)S(1)} %bitcast.13, bf16[2,3,192,128]{3,2,1,0:T(8,128)(2,1)S(1)} %bitcast.15, bf16[3,3,3,192,192]{4,3,2,1,0:T(8,128)(2,1)S(1)} %copy-done, ...), custom_call_target="tpu_custom_call" | custom-call | flops 10000000000 | tf_op jit(solution)/shard_map/forward_local/pallas_call | solution.py:307
  25.1 0.4 %collective-permute-start.2 = (bf16[6,192,128]{2,1,0:T(8,128)(2,1)}, bf16[6,192,128]{2,1,0:T(8,128)(2,1)S(1)}, u32[]{:S(2)}, u32[]{:S(2)}) collective-permute-start(bf16[6,192,128]{2,1,0:T(8,128)(2,1)} %get-tuple-element.25), channel_id=1, source_target_pairs={{0,1},{1,0},{2,3},{3,2},{4,5},{5,4},{6,7},{7,6},{8,9},{9,8},{10,11... | collective-permute-start | bytes 884744 | tf_op jit(solution)/shard_map/ppermute | solution.py:407
  25.5 0.0 collective-permute-done.3.outer_hbm
  25.5 1.4 %collective-permute-done.2.inner_hbm = bf16[6,192,128]{2,1,0:T(8,128)(2,1)S(1)} collective-permute-done((bf16[6,192,128]{2,1,0:T(8,128)(2,1)}, bf16[6,192,128]{2,1,0:T(8,128)(2,1)S(1)}, u32[]{:S(2)}, u32[]{:S(2)}) %collective-permute-start.2) | collective-permute-done | bytes 294944 | tf_op jit(solution)/shard_map/ppermute | solution.py:407
  27.0 0.0 copy-start.7
  27.0 0.7 %copy-done.7 = bf16[6,192,128]{2,1,0:T(8,128)(2,1)} copy-done((bf16[6,192,128]{2,1,0:T(8,128)(2,1)}, bf16[6,192,128]{2,1,0:T(8,128)(2,1)S(1)}, u32[]{:S(2)}) %copy-start.7) | copy-done | bytes 294936
  27.7 3.6 %forward_edge.1 = bf16[4,3,192,128]{3,2,1,0:T(8,128)(2,1)} custom-call(bf16[6,192,128]{2,1,0:T(8,128)(2,1)} %copy-done.7, bf16[6,192,128]{2,1,0:T(8,128)(2,1)} %collective-permute-done.3.outer_hbm, f32[2,4,192,128]{3,2,1,0:T(8,128)S(1)} %get-tuple-element.27.partial, ...), custom_call_target="tpu_custom_call", output_to_operand_aliasing={{}: (6, {})} | custom-call | tf_op jit(solution)/shard_map/forward_edge/pallas_call | solution.py:307
  31.3 5.4 %all-to-all-done = bf16[16,3,48,128]{3,2,1,0:T(8,128)(2,1)} async-done(((bf16[16,3,48,128]{3,2,1,0:T(8,128)(2,1)}), bf16[16,3,48,128]{3,2,1,0:T(8,128)(2,1)}, u32[]{:S(2)}, u32[]{:S(2)}) %all-to-all-start) | async-done | bytes 589856 | tf_op jit(solution)/shard_map/all_to_all | solution.py:378
  36.7 2.0 %unpack.1 = bf16[4,48,8,192]{3,2,1,0:T(8,128)(2,1)} custom-call(bf16[48,48,128]{2,1,0:T(8,128)(2,1)} %bitcast.7.src_hbm), custom_call_target="tpu_custom_call" | custom-call | tf_op jit(solution)/shard_map/unpack/pallas_call | solution.py:307
Async XLA Ops:
  0.6 2.5 %copy-start = (bf16[3,3,3,192,192]{4,3,2,1,0:T(8,128)(2,1)S(1)}, bf16[3,3,3,192,192]{4,3,2,1,0:T(8,128)(2,1)}, u32[]{:S(2)}) copy-start(bf16[3,3,3,192,192]{4,3,2,1,0:T(8,128)(2,1)} %kern.2) | copy-start | bytes 5971972
  0.6 2.5 %copy-start.1 = (bf16[4,3,128,192]{2,3,1,0:T(8,128)(2,1)S(1)}, bf16[4,3,128,192]{2,3,1,0:T(8,128)(2,1)}, u32[]{:S(2)}) copy-start(bf16[4,3,128,192]{2,3,1,0:T(8,128)(2,1)} %param.9) | copy-start | bytes 1769476
  0.7 2.5 %copy-start.2 = (bf16[4,3,128,192]{2,3,1,0:T(8,128)(2,1)S(1)}, bf16[4,3,128,192]{2,3,1,0:T(8,128)(2,1)}, u32[]{:S(2)}) copy-start(bf16[4,3,128,192]{2,3,1,0:T(8,128)(2,1)} %param.7) | copy-start | bytes 1769476
  0.7 2.5 %copy-start.3 = (bf16[2,3,128,192]{2,3,1,0:T(8,128)(2,1)S(1)}, bf16[2,3,128,192]{2,3,1,0:T(8,128)(2,1)}, u32[]{:S(2)}) copy-start(bf16[2,3,128,192]{2,3,1,0:T(8,128)(2,1)} %param.8) | copy-start | bytes 884740
  0.7 2.5 %copy-start.4 = (f32[192]{0:T(256)S(1)}, f32[192]{0:T(256)}, u32[]{:S(2)}) copy-start(f32[192]{0:T(256)} %param.11) | copy-start | bytes 2308
  0.7 2.5 %copy-start.5 = (f32[192]{0:T(256)S(1)}, f32[192]{0:T(256)}, u32[]{:S(2)}) copy-start(f32[192]{0:T(256)} %param.12) | copy-start | bytes 2308
  1.9 6.0 %collective-permute-start = (bf16[4,192,128]{2,1,0:T(8,128)(2,1)S(1)}, bf16[4,192,128]{2,1,0:T(8,128)(2,1)S(1)}, u32[]{:S(2)}, u32[]{:S(2)}) collective-permute-start(bf16[4,192,128]{2,1,0:T(8,128)(2,1)S(1)} %get-tuple-element.16), channel_id=1, source_target_pairs={{0,1},{1,0},{2,3},{3,2},{4,5},{5,4},{6,7},{7,6},{8,9},{9,8},{10,11... | collective-permute-start | bytes 589832 | tf_op jit(solution)/shard_map/ppermute | solution.py:353
  2.4 5.5 %collective-permute-start.1 = (bf16[4,192,128]{2,1,0:T(8,128)(2,1)S(1)}, bf16[4,192,128]{2,1,0:T(8,128)(2,1)S(1)}, u32[]{:S(2)}, u32[]{:S(2)}) collective-permute-start(bf16[4,192,128]{2,1,0:T(8,128)(2,1)S(1)} %get-tuple-element.17), channel_id=1, source_target_pairs={{1,2},{3,4},{5,6},{7,8},{9,10},{11,12},{13,14},{2,1},{4,3},{6,5},{... | collective-permute-start | bytes 589832 | tf_op jit(solution)/shard_map/ppermute | solution.py:354
  6.5 19.1 %collective-permute-start.3 = (bf16[6,192,128]{2,1,0:T(8,128)(2,1)}, bf16[6,192,128]{2,1,0:T(8,128)(2,1)}, u32[]{:S(2)}, u32[]{:S(2)}) collective-permute-start(bf16[6,192,128]{2,1,0:T(8,128)(2,1)} %get-tuple-element.26), channel_id=1, source_target_pairs={{1,2},{3,4},{5,6},{7,8},{9,10},{11,12},{13,14},{2,1},{4,3},{6,5},{... | collective-permute-start | bytes 884744 | tf_op jit(solution)/shard_map/ppermute | solution.py:368
  7.9 13.2 %copy-start.6 = (f32[192]{0:T(256)S(1)}, f32[192]{0:T(256)}, u32[]{:S(2)}) copy-start(f32[192]{0:T(256)} %param.13) | copy-start | bytes 2308
  10.3 26.3 %all-to-all-start = ((bf16[16,3,48,128]{3,2,1,0:T(8,128)(2,1)}), bf16[16,3,48,128]{3,2,1,0:T(8,128)(2,1)}, u32[]{:S(2)}, u32[]{:S(2)}) async-start(bf16[16,3,48,128]{3,2,1,0:T(8,128)(2,1)} %backward_edge.1), calls=%async_computation | async-start | bytes 1179648 | tf_op jit(solution)/shard_map/all_to_all | solution.py:378
  25.1 1.9 %collective-permute-start.2 = (bf16[6,192,128]{2,1,0:T(8,128)(2,1)}, bf16[6,192,128]{2,1,0:T(8,128)(2,1)S(1)}, u32[]{:S(2)}, u32[]{:S(2)}) collective-permute-start(bf16[6,192,128]{2,1,0:T(8,128)(2,1)} %get-tuple-element.25), channel_id=1, source_target_pairs={{0,1},{1,0},{2,3},{3,2},{4,5},{5,4},{6,7},{7,6},{8,9},{9,8},{10,11... | collective-permute-start | bytes 884744 | tf_op jit(solution)/shard_map/ppermute | solution.py:407
  27.0 0.7 %copy-start.7 = (bf16[6,192,128]{2,1,0:T(8,128)(2,1)}, bf16[6,192,128]{2,1,0:T(8,128)(2,1)S(1)}, u32[]{:S(2)}) copy-start(bf16[6,192,128]{2,1,0:T(8,128)(2,1)S(1)} %collective-permute-done.2.inner_hbm) | copy-start | bytes 884740

commit v6 on v5

--- a/solution.py
+++ b/solution.py
@@ -26,7 +26,7 @@
             seen = jnp.where(at < cols - 1, pltpu.roll(x32, cols - 1, 1), 0.0)
         else:
             seen = jnp.where(at > 0, pltpu.roll(x32, 1, 1), 0.0)
-        dst[row0 + n * chans : row0 + (n + 1) * chans, lanes : lanes + cols] = seen.astype(dst.dtype)
+        dst[pl.ds(row0 + n * chans, chans), pl.ds(lanes, cols)] = seen.astype(dst.dtype)
 
 
 def normalized(x, gain, shift):
@@ -104,7 +104,7 @@
     return inner, rows - 1 - inner
 
 
-def staging_kernel(cot, to_inner, to_outer, sems):
+def staging_kernel(cot, to_outer, to_inner, sems):
     inner, outer = rows_sent(cot.shape[1])
     for c in fetch([(cot.at[:, inner], to_inner), (cot.at[:, outer], to_outer)], sems):
         c.wait()
@@ -123,9 +123,11 @@
         [(feat.at[:, outer], to_outer.at[pl.ds(past, frames)]), (cache.at[:, outer], to_outer.at[pl.ds(0, past)])],
         edge_sems,
     )
-    for p in range(rows):
+    @pl.loop(0, rows)
+    def _(p):
         for f in range(frames):
-            shifted_to(stack, p * block, f * cols, cot[f, p], (1, 0, -1))
+            shifted_to(stack, pl.multiple_of(p * block, 64), f * cols, cot[f, p], (1, 0, -1))
+
     for t in range(3):
         taps = [kern[t, 2 - d, j] for d in range(3) for j in range(3)]
         rows_of_t = pl.ds((2 - t) * chans, chans)
@@ -148,7 +150,7 @@
 
 
 def backward_edge_kernel(
-    cot, inner, outer, feat, partial, weights, gain_in, shift_in, middle, out, stack, sent, out_sem, *, packed
+    cot, outer, inner, feat, partial, weights, gain_in, shift_in, middle, out, stack, sent, out_sem, *, packed
 ):
     frames, rows, chans, cols = cot.shape
     block = 3 * chans
@@ -342,7 +344,7 @@
     def sent(n):
         return (slabs, n, frames * per * chans // 128, 128) if packed else (frames, n, cols, chans)
 
-    cot_in, cot_across = call(
+    cot_across, cot_in = call(
         staging_kernel,
         "staging",
         [(cot, HBM)],
@@ -350,8 +352,8 @@
         [pltpu.SemaphoreType.DMA((2,))],
         flops=HINT,
     )
+    cot_across = lax.ppermute(cot_across, "slab", across)
     cot_in = lax.ppermute(cot_in, "slab", within)
-    cot_across = lax.ppermute(cot_across, "slab", across)
     middle, act_across, part, lhs = call(
         functools.partial(backward_local_kernel, packed=packed),
         "backward_local",
@@ -369,7 +371,7 @@
     grad = call(
         functools.partial(backward_edge_kernel, packed=packed),
         "backward_edge",
-        [(a, VMEM) for a in (cot, cot_in, cot_across, feat, part, lhs, gain, shift, middle)],
+        [(a, VMEM) for a in (cot, cot_across, cot_in, feat, part, lhs, gain, shift, middle)],
         [(bf16(sent(rows)), HBM)],
         [vmem16((2, block, frames * cols)), vmem16(sent(edge_rows)), pltpu.SemaphoreType.DMA((3,))],
     )

time: 39 us -> 38.8 us (level)
    all_to_all x1, starting transfers between devices: 10.7 us -> 6.77 us  [body(): lax.all_to_all(grad, 'slab', split_axis=0, concat_axis=0, tiled=True)]
    ppermute x1, starting transfers between devices: 0.52 us -> 4.38 us  [body(): cot_in = lax.ppermute(cot_in, 'slab', within)]
  transfers between devices with their start and end apart: 5 -> 5, of which waited for: 2 -> 2; matrix products, arithmetic and copies ran while one was open for 0% -> 0% of each run, Pallas kernels for 35% -> 34%
where the time goes in v6:
time: 38.8 us; the launch traced here: 38.5 us
  Pallas kernels  16.4 us (42%)
  starting transfers between devices  13.8 us (36%)
  waiting for transfers between devices  6.84 us (18%)
  between operations  0.77 us (2%)
  local copies, waits for them, and re-layouts  0.75 us (2%)
    pallas_call x6, Pallas kernels, call(): pl.pallas_call(kernel, out_shape=[pltpu.HBM(o.shape, o.dtype) if where is...  16.4 us
    all_to_all x1, starting transfers between devices, body(): lax.all_to_all(grad, 'slab', split_axis=0, concat_axis=0, tiled=True)  6.77 us
    all_to_all x1, waiting for transfers between devices, body(): lax.all_to_all(grad, 'slab', split_axis=0, concat_axis=0, tiled=True)  5.41 us
    ppermute x1, starting transfers between devices, body(): cot_in = lax.ppermute(cot_in, 'slab', within)  4.38 us
    ppermute x1, waiting for transfers between devices, body(): act_in = lax.ppermute(act_in, 'slab', within)  1.43 us
    ppermute x1, starting transfers between devices, body(): act_across = lax.ppermute(act_across, 'slab', across)  1.38 us
    ppermute x1, starting transfers between devices, body(): cot_across = lax.ppermute(cot_across, 'slab', across)  0.8 us
  transfers between devices with their start and end apart: 5, of which 2 were waited for; matrix products, arithmetic and copies ran while one was open for 0% of the time, Pallas kernels for 34%

profile of v6, /device:TPU:0, one launch (start us, length us, event | category | flops | bytes accessed | tf_op | source)
XLA Modules:
  0.0 38.5 jit_solution(9176248783528451868)
XLA Ops:
  0.6 0.0 copy-start
  0.6 0.0 copy-start.1
  0.7 0.0 copy-start.2
  0.7 0.0 copy-start.3
  0.7 0.0 copy-start.4
  0.7 0.0 copy-start.5
  0.7 1.2 %staging.1 = (bf16[4,192,128]{2,1,0:T(8,128)(2,1)S(1)}, bf16[4,192,128]{2,1,0:T(8,128)(2,1)S(1)}) custom-call(bf16[4,3,192,128]{3,2,1,0:T(8,128)(2,1)} %bitcast.8), custom_call_target="tpu_custom_call" | custom-call | flops 10000000000 | tf_op jit(solution)/shard_map/staging/pallas_call | solution.py:309
  1.9 0.8 %collective-permute-start = (bf16[4,192,128]{2,1,0:T(8,128)(2,1)S(1)}, bf16[4,192,128]{2,1,0:T(8,128)(2,1)S(1)}, u32[]{:S(2)}, u32[]{:S(2)}) collective-permute-start(bf16[4,192,128]{2,1,0:T(8,128)(2,1)S(1)} %get-tuple-element.16), channel_id=1, source_target_pairs={{1,2},{3,4},{5,6},{7,8},{9,10},{11,12},{13,14},{2,1},{4,3},{6,5},{... | collective-permute-start | bytes 589832 | tf_op jit(solution)/shard_map/ppermute | solution.py:355
  2.7 4.4 %collective-permute-start.1 = (bf16[4,192,128]{2,1,0:T(8,128)(2,1)S(1)}, bf16[4,192,128]{2,1,0:T(8,128)(2,1)S(1)}, u32[]{:S(2)}, u32[]{:S(2)}) collective-permute-start(bf16[4,192,128]{2,1,0:T(8,128)(2,1)S(1)} %get-tuple-element.17), channel_id=1, source_target_pairs={{0,1},{1,0},{2,3},{3,2},{4,5},{5,4},{6,7},{7,6},{8,9},{9,8},{10,11... | collective-permute-start | bytes 589832 | tf_op jit(solution)/shard_map/ppermute | solution.py:356
  7.1 0.0 copy-done
  7.1 0.0 copy-done.1
  7.1 0.0 copy-done.2
  7.1 0.0 copy-done.3
  7.1 0.0 copy-done.4
  7.1 0.0 copy-done.5
  7.1 3.1 %backward_local.1 = (bf16[16,1,48,128]{3,2,1,0:T(8,128)(2,1)S(1)}, bf16[6,192,128]{2,1,0:T(8,128)(2,1)}, f32[2,4,192,128]{3,2,1,0:T(8,128)S(1)}, bf16[576,1728]{1,0:T(8,128)(2,1)S(1)}) custom-call(bf16[4,3,192,128]{3,2,1,0:T(8,128)(2,1)S(1)} %bitcast.9, bf16[4,3,192,128]{3,2,1,0:T(8,128)(2,1)S(1)} %bitcast.11, bf16[2,3,192,128]{3,2,1,0:T(8,128)(2,1)S(1)} %bitcast.14, ...), custom_call_target="tpu_custom_call" | custom-call | tf_op jit(solution)/shard_map/backward_local/pallas_call | solution.py:309
  10.3 1.4 %collective-permute-start.3 = (bf16[6,192,128]{2,1,0:T(8,128)(2,1)}, bf16[6,192,128]{2,1,0:T(8,128)(2,1)}, u32[]{:S(2)}, u32[]{:S(2)}) collective-permute-start(bf16[6,192,128]{2,1,0:T(8,128)(2,1)} %get-tuple-element.26), channel_id=1, source_target_pairs={{1,2},{3,4},{5,6},{7,8},{9,10},{11,12},{13,14},{2,1},{4,3},{6,5},{... | collective-permute-start | bytes 884744 | tf_op jit(solution)/shard_map/ppermute | solution.py:370
  11.6 0.0 collective-permute-done.outer
  11.6 0.0 collective-permute-done.1.inner
  11.6 0.0 copy-start.6
  11.6 2.5 %backward_edge.1 = bf16[16,3,48,128]{3,2,1,0:T(8,128)(2,1)} custom-call(bf16[4,3,192,128]{3,2,1,0:T(8,128)(2,1)S(1)} %bitcast.10, bf16[4,192,128]{2,1,0:T(8,128)(2,1)S(1)} %collective-permute-done.outer, bf16[4,192,128]{2,1,0:T(8,128)(2,1)S(1)} %collective-permute-done.1.inner, bf16[4,3,192,128]{3,2,1,0:T(8,128)(2,1)S(1)} %bitcast.12, ...), custom_call_target="tpu_custom_call" | custom-call | tf_op jit(solution)/shard_map/backward_edge/pallas_call | solution.py:309
  14.1 6.8 %all-to-all-start = ((bf16[16,3,48,128]{3,2,1,0:T(8,128)(2,1)}), bf16[16,3,48,128]{3,2,1,0:T(8,128)(2,1)}, u32[]{:S(2)}, u32[]{:S(2)}) async-start(bf16[16,3,48,128]{3,2,1,0:T(8,128)(2,1)} %backward_edge.1), calls=%async_computation | async-start | bytes 1179648 | tf_op jit(solution)/shard_map/all_to_all | solution.py:380
  20.9 0.0 copy-done.6
  20.9 4.0 %forward_local.1 = (bf16[4,3,192,128]{3,2,1,0:T(8,128)(2,1)}, bf16[6,192,128]{2,1,0:T(8,128)(2,1)}, f32[2,4,192,128]{3,2,1,0:T(8,128)S(1)}, bf16[3,192,1728]{2,1,0:T(8,128)(2,1)S(1)}) custom-call(bf16[4,3,192,128]{3,2,1,0:T(8,128)(2,1)S(1)} %bitcast.13, bf16[2,3,192,128]{3,2,1,0:T(8,128)(2,1)S(1)} %bitcast.15, bf16[3,3,3,192,192]{4,3,2,1,0:T(8,128)(2,1)S(1)} %copy-done, ...), custom_call_target="tpu_custom_call" | custom-call | flops 10000000000 | tf_op jit(solution)/shard_map/forward_local/pallas_call | solution.py:309
  24.9 0.4 %collective-permute-start.2 = (bf16[6,192,128]{2,1,0:T(8,128)(2,1)}, bf16[6,192,128]{2,1,0:T(8,128)(2,1)S(1)}, u32[]{:S(2)}, u32[]{:S(2)}) collective-permute-start(bf16[6,192,128]{2,1,0:T(8,128)(2,1)} %get-tuple-element.25), channel_id=1, source_target_pairs={{0,1},{1,0},{2,3},{3,2},{4,5},{5,4},{6,7},{7,6},{8,9},{9,8},{10,11... | collective-permute-start | bytes 884744 | tf_op jit(solution)/shard_map/ppermute | solution.py:409
  25.4 0.0 collective-permute-done.3.outer_hbm
  25.4 1.4 %collective-permute-done.2.inner_hbm = bf16[6,192,128]{2,1,0:T(8,128)(2,1)S(1)} collective-permute-done((bf16[6,192,128]{2,1,0:T(8,128)(2,1)}, bf16[6,192,128]{2,1,0:T(8,128)(2,1)S(1)}, u32[]{:S(2)}, u32[]{:S(2)}) %collective-permute-start.2) | collective-permute-done | bytes 294944 | tf_op jit(solution)/shard_map/ppermute | solution.py:409
  26.8 0.0 copy-start.7
  26.8 0.7 %copy-done.7 = bf16[6,192,128]{2,1,0:T(8,128)(2,1)} copy-done((bf16[6,192,128]{2,1,0:T(8,128)(2,1)}, bf16[6,192,128]{2,1,0:T(8,128)(2,1)S(1)}, u32[]{:S(2)}) %copy-start.7) | copy-done | bytes 294936
  27.5 3.6 %forward_edge.1 = bf16[4,3,192,128]{3,2,1,0:T(8,128)(2,1)} custom-call(bf16[6,192,128]{2,1,0:T(8,128)(2,1)} %copy-done.7, bf16[6,192,128]{2,1,0:T(8,128)(2,1)} %collective-permute-done.3.outer_hbm, f32[2,4,192,128]{3,2,1,0:T(8,128)S(1)} %get-tuple-element.27.partial, ...), custom_call_target="tpu_custom_call", output_to_operand_aliasing={{}: (6, {})} | custom-call | tf_op jit(solution)/shard_map/forward_edge/pallas_call | solution.py:309
  31.1 5.4 %all-to-all-done = bf16[16,3,48,128]{3,2,1,0:T(8,128)(2,1)} async-done(((bf16[16,3,48,128]{3,2,1,0:T(8,128)(2,1)}), bf16[16,3,48,128]{3,2,1,0:T(8,128)(2,1)}, u32[]{:S(2)}, u32[]{:S(2)}) %all-to-all-start) | async-done | bytes 589856 | tf_op jit(solution)/shard_map/all_to_all | solution.py:380
  36.5 2.0 %unpack.1 = bf16[4,48,8,192]{3,2,1,0:T(8,128)(2,1)} custom-call(bf16[48,48,128]{2,1,0:T(8,128)(2,1)} %bitcast.7.src_hbm), custom_call_target="tpu_custom_call" | custom-call | tf_op jit(solution)/shard_map/unpack/pallas_call | solution.py:309
Async XLA Ops:
  0.6 6.5 %copy-start = (bf16[3,3,3,192,192]{4,3,2,1,0:T(8,128)(2,1)S(1)}, bf16[3,3,3,192,192]{4,3,2,1,0:T(8,128)(2,1)}, u32[]{:S(2)}) copy-start(bf16[3,3,3,192,192]{4,3,2,1,0:T(8,128)(2,1)} %kern.2) | copy-start | bytes 5971972
  0.6 6.5 %copy-start.1 = (bf16[4,3,128,192]{2,3,1,0:T(8,128)(2,1)S(1)}, bf16[4,3,128,192]{2,3,1,0:T(8,128)(2,1)}, u32[]{:S(2)}) copy-start(bf16[4,3,128,192]{2,3,1,0:T(8,128)(2,1)} %param.9) | copy-start | bytes 1769476
  0.7 6.5 %copy-start.2 = (bf16[4,3,128,192]{2,3,1,0:T(8,128)(2,1)S(1)}, bf16[4,3,128,192]{2,3,1,0:T(8,128)(2,1)}, u32[]{:S(2)}) copy-start(bf16[4,3,128,192]{2,3,1,0:T(8,128)(2,1)} %param.7) | copy-start | bytes 1769476
  0.7 6.4 %copy-start.3 = (bf16[2,3,128,192]{2,3,1,0:T(8,128)(2,1)S(1)}, bf16[2,3,128,192]{2,3,1,0:T(8,128)(2,1)}, u32[]{:S(2)}) copy-start(bf16[2,3,128,192]{2,3,1,0:T(8,128)(2,1)} %param.8) | copy-start | bytes 884740
  0.7 6.4 %copy-start.4 = (f32[192]{0:T(256)S(1)}, f32[192]{0:T(256)}, u32[]{:S(2)}) copy-start(f32[192]{0:T(256)} %param.11) | copy-start | bytes 2308
  0.7 6.4 %copy-start.5 = (f32[192]{0:T(256)S(1)}, f32[192]{0:T(256)}, u32[]{:S(2)}) copy-start(f32[192]{0:T(256)} %param.12) | copy-start | bytes 2308
  1.9 9.7 %collective-permute-start = (bf16[4,192,128]{2,1,0:T(8,128)(2,1)S(1)}, bf16[4,192,128]{2,1,0:T(8,128)(2,1)S(1)}, u32[]{:S(2)}, u32[]{:S(2)}) collective-permute-start(bf16[4,192,128]{2,1,0:T(8,128)(2,1)S(1)} %get-tuple-element.16), channel_id=1, source_target_pairs={{1,2},{3,4},{5,6},{7,8},{9,10},{11,12},{13,14},{2,1},{4,3},{6,5},{... | collective-permute-start | bytes 589832 | tf_op jit(solution)/shard_map/ppermute | solution.py:355
  2.7 8.9 %collective-permute-start.1 = (bf16[4,192,128]{2,1,0:T(8,128)(2,1)S(1)}, bf16[4,192,128]{2,1,0:T(8,128)(2,1)S(1)}, u32[]{:S(2)}, u32[]{:S(2)}) collective-permute-start(bf16[4,192,128]{2,1,0:T(8,128)(2,1)S(1)} %get-tuple-element.17), channel_id=1, source_target_pairs={{0,1},{1,0},{2,3},{3,2},{4,5},{5,4},{6,7},{7,6},{8,9},{9,8},{10,11... | collective-permute-start | bytes 589832 | tf_op jit(solution)/shard_map/ppermute | solution.py:356
  10.3 15.1 %collective-permute-start.3 = (bf16[6,192,128]{2,1,0:T(8,128)(2,1)}, bf16[6,192,128]{2,1,0:T(8,128)(2,1)}, u32[]{:S(2)}, u32[]{:S(2)}) collective-permute-start(bf16[6,192,128]{2,1,0:T(8,128)(2,1)} %get-tuple-element.26), channel_id=1, source_target_pairs={{1,2},{3,4},{5,6},{7,8},{9,10},{11,12},{13,14},{2,1},{4,3},{6,5},{... | collective-permute-start | bytes 884744 | tf_op jit(solution)/shard_map/ppermute | solution.py:370
  11.6 9.3 %copy-start.6 = (f32[192]{0:T(256)S(1)}, f32[192]{0:T(256)}, u32[]{:S(2)}) copy-start(f32[192]{0:T(256)} %param.13) | copy-start | bytes 2308
  14.1 22.4 %all-to-all-start = ((bf16[16,3,48,128]{3,2,1,0:T(8,128)(2,1)}), bf16[16,3,48,128]{3,2,1,0:T(8,128)(2,1)}, u32[]{:S(2)}, u32[]{:S(2)}) async-start(bf16[16,3,48,128]{3,2,1,0:T(8,128)(2,1)} %backward_edge.1), calls=%async_computation | async-start | bytes 1179648 | tf_op jit(solution)/shard_map/all_to_all | solution.py:380
  24.9 1.9 %collective-permute-start.2 = (bf16[6,192,128]{2,1,0:T(8,128)(2,1)}, bf16[6,192,128]{2,1,0:T(8,128)(2,1)S(1)}, u32[]{:S(2)}, u32[]{:S(2)}) collective-permute-start(bf16[6,192,128]{2,1,0:T(8,128)(2,1)} %get-tuple-element.25), channel_id=1, source_target_pairs={{0,1},{1,0},{2,3},{3,2},{4,5},{5,4},{6,7},{7,6},{8,9},{9,8},{10,11... | collective-permute-start | bytes 884744 | tf_op jit(solution)/shard_map/ppermute | solution.py:409
  26.8 0.7 %copy-start.7 = (bf16[6,192,128]{2,1,0:T(8,128)(2,1)}, bf16[6,192,128]{2,1,0:T(8,128)(2,1)S(1)}, u32[]{:S(2)}) copy-start(bf16[6,192,128]{2,1,0:T(8,128)(2,1)S(1)} %collective-permute-done.2.inner_hbm) | copy-start | bytes 884740

commit v7 on v6

--- a/solution.py
+++ b/solution.py
@@ -156,7 +156,7 @@
     block = 3 * chans
     written = []
     if rows > 2:
-        written.append(pltpu.make_async_copy(middle, out.at[:, 1 : rows - 1], out_sem.at[2]))
+        written.append(pltpu.make_async_copy(middle, out.at[:, 1 : rows - 1], out_sem.at[4]))
         written[0].start()
     slot = jnp.where(lax.rem(lax.axis_index("slab"), 2) == 0, 1, 0)
     for f in range(frames):
@@ -172,8 +172,10 @@
                 acc = [a + b for a, b in zip(acc, more)]
         grads = [finish(acc[f], feat[f, r], cot[f, r], gain, shift) for f in range(frames)]
         put_row(sent, edge, grads, packed)
-        written.append(pltpu.make_async_copy(sent.at[:, edge], out.at[:, r], out_sem.at[edge]))
-        written[-1].start()
+        half = out.shape[0] // 2
+        for n, part in enumerate((pl.ds(0, half), pl.ds(half, half))):
+            written.append(pltpu.make_async_copy(sent.at[part, edge], out.at[part, r], out_sem.at[2 * edge + n]))
+            written[-1].start()
     for c in written:
         c.wait()
 
@@ -373,14 +375,14 @@
         "backward_edge",
         [(a, VMEM) for a in (cot, cot_across, cot_in, feat, part, lhs, gain, shift, middle)],
         [(bf16(sent(rows)), HBM)],
-        [vmem16((2, block, frames * cols)), vmem16(sent(edge_rows)), pltpu.SemaphoreType.DMA((3,))],
+        [vmem16((2, block, frames * cols)), vmem16(sent(edge_rows)), pltpu.SemaphoreType.DMA((5,))],
     )
 
     if packed:
         moved = lax.all_to_all(grad, "slab", split_axis=0, concat_axis=0, tiled=True)
         moved = moved.reshape(slabs * rows, -1, 128)
         relaid = (frames, slabs * rows, per, chans)
-        parts = 4 if slabs * rows % 4 == 0 else 1
+        parts = 2 if slabs * rows % 2 == 0 else 1
         relaid = call(
             unpack_kernel,
             "unpack",

time: 38.8 us -> 38.8 us (level)
  no operation moved by 1% of the time
where the time goes in v7:
time: 38.8 us; the launch traced here: 38.5 us
  Pallas kernels  16.4 us (42%)
  starting transfers between devices  13.8 us (36%)
  waiting for transfers between devices  6.84 us (18%)
  between operations  0.77 us (2%)
  local copies, waits for them, and re-layouts  0.75 us (2%)
    pallas_call x6, Pallas kernels, call(): pl.pallas_call(kernel, out_shape=[pltpu.HBM(o.shape, o.dtype) if where is...  16.4 us
    all_to_all x1, starting transfers between devices, body(): lax.all_to_all(grad, 'slab', split_axis=0, concat_axis=0, tiled=True)  6.77 us
    all_to_all x1, waiting for transfers between devices, body(): lax.all_to_all(grad, 'slab', split_axis=0, concat_axis=0, tiled=True)  5.4 us
    ppermute x1, starting transfers between devices, body(): cot_in = lax.ppermute(cot_in, 'slab', within)  4.38 us
    ppermute x1, waiting for transfers between devices, body(): act_in = lax.ppermute(act_in, 'slab', within)  1.44 us
    ppermute x1, starting transfers between devices, body(): act_across = lax.ppermute(act_across, 'slab', across)  1.38 us
    ppermute x1, starting transfers between devices, body(): cot_across = lax.ppermute(cot_across, 'slab', across)  0.8 us
  transfers between devices with their start and end apart: 5, of which 2 were waited for; matrix products, arithmetic and copies ran while one was open for 0% of the time, Pallas kernels for 34%

profile of v7, /device:TPU:0, one launch (start us, length us, event | category | flops | bytes accessed | tf_op | source)
XLA Modules:
  0.0 38.5 jit_solution(1351818482580253476)
XLA Ops:
  0.6 0.0 copy-start
  0.6 0.0 copy-start.1
  0.7 0.0 copy-start.2
  0.7 0.0 copy-start.3
  0.7 0.0 copy-start.4
  0.7 0.0 copy-start.5
  0.7 1.2 %staging.1 = (bf16[4,192,128]{2,1,0:T(8,128)(2,1)S(1)}, bf16[4,192,128]{2,1,0:T(8,128)(2,1)S(1)}) custom-call(bf16[4,3,192,128]{3,2,1,0:T(8,128)(2,1)} %bitcast.8), custom_call_target="tpu_custom_call" | custom-call | flops 10000000000 | tf_op jit(solution)/shard_map/staging/pallas_call | solution.py:311
  1.9 0.8 %collective-permute-start = (bf16[4,192,128]{2,1,0:T(8,128)(2,1)S(1)}, bf16[4,192,128]{2,1,0:T(8,128)(2,1)S(1)}, u32[]{:S(2)}, u32[]{:S(2)}) collective-permute-start(bf16[4,192,128]{2,1,0:T(8,128)(2,1)S(1)} %get-tuple-element.16), channel_id=1, source_target_pairs={{1,2},{3,4},{5,6},{7,8},{9,10},{11,12},{13,14},{2,1},{4,3},{6,5},{... | collective-permute-start | bytes 589832 | tf_op jit(solution)/shard_map/ppermute | solution.py:357
  2.7 4.4 %collective-permute-start.1 = (bf16[4,192,128]{2,1,0:T(8,128)(2,1)S(1)}, bf16[4,192,128]{2,1,0:T(8,128)(2,1)S(1)}, u32[]{:S(2)}, u32[]{:S(2)}) collective-permute-start(bf16[4,192,128]{2,1,0:T(8,128)(2,1)S(1)} %get-tuple-element.17), channel_id=1, source_target_pairs={{0,1},{1,0},{2,3},{3,2},{4,5},{5,4},{6,7},{7,6},{8,9},{9,8},{10,11... | collective-permute-start | bytes 589832 | tf_op jit(solution)/shard_map/ppermute | solution.py:358
  7.1 0.0 copy-done
  7.1 0.0 copy-done.1
  7.1 0.0 copy-done.2
  7.1 0.0 copy-done.3
  7.1 0.0 copy-done.4
  7.1 0.0 copy-done.5
  7.1 3.1 %backward_local.1 = (bf16[16,1,48,128]{3,2,1,0:T(8,128)(2,1)S(1)}, bf16[6,192,128]{2,1,0:T(8,128)(2,1)}, f32[2,4,192,128]{3,2,1,0:T(8,128)S(1)}, bf16[576,1728]{1,0:T(8,128)(2,1)S(1)}) custom-call(bf16[4,3,192,128]{3,2,1,0:T(8,128)(2,1)S(1)} %bitcast.9, bf16[4,3,192,128]{3,2,1,0:T(8,128)(2,1)S(1)} %bitcast.11, bf16[2,3,192,128]{3,2,1,0:T(8,128)(2,1)S(1)} %bitcast.14, ...), custom_call_target="tpu_custom_call" | custom-call | tf_op jit(solution)/shard_map/backward_local/pallas_call | solution.py:311
  10.3 1.4 %collective-permute-start.3 = (bf16[6,192,128]{2,1,0:T(8,128)(2,1)}, bf16[6,192,128]{2,1,0:T(8,128)(2,1)}, u32[]{:S(2)}, u32[]{:S(2)}) collective-permute-start(bf16[6,192,128]{2,1,0:T(8,128)(2,1)} %get-tuple-element.26), channel_id=1, source_target_pairs={{1,2},{3,4},{5,6},{7,8},{9,10},{11,12},{13,14},{2,1},{4,3},{6,5},{... | collective-permute-start | bytes 884744 | tf_op jit(solution)/shard_map/ppermute | solution.py:372
  11.6 0.0 collective-permute-done.outer
  11.6 0.0 collective-permute-done.1.inner
  11.6 0.0 copy-start.6
  11.6 2.5 %backward_edge.1 = bf16[16,3,48,128]{3,2,1,0:T(8,128)(2,1)} custom-call(bf16[4,3,192,128]{3,2,1,0:T(8,128)(2,1)S(1)} %bitcast.10, bf16[4,192,128]{2,1,0:T(8,128)(2,1)S(1)} %collective-permute-done.outer, bf16[4,192,128]{2,1,0:T(8,128)(2,1)S(1)} %collective-permute-done.1.inner, bf16[4,3,192,128]{3,2,1,0:T(8,128)(2,1)S(1)} %bitcast.12, ...), custom_call_target="tpu_custom_call" | custom-call | tf_op jit(solution)/shard_map/backward_edge/pallas_call | solution.py:311
  14.1 6.8 %all-to-all-start = ((bf16[16,3,48,128]{3,2,1,0:T(8,128)(2,1)}), bf16[16,3,48,128]{3,2,1,0:T(8,128)(2,1)}, u32[]{:S(2)}, u32[]{:S(2)}) async-start(bf16[16,3,48,128]{3,2,1,0:T(8,128)(2,1)} %backward_edge.1), calls=%async_computation | async-start | bytes 1179648 | tf_op jit(solution)/shard_map/all_to_all | solution.py:382
  20.9 0.0 copy-done.6
  20.9 4.0 %forward_local.1 = (bf16[4,3,192,128]{3,2,1,0:T(8,128)(2,1)}, bf16[6,192,128]{2,1,0:T(8,128)(2,1)}, f32[2,4,192,128]{3,2,1,0:T(8,128)S(1)}, bf16[3,192,1728]{2,1,0:T(8,128)(2,1)S(1)}) custom-call(bf16[4,3,192,128]{3,2,1,0:T(8,128)(2,1)S(1)} %bitcast.13, bf16[2,3,192,128]{3,2,1,0:T(8,128)(2,1)S(1)} %bitcast.15, bf16[3,3,3,192,192]{4,3,2,1,0:T(8,128)(2,1)S(1)} %copy-done, ...), custom_call_target="tpu_custom_call" | custom-call | flops 10000000000 | tf_op jit(solution)/shard_map/forward_local/pallas_call | solution.py:311
  25.0 0.4 %collective-permute-start.2 = (bf16[6,192,128]{2,1,0:T(8,128)(2,1)}, bf16[6,192,128]{2,1,0:T(8,128)(2,1)S(1)}, u32[]{:S(2)}, u32[]{:S(2)}) collective-permute-start(bf16[6,192,128]{2,1,0:T(8,128)(2,1)} %get-tuple-element.25), channel_id=1, source_target_pairs={{0,1},{1,0},{2,3},{3,2},{4,5},{5,4},{6,7},{7,6},{8,9},{9,8},{10,11... | collective-permute-start | bytes 884744 | tf_op jit(solution)/shard_map/ppermute | solution.py:411
  25.4 0.0 collective-permute-done.3.outer_hbm
  25.4 1.4 %collective-permute-done.2.inner_hbm = bf16[6,192,128]{2,1,0:T(8,128)(2,1)S(1)} collective-permute-done((bf16[6,192,128]{2,1,0:T(8,128)(2,1)}, bf16[6,192,128]{2,1,0:T(8,128)(2,1)S(1)}, u32[]{:S(2)}, u32[]{:S(2)}) %collective-permute-start.2) | collective-permute-done | bytes 294944 | tf_op jit(solution)/shard_map/ppermute | solution.py:411
  26.8 0.0 copy-start.7
  26.8 0.7 %copy-done.7 = bf16[6,192,128]{2,1,0:T(8,128)(2,1)} copy-done((bf16[6,192,128]{2,1,0:T(8,128)(2,1)}, bf16[6,192,128]{2,1,0:T(8,128)(2,1)S(1)}, u32[]{:S(2)}) %copy-start.7) | copy-done | bytes 294936
  27.6 3.6 %forward_edge.1 = bf16[4,3,192,128]{3,2,1,0:T(8,128)(2,1)} custom-call(bf16[6,192,128]{2,1,0:T(8,128)(2,1)} %copy-done.7, bf16[6,192,128]{2,1,0:T(8,128)(2,1)} %collective-permute-done.3.outer_hbm, f32[2,4,192,128]{3,2,1,0:T(8,128)S(1)} %get-tuple-element.27.partial, ...), custom_call_target="tpu_custom_call", output_to_operand_aliasing={{}: (6, {})} | custom-call | tf_op jit(solution)/shard_map/forward_edge/pallas_call | solution.py:311
  31.1 5.4 %all-to-all-done = bf16[16,3,48,128]{3,2,1,0:T(8,128)(2,1)} async-done(((bf16[16,3,48,128]{3,2,1,0:T(8,128)(2,1)}), bf16[16,3,48,128]{3,2,1,0:T(8,128)(2,1)}, u32[]{:S(2)}, u32[]{:S(2)}) %all-to-all-start) | async-done | bytes 589856 | tf_op jit(solution)/shard_map/all_to_all | solution.py:382
  36.5 2.0 %unpack.1 = bf16[4,48,8,192]{3,2,1,0:T(8,128)(2,1)} custom-call(bf16[48,48,128]{2,1,0:T(8,128)(2,1)} %bitcast.7.src_hbm), custom_call_target="tpu_custom_call" | custom-call | tf_op jit(solution)/shard_map/unpack/pallas_call | solution.py:311
Async XLA Ops:
  0.6 6.5 %copy-start = (bf16[3,3,3,192,192]{4,3,2,1,0:T(8,128)(2,1)S(1)}, bf16[3,3,3,192,192]{4,3,2,1,0:T(8,128)(2,1)}, u32[]{:S(2)}) copy-start(bf16[3,3,3,192,192]{4,3,2,1,0:T(8,128)(2,1)} %kern.2) | copy-start | bytes 5971972
  0.6 6.5 %copy-start.1 = (bf16[4,3,128,192]{2,3,1,0:T(8,128)(2,1)S(1)}, bf16[4,3,128,192]{2,3,1,0:T(8,128)(2,1)}, u32[]{:S(2)}) copy-start(bf16[4,3,128,192]{2,3,1,0:T(8,128)(2,1)} %param.9) | copy-start | bytes 1769476
  0.7 6.5 %copy-start.2 = (bf16[4,3,128,192]{2,3,1,0:T(8,128)(2,1)S(1)}, bf16[4,3,128,192]{2,3,1,0:T(8,128)(2,1)}, u32[]{:S(2)}) copy-start(bf16[4,3,128,192]{2,3,1,0:T(8,128)(2,1)} %param.7) | copy-start | bytes 1769476
  0.7 6.4 %copy-start.3 = (bf16[2,3,128,192]{2,3,1,0:T(8,128)(2,1)S(1)}, bf16[2,3,128,192]{2,3,1,0:T(8,128)(2,1)}, u32[]{:S(2)}) copy-start(bf16[2,3,128,192]{2,3,1,0:T(8,128)(2,1)} %param.8) | copy-start | bytes 884740
  0.7 6.4 %copy-start.4 = (f32[192]{0:T(256)S(1)}, f32[192]{0:T(256)}, u32[]{:S(2)}) copy-start(f32[192]{0:T(256)} %param.11) | copy-start | bytes 2308
  0.7 6.4 %copy-start.5 = (f32[192]{0:T(256)S(1)}, f32[192]{0:T(256)}, u32[]{:S(2)}) copy-start(f32[192]{0:T(256)} %param.12) | copy-start | bytes 2308
  1.9 9.7 %collective-permute-start = (bf16[4,192,128]{2,1,0:T(8,128)(2,1)S(1)}, bf16[4,192,128]{2,1,0:T(8,128)(2,1)S(1)}, u32[]{:S(2)}, u32[]{:S(2)}) collective-permute-start(bf16[4,192,128]{2,1,0:T(8,128)(2,1)S(1)} %get-tuple-element.16), channel_id=1, source_target_pairs={{1,2},{3,4},{5,6},{7,8},{9,10},{11,12},{13,14},{2,1},{4,3},{6,5},{... | collective-permute-start | bytes 589832 | tf_op jit(solution)/shard_map/ppermute | solution.py:357
  2.7 8.9 %collective-permute-start.1 = (bf16[4,192,128]{2,1,0:T(8,128)(2,1)S(1)}, bf16[4,192,128]{2,1,0:T(8,128)(2,1)S(1)}, u32[]{:S(2)}, u32[]{:S(2)}) collective-permute-start(bf16[4,192,128]{2,1,0:T(8,128)(2,1)S(1)} %get-tuple-element.17), channel_id=1, source_target_pairs={{0,1},{1,0},{2,3},{3,2},{4,5},{5,4},{6,7},{7,6},{8,9},{9,8},{10,11... | collective-permute-start | bytes 589832 | tf_op jit(solution)/shard_map/ppermute | solution.py:358
  10.3 15.1 %collective-permute-start.3 = (bf16[6,192,128]{2,1,0:T(8,128)(2,1)}, bf16[6,192,128]{2,1,0:T(8,128)(2,1)}, u32[]{:S(2)}, u32[]{:S(2)}) collective-permute-start(bf16[6,192,128]{2,1,0:T(8,128)(2,1)} %get-tuple-element.26), channel_id=1, source_target_pairs={{1,2},{3,4},{5,6},{7,8},{9,10},{11,12},{13,14},{2,1},{4,3},{6,5},{... | collective-permute-start | bytes 884744 | tf_op jit(solution)/shard_map/ppermute | solution.py:372
  11.6 9.3 %copy-start.6 = (f32[192]{0:T(256)S(1)}, f32[192]{0:T(256)}, u32[]{:S(2)}) copy-start(f32[192]{0:T(256)} %param.13) | copy-start | bytes 2308
  14.1 22.4 %all-to-all-start = ((bf16[16,3,48,128]{3,2,1,0:T(8,128)(2,1)}), bf16[16,3,48,128]{3,2,1,0:T(8,128)(2,1)}, u32[]{:S(2)}, u32[]{:S(2)}) async-start(bf16[16,3,48,128]{3,2,1,0:T(8,128)(2,1)} %backward_edge.1), calls=%async_computation | async-start | bytes 1179648 | tf_op jit(solution)/shard_map/all_to_all | solution.py:382
  25.0 1.9 %collective-permute-start.2 = (bf16[6,192,128]{2,1,0:T(8,128)(2,1)}, bf16[6,192,128]{2,1,0:T(8,128)(2,1)S(1)}, u32[]{:S(2)}, u32[]{:S(2)}) collective-permute-start(bf16[6,192,128]{2,1,0:T(8,128)(2,1)} %get-tuple-element.25), channel_id=1, source_target_pairs={{0,1},{1,0},{2,3},{3,2},{4,5},{5,4},{6,7},{7,6},{8,9},{9,8},{10,11... | collective-permute-start | bytes 884744 | tf_op jit(solution)/shard_map/ppermute | solution.py:411
  26.8 0.7 %copy-start.7 = (bf16[6,192,128]{2,1,0:T(8,128)(2,1)}, bf16[6,192,128]{2,1,0:T(8,128)(2,1)S(1)}, u32[]{:S(2)}) copy-start(bf16[6,192,128]{2,1,0:T(8,128)(2,1)S(1)} %collective-permute-done.2.inner_hbm) | copy-start | bytes 884740

commit v8 on v7

--- a/solution.py
+++ b/solution.py
@@ -382,7 +382,7 @@
         moved = lax.all_to_all(grad, "slab", split_axis=0, concat_axis=0, tiled=True)
         moved = moved.reshape(slabs * rows, -1, 128)
         relaid = (frames, slabs * rows, per, chans)
-        parts = 2 if slabs * rows % 2 == 0 else 1
+        parts = 4 if slabs * rows % 4 == 0 else 1
         relaid = call(
             unpack_kernel,
             "unpack",

time: 38.8 us -> 38.8 us (level)
  no operation moved by 1% of the time
where the time goes in v8:
time: 38.8 us; the launch traced here: 38.5 us
  Pallas kernels  16.4 us (42%)
  starting transfers between devices  13.8 us (36%)
  waiting for transfers between devices  6.84 us (18%)
  between operations  0.77 us (2%)
  local copies, waits for them, and re-layouts  0.75 us (2%)
    pallas_call x6, Pallas kernels, call(): pl.pallas_call(kernel, out_shape=[pltpu.HBM(o.shape, o.dtype) if where is...  16.4 us
    all_to_all x1, starting transfers between devices, body(): lax.all_to_all(grad, 'slab', split_axis=0, concat_axis=0, tiled=True)  6.77 us
    all_to_all x1, waiting for transfers between devices, body(): lax.all_to_all(grad, 'slab', split_axis=0, concat_axis=0, tiled=True)  5.4 us
    ppermute x1, starting transfers between devices, body(): cot_in = lax.ppermute(cot_in, 'slab', within)  4.38 us
    ppermute x1, waiting for transfers between devices, body(): act_in = lax.ppermute(act_in, 'slab', within)  1.44 us
    ppermute x1, starting transfers between devices, body(): act_across = lax.ppermute(act_across, 'slab', across)  1.38 us
    ppermute x1, starting transfers between devices, body(): cot_across = lax.ppermute(cot_across, 'slab', across)  0.8 us
  transfers between devices with their start and end apart: 5, of which 2 were waited for; matrix products, arithmetic and copies ran while one was open for 0% of the time, Pallas kernels for 34%

profile of v8, /device:TPU:0, one launch (start us, length us, event | category | flops | bytes accessed | tf_op | source)
XLA Modules:
  0.0 38.5 jit_solution(18041606092400449785)
XLA Ops:
  0.6 0.0 copy-start
  0.6 0.0 copy-start.1
  0.7 0.0 copy-start.2
  0.7 0.0 copy-start.3
  0.7 0.0 copy-start.4
  0.7 0.0 copy-start.5
  0.7 1.2 %staging.1 = (bf16[4,192,128]{2,1,0:T(8,128)(2,1)S(1)}, bf16[4,192,128]{2,1,0:T(8,128)(2,1)S(1)}) custom-call(bf16[4,3,192,128]{3,2,1,0:T(8,128)(2,1)} %bitcast.8), custom_call_target="tpu_custom_call" | custom-call | flops 10000000000 | tf_op jit(solution)/shard_map/staging/pallas_call | solution.py:311
  1.9 0.8 %collective-permute-start = (bf16[4,192,128]{2,1,0:T(8,128)(2,1)S(1)}, bf16[4,192,128]{2,1,0:T(8,128)(2,1)S(1)}, u32[]{:S(2)}, u32[]{:S(2)}) collective-permute-start(bf16[4,192,128]{2,1,0:T(8,128)(2,1)S(1)} %get-tuple-element.16), channel_id=1, source_target_pairs={{1,2},{3,4},{5,6},{7,8},{9,10},{11,12},{13,14},{2,1},{4,3},{6,5},{... | collective-permute-start | bytes 589832 | tf_op jit(solution)/shard_map/ppermute | solution.py:357
  2.7 4.4 %collective-permute-start.1 = (bf16[4,192,128]{2,1,0:T(8,128)(2,1)S(1)}, bf16[4,192,128]{2,1,0:T(8,128)(2,1)S(1)}, u32[]{:S(2)}, u32[]{:S(2)}) collective-permute-start(bf16[4,192,128]{2,1,0:T(8,128)(2,1)S(1)} %get-tuple-element.17), channel_id=1, source_target_pairs={{0,1},{1,0},{2,3},{3,2},{4,5},{5,4},{6,7},{7,6},{8,9},{9,8},{10,11... | collective-permute-start | bytes 589832 | tf_op jit(solution)/shard_map/ppermute | solution.py:358
  7.1 0.0 copy-done
  7.1 0.0 copy-done.1
  7.1 0.0 copy-done.2
  7.1 0.0 copy-done.3
  7.1 0.0 copy-done.4
  7.1 0.0 copy-done.5
  7.1 3.1 %backward_local.1 = (bf16[16,1,48,128]{3,2,1,0:T(8,128)(2,1)S(1)}, bf16[6,192,128]{2,1,0:T(8,128)(2,1)}, f32[2,4,192,128]{3,2,1,0:T(8,128)S(1)}, bf16[576,1728]{1,0:T(8,128)(2,1)S(1)}) custom-call(bf16[4,3,192,128]{3,2,1,0:T(8,128)(2,1)S(1)} %bitcast.9, bf16[4,3,192,128]{3,2,1,0:T(8,128)(2,1)S(1)} %bitcast.11, bf16[2,3,192,128]{3,2,1,0:T(8,128)(2,1)S(1)} %bitcast.14, ...), custom_call_target="tpu_custom_call" | custom-call | tf_op jit(solution)/shard_map/backward_local/pallas_call | solution.py:311
  10.3 1.4 %collective-permute-start.3 = (bf16[6,192,128]{2,1,0:T(8,128)(2,1)}, bf16[6,192,128]{2,1,0:T(8,128)(2,1)}, u32[]{:S(2)}, u32[]{:S(2)}) collective-permute-start(bf16[6,192,128]{2,1,0:T(8,128)(2,1)} %get-tuple-element.26), channel_id=1, source_target_pairs={{1,2},{3,4},{5,6},{7,8},{9,10},{11,12},{13,14},{2,1},{4,3},{6,5},{... | collective-permute-start | bytes 884744 | tf_op jit(solution)/shard_map/ppermute | solution.py:372
  11.6 0.0 collective-permute-done.outer
  11.6 0.0 collective-permute-done.1.inner
  11.6 0.0 copy-start.6
  11.6 2.5 %backward_edge.1 = bf16[16,3,48,128]{3,2,1,0:T(8,128)(2,1)} custom-call(bf16[4,3,192,128]{3,2,1,0:T(8,128)(2,1)S(1)} %bitcast.10, bf16[4,192,128]{2,1,0:T(8,128)(2,1)S(1)} %collective-permute-done.outer, bf16[4,192,128]{2,1,0:T(8,128)(2,1)S(1)} %collective-permute-done.1.inner, bf16[4,3,192,128]{3,2,1,0:T(8,128)(2,1)S(1)} %bitcast.12, ...), custom_call_target="tpu_custom_call" | custom-call | tf_op jit(solution)/shard_map/backward_edge/pallas_call | solution.py:311
  14.1 6.8 %all-to-all-start = ((bf16[16,3,48,128]{3,2,1,0:T(8,128)(2,1)}), bf16[16,3,48,128]{3,2,1,0:T(8,128)(2,1)}, u32[]{:S(2)}, u32[]{:S(2)}) async-start(bf16[16,3,48,128]{3,2,1,0:T(8,128)(2,1)} %backward_edge.1), calls=%async_computation | async-start | bytes 1179648 | tf_op jit(solution)/shard_map/all_to_all | solution.py:382
  20.9 0.0 copy-done.6
  20.9 4.0 %forward_local.1 = (bf16[4,3,192,128]{3,2,1,0:T(8,128)(2,1)}, bf16[6,192,128]{2,1,0:T(8,128)(2,1)}, f32[2,4,192,128]{3,2,1,0:T(8,128)S(1)}, bf16[3,192,1728]{2,1,0:T(8,128)(2,1)S(1)}) custom-call(bf16[4,3,192,128]{3,2,1,0:T(8,128)(2,1)S(1)} %bitcast.13, bf16[2,3,192,128]{3,2,1,0:T(8,128)(2,1)S(1)} %bitcast.15, bf16[3,3,3,192,192]{4,3,2,1,0:T(8,128)(2,1)S(1)} %copy-done, ...), custom_call_target="tpu_custom_call" | custom-call | flops 10000000000 | tf_op jit(solution)/shard_map/forward_local/pallas_call | solution.py:311
  25.0 0.4 %collective-permute-start.2 = (bf16[6,192,128]{2,1,0:T(8,128)(2,1)}, bf16[6,192,128]{2,1,0:T(8,128)(2,1)S(1)}, u32[]{:S(2)}, u32[]{:S(2)}) collective-permute-start(bf16[6,192,128]{2,1,0:T(8,128)(2,1)} %get-tuple-element.25), channel_id=1, source_target_pairs={{0,1},{1,0},{2,3},{3,2},{4,5},{5,4},{6,7},{7,6},{8,9},{9,8},{10,11... | collective-permute-start | bytes 884744 | tf_op jit(solution)/shard_map/ppermute | solution.py:411
  25.4 0.0 collective-permute-done.3.outer_hbm
  25.4 1.4 %collective-permute-done.2.inner_hbm = bf16[6,192,128]{2,1,0:T(8,128)(2,1)S(1)} collective-permute-done((bf16[6,192,128]{2,1,0:T(8,128)(2,1)}, bf16[6,192,128]{2,1,0:T(8,128)(2,1)S(1)}, u32[]{:S(2)}, u32[]{:S(2)}) %collective-permute-start.2) | collective-permute-done | bytes 294944 | tf_op jit(solution)/shard_map/ppermute | solution.py:411
  26.8 0.0 copy-start.7
  26.8 0.7 %copy-done.7 = bf16[6,192,128]{2,1,0:T(8,128)(2,1)} copy-done((bf16[6,192,128]{2,1,0:T(8,128)(2,1)}, bf16[6,192,128]{2,1,0:T(8,128)(2,1)S(1)}, u32[]{:S(2)}) %copy-start.7) | copy-done | bytes 294936
  27.6 3.6 %forward_edge.1 = bf16[4,3,192,128]{3,2,1,0:T(8,128)(2,1)} custom-call(bf16[6,192,128]{2,1,0:T(8,128)(2,1)} %copy-done.7, bf16[6,192,128]{2,1,0:T(8,128)(2,1)} %collective-permute-done.3.outer_hbm, f32[2,4,192,128]{3,2,1,0:T(8,128)S(1)} %get-tuple-element.27.partial, ...), custom_call_target="tpu_custom_call", output_to_operand_aliasing={{}: (6, {})} | custom-call | tf_op jit(solution)/shard_map/forward_edge/pallas_call | solution.py:311
  31.1 5.4 %all-to-all-done = bf16[16,3,48,128]{3,2,1,0:T(8,128)(2,1)} async-done(((bf16[16,3,48,128]{3,2,1,0:T(8,128)(2,1)}), bf16[16,3,48,128]{3,2,1,0:T(8,128)(2,1)}, u32[]{:S(2)}, u32[]{:S(2)}) %all-to-all-start) | async-done | bytes 589856 | tf_op jit(solution)/shard_map/all_to_all | solution.py:382
  36.5 2.0 %unpack.1 = bf16[4,48,8,192]{3,2,1,0:T(8,128)(2,1)} custom-call(bf16[48,48,128]{2,1,0:T(8,128)(2,1)} %bitcast.7.src_hbm), custom_call_target="tpu_custom_call" | custom-call | tf_op jit(solution)/shard_map/unpack/pallas_call | solution.py:311
Async XLA Ops:
  0.6 6.5 %copy-start = (bf16[3,3,3,192,192]{4,3,2,1,0:T(8,128)(2,1)S(1)}, bf16[3,3,3,192,192]{4,3,2,1,0:T(8,128)(2,1)}, u32[]{:S(2)}) copy-start(bf16[3,3,3,192,192]{4,3,2,1,0:T(8,128)(2,1)} %kern.2) | copy-start | bytes 5971972
  0.6 6.5 %copy-start.1 = (bf16[4,3,128,192]{2,3,1,0:T(8,128)(2,1)S(1)}, bf16[4,3,128,192]{2,3,1,0:T(8,128)(2,1)}, u32[]{:S(2)}) copy-start(bf16[4,3,128,192]{2,3,1,0:T(8,128)(2,1)} %param.9) | copy-start | bytes 1769476
  0.7 6.5 %copy-start.2 = (bf16[4,3,128,192]{2,3,1,0:T(8,128)(2,1)S(1)}, bf16[4,3,128,192]{2,3,1,0:T(8,128)(2,1)}, u32[]{:S(2)}) copy-start(bf16[4,3,128,192]{2,3,1,0:T(8,128)(2,1)} %param.7) | copy-start | bytes 1769476
  0.7 6.4 %copy-start.3 = (bf16[2,3,128,192]{2,3,1,0:T(8,128)(2,1)S(1)}, bf16[2,3,128,192]{2,3,1,0:T(8,128)(2,1)}, u32[]{:S(2)}) copy-start(bf16[2,3,128,192]{2,3,1,0:T(8,128)(2,1)} %param.8) | copy-start | bytes 884740
  0.7 6.4 %copy-start.4 = (f32[192]{0:T(256)S(1)}, f32[192]{0:T(256)}, u32[]{:S(2)}) copy-start(f32[192]{0:T(256)} %param.11) | copy-start | bytes 2308
  0.7 6.4 %copy-start.5 = (f32[192]{0:T(256)S(1)}, f32[192]{0:T(256)}, u32[]{:S(2)}) copy-start(f32[192]{0:T(256)} %param.12) | copy-start | bytes 2308
  1.9 9.7 %collective-permute-start = (bf16[4,192,128]{2,1,0:T(8,128)(2,1)S(1)}, bf16[4,192,128]{2,1,0:T(8,128)(2,1)S(1)}, u32[]{:S(2)}, u32[]{:S(2)}) collective-permute-start(bf16[4,192,128]{2,1,0:T(8,128)(2,1)S(1)} %get-tuple-element.16), channel_id=1, source_target_pairs={{1,2},{3,4},{5,6},{7,8},{9,10},{11,12},{13,14},{2,1},{4,3},{6,5},{... | collective-permute-start | bytes 589832 | tf_op jit(solution)/shard_map/ppermute | solution.py:357
  2.7 8.9 %collective-permute-start.1 = (bf16[4,192,128]{2,1,0:T(8,128)(2,1)S(1)}, bf16[4,192,128]{2,1,0:T(8,128)(2,1)S(1)}, u32[]{:S(2)}, u32[]{:S(2)}) collective-permute-start(bf16[4,192,128]{2,1,0:T(8,128)(2,1)S(1)} %get-tuple-element.17), channel_id=1, source_target_pairs={{0,1},{1,0},{2,3},{3,2},{4,5},{5,4},{6,7},{7,6},{8,9},{9,8},{10,11... | collective-permute-start | bytes 589832 | tf_op jit(solution)/shard_map/ppermute | solution.py:358
  10.3 15.1 %collective-permute-start.3 = (bf16[6,192,128]{2,1,0:T(8,128)(2,1)}, bf16[6,192,128]{2,1,0:T(8,128)(2,1)}, u32[]{:S(2)}, u32[]{:S(2)}) collective-permute-start(bf16[6,192,128]{2,1,0:T(8,128)(2,1)} %get-tuple-element.26), channel_id=1, source_target_pairs={{1,2},{3,4},{5,6},{7,8},{9,10},{11,12},{13,14},{2,1},{4,3},{6,5},{... | collective-permute-start | bytes 884744 | tf_op jit(solution)/shard_map/ppermute | solution.py:372
  11.6 9.3 %copy-start.6 = (f32[192]{0:T(256)S(1)}, f32[192]{0:T(256)}, u32[]{:S(2)}) copy-start(f32[192]{0:T(256)} %param.13) | copy-start | bytes 2308
  14.1 22.4 %all-to-all-start = ((bf16[16,3,48,128]{3,2,1,0:T(8,128)(2,1)}), bf16[16,3,48,128]{3,2,1,0:T(8,128)(2,1)}, u32[]{:S(2)}, u32[]{:S(2)}) async-start(bf16[16,3,48,128]{3,2,1,0:T(8,128)(2,1)} %backward_edge.1), calls=%async_computation | async-start | bytes 1179648 | tf_op jit(solution)/shard_map/all_to_all | solution.py:382
  25.0 1.9 %collective-permute-start.2 = (bf16[6,192,128]{2,1,0:T(8,128)(2,1)}, bf16[6,192,128]{2,1,0:T(8,128)(2,1)S(1)}, u32[]{:S(2)}, u32[]{:S(2)}) collective-permute-start(bf16[6,192,128]{2,1,0:T(8,128)(2,1)} %get-tuple-element.25), channel_id=1, source_target_pairs={{0,1},{1,0},{2,3},{3,2},{4,5},{5,4},{6,7},{7,6},{8,9},{9,8},{10,11... | collective-permute-start | bytes 884744 | tf_op jit(solution)/shard_map/ppermute | solution.py:411
  26.8 0.7 %copy-start.7 = (bf16[6,192,128]{2,1,0:T(8,128)(2,1)}, bf16[6,192,128]{2,1,0:T(8,128)(2,1)S(1)}, u32[]{:S(2)}) copy-start(bf16[6,192,128]{2,1,0:T(8,128)(2,1)S(1)} %collective-permute-done.2.inner_hbm) | copy-start | bytes 884740
